TPU v7x, 32 devices: a whole 2x2x4 slice. The times are simulated.
32 devices in a mesh: fsdp: 4 (over x, core), ctx: 2 (over y), tp: 4 (over z).
Axes of the slice: x: 2, y: 2, z: 4, core: 2. Of those that a mesh axis runs over, the one named last changes fastest.
Arguments:
- tokens: bfloat16 [16, 2048, 1152], P('fsdp', ('ctx', 'tp')), may hold values from -6 to 6
- picture: int32 [16, 2048], P('fsdp', 'ctx'), may hold values from 0 to 3, never falling along the last dimension, each value on 1 to 1024 neighbouring positions
- ln1_gain: float32 [1152], replicated, may hold values from 0.5 to 1.5
- ln1_bias: float32 [1152], replicated, may hold values from -1 to 1
- w_query: bfloat16 [1152, 1152], P('fsdp', 'tp'), may hold values from -0.1875 to 0.1875
- b_query: float32 [1152], replicated, may hold values from -1 to 1
- w_key: bfloat16 [1152, 1152], P('fsdp', 'tp'), may hold values from -0.1875 to 0.1875
- w_value: bfloat16 [1152, 1152], P('fsdp', 'tp'), may hold values from -0.1875 to 0.1875
- b_value: float32 [1152], replicated, may hold values from -1 to 1
- w_output: bfloat16 [1152, 1152], P('tp', 'fsdp'), may hold values from -4 to 4
- b_output: float32 [1152], replicated, may hold values from -1 to 1
- ln2_gain: float32 [1152], replicated, may hold values from 0.5 to 1.5
- ln2_bias: float32 [1152], replicated, may hold values from -1 to 1
- w_first: bfloat16 [1152, 4304], P('fsdp', 'tp'), may hold values from -0.1875 to 0.1875
- b_first: float32 [4304], replicated, may hold values from -1 to 1
- w_second: bfloat16 [4304, 1152], P('tp', 'fsdp'), may hold values from -0.09375 to 0.09375
- b_second: float32 [1152], replicated, may hold values from -1 to 1
- cotangent: bfloat16 [16, 2048, 1152], P('fsdp', ('ctx', 'tp')), may hold values from -6 to 6
Outputs:
- output: bfloat16 [16, 2048, 1152], P('fsdp', ('ctx', 'tp'))
- grad_tokens: float32 [16, 2048, 1152], P('fsdp', ('ctx', 'tp'))
- grad_ln1_gain: float32 [1152], replicated
- grad_ln1_bias: float32 [1152], replicated
- grad_w_query: float32 [1152, 1152], P(('fsdp', 'ctx'), 'tp')
- grad_b_query: float32 [1152], replicated
- grad_w_key: float32 [1152, 1152], P(('fsdp', 'ctx'), 'tp')
- grad_w_value: float32 [1152, 1152], P(('fsdp', 'ctx'), 'tp')
- grad_b_value: float32 [1152], replicated
- grad_w_output: float32 [1152, 1152], P('tp', ('fsdp', 'ctx'))
- grad_b_output: float32 [1152], replicated
- grad_ln2_gain: float32 [1152], replicated
- grad_ln2_bias: float32 [1152], replicated
- grad_w_first: float32 [1152, 4304], P(('fsdp', 'ctx'), 'tp')
- grad_b_first: float32 [4304], replicated
- grad_w_second: float32 [4304, 1152], P('tp', ('fsdp', 'ctx'))
- grad_b_second: float32 [1152], replicated
Inputs may be any that keep to these rules, and one draw needn't show every extreme that they name: In each row picture numbers never fall along the 2048 tokens; each picture holds 1 to 1024 tokens and one holds exactly 1024.
All inputs are finite; a program needn't handle non-finite values.
Results may differ from a plain program's by a relative error of at most 0.02.
Values may be sent and summed in bfloat16 or wider, within the bound.
A program may use at most 512 MiB of HBM per device.

v0:
```python
import jax
import jax.numpy as jnp
from jax import lax
from jax.sharding import PartitionSpec as P

D = 1152
HD = 72
FF = 4304


EPSILON = 1e-06


def layer_norm(values, gain, bias):
    centred = values - jnp.mean(values, axis=-1, keepdims=True)
    variance = jnp.mean(centred * centred, axis=-1, keepdims=True)
    return centred * lax.rsqrt(variance + EPSILON) * gain + bias


def matmul(left, right):
    return jnp.dot(left, right, preferred_element_type=jnp.float32)


def shards(
    tokens,
    picture,
    ln1_gain,
    ln1_bias,
    w_query,
    b_query,
    w_key,
    w_value,
    b_value,
    w_output,
    b_output,
    ln2_gain,
    ln2_bias,
    w_first,
    b_first,
    w_second,
    b_second,
    cotangent,
):
    tp_index = lax.axis_index("tp")
    wq_all, wk_all, wv_all, wo_all, wf_all, ws_all = (
        lax.all_gather(w_query, "fsdp", axis=0, tiled=True),
        lax.all_gather(w_key, "fsdp", axis=0, tiled=True),
        lax.all_gather(w_value, "fsdp", axis=0, tiled=True),
        lax.all_gather(w_output, "fsdp", axis=1, tiled=True),
        lax.all_gather(w_first, "fsdp", axis=0, tiled=True),
        lax.all_gather(w_second, "fsdp", axis=1, tiled=True),
    )
    columns = wq_all.shape[1]
    heads_dev = columns // HD
    units = wf_all.shape[1]
    bq_local = lax.dynamic_slice_in_dim(b_query, tp_index * columns, columns)
    bv_local = lax.dynamic_slice_in_dim(b_value, tp_index * columns, columns)
    first_use, second_use = (wf_all, ws_all)
    first_bias = lax.dynamic_slice_in_dim(b_first, tp_index * units, units)
    scale = HD ** (-0.5)
    grad_query = jnp.zeros(wq_all.shape, jnp.float32)
    grad_key = jnp.zeros(wk_all.shape, jnp.float32)
    grad_value = jnp.zeros(wv_all.shape, jnp.float32)
    grad_out = jnp.zeros(wo_all.shape, jnp.float32)
    grad_first = jnp.zeros(first_use.shape, jnp.float32)
    grad_second = jnp.zeros(second_use.shape, jnp.float32)
    grad_first_bias = jnp.zeros(first_bias.shape, jnp.float32)
    grad_bq = jnp.zeros((columns,), jnp.float32)
    grad_bv = jnp.zeros((columns,), jnp.float32)
    grad_bo = jnp.zeros((D,), jnp.float32)
    grad_bs = jnp.zeros((D,), jnp.float32)
    grad_g1 = jnp.zeros((D,), jnp.float32)
    grad_c1 = jnp.zeros((D,), jnp.float32)
    grad_g2 = jnp.zeros((D,), jnp.float32)
    grad_c2 = jnp.zeros((D,), jnp.float32)
    outputs = []
    input_grads = []
    for batch_index in range(tokens.shape[0]):
        row_input = tokens[batch_index].astype(jnp.float32)
        query_ids = picture[batch_index]
        row_cot = cotangent[batch_index]
        normed = layer_norm(row_input, ln1_gain, ln1_bias).astype(jnp.bfloat16)
        normed_all = lax.all_gather(normed, "tp", axis=0, tiled=True)
        half_rows = normed_all.shape[0]
        queries = (matmul(normed_all, wq_all) + bq_local).astype(jnp.bfloat16)
        keys = matmul(normed_all, wk_all).astype(jnp.bfloat16)
        values = (matmul(normed_all, wv_all) + bv_local).astype(jnp.bfloat16)
        keys_all, values_all, key_ids = (
            lax.all_gather(keys, "ctx", axis=0, tiled=True),
            lax.all_gather(values, "ctx", axis=0, tiled=True),
            lax.all_gather(query_ids, "ctx", axis=0, tiled=True),
        )
        key_rows = keys_all.shape[0]
        query_heads = queries.reshape(half_rows, heads_dev, HD)
        key_heads = keys_all.reshape(key_rows, heads_dev, HD)
        value_heads = values_all.reshape(key_rows, heads_dev, HD)
        same = (query_ids[:, None] == key_ids[None, :])[None, :, :]

        def masked_scores():
            raw = (
                jnp.einsum(
                    "qhd,khd->hqk", query_heads, key_heads, preferred_element_type=jnp.float32
                )
                * scale
            )
            return jnp.where(same, raw, -1e30)

        scores = masked_scores()
        row_max = jnp.max(scores, axis=-1, keepdims=True)
        row_total = jnp.sum(jnp.exp(scores - row_max), axis=-1, keepdims=True)
        probs_low = (jnp.exp(scores - row_max) / row_total).astype(jnp.bfloat16)
        attended = (
            jnp.einsum("hqk,khd->qhd", probs_low, value_heads, preferred_element_type=jnp.float32)
            .reshape(half_rows, columns)
            .astype(jnp.bfloat16)
        )
        hidden = (
            row_input
            + lax.psum_scatter(
                matmul(attended, wo_all).astype(jnp.bfloat16), "tp", scatter_dimension=0, tiled=True
            ).astype(jnp.float32)
            + b_output
        )
        normed_two = layer_norm(hidden, ln2_gain, ln2_bias).astype(jnp.bfloat16)
        normed_two_all, cot_all = (
            lax.all_gather(normed_two, "tp", axis=0, tiled=True),
            lax.all_gather(row_cot, "tp", axis=0, tiled=True),
        )
        before = matmul(normed_two_all, first_use) + first_bias
        active = jax.nn.gelu(before).astype(jnp.bfloat16)
        mixed = (
            lax.psum_scatter(
                matmul(active, second_use).astype(jnp.bfloat16),
                "tp",
                scatter_dimension=0,
                tiled=True,
            ).astype(jnp.float32)
            + b_second
        )
        d_active = matmul(cot_all, second_use.T)
        _, gelu_back = jax.vjp(jax.nn.gelu, before)
        d_before = gelu_back(d_active)[0].astype(jnp.bfloat16)
        grad_second = grad_second + matmul(active.T, cot_all)
        grad_first = grad_first + matmul(normed_two_all.T, d_before)
        grad_first_bias = grad_first_bias + jnp.sum(d_before.astype(jnp.float32), axis=0)
        d_normed_two = lax.psum_scatter(
            matmul(d_before, first_use.T).astype(jnp.bfloat16),
            "tp",
            scatter_dimension=0,
            tiled=True,
        ).astype(jnp.float32)
        outputs.append((hidden + mixed).astype(jnp.bfloat16))
        cot_float = row_cot.astype(jnp.float32)
        grad_bs = grad_bs + jnp.sum(cot_float, axis=0)
        _, norm_two_back = jax.vjp(layer_norm, hidden, ln2_gain, ln2_bias)
        d_hidden_norm, d_gain_two, d_bias_two = norm_two_back(d_normed_two)
        grad_g2 = grad_g2 + d_gain_two
        grad_c2 = grad_c2 + d_bias_two
        d_hidden = cot_float + d_hidden_norm
        d_attention = d_hidden.astype(jnp.bfloat16)
        grad_bo = grad_bo + jnp.sum(d_attention.astype(jnp.float32), axis=0)
        d_attention_all = lax.all_gather(d_attention, "tp", axis=0, tiled=True)
        grad_out = grad_out + matmul(attended.T, d_attention_all)
        d_attended = (
            matmul(d_attention_all, wo_all.T).astype(jnp.bfloat16).reshape(half_rows, heads_dev, HD)
        )
        scores_again = masked_scores()
        probs = jnp.exp(scores_again - row_max) / row_total
        probs_again = probs.astype(jnp.bfloat16)
        d_values_full = jnp.einsum(
            "hqk,qhd->khd", probs_again, d_attended, preferred_element_type=jnp.float32
        ).reshape(key_rows, columns)
        d_probs = jnp.einsum(
            "qhd,khd->hqk", d_attended, value_heads, preferred_element_type=jnp.float32
        )
        weighted = jnp.sum(probs * d_probs, axis=-1, keepdims=True)
        d_scores = (probs * (d_probs - weighted)).astype(jnp.bfloat16)
        d_queries = (
            (
                jnp.einsum("hqk,khd->qhd", d_scores, key_heads, preferred_element_type=jnp.float32)
                * scale
            )
            .reshape(half_rows, columns)
            .astype(jnp.bfloat16)
        )
        d_keys_full = (
            jnp.einsum("hqk,qhd->khd", d_scores, query_heads, preferred_element_type=jnp.float32)
            * scale
        ).reshape(key_rows, columns)
        d_keys_sum, d_values_sum = (
            lax.psum_scatter(
                d_keys_full.astype(jnp.bfloat16), "ctx", scatter_dimension=0, tiled=True
            ).astype(jnp.float32),
            lax.psum_scatter(
                d_values_full.astype(jnp.bfloat16), "ctx", scatter_dimension=0, tiled=True
            ).astype(jnp.float32),
        )
        d_keys = d_keys_sum.astype(jnp.bfloat16)
        d_values = d_values_sum.astype(jnp.bfloat16)
        grad_query = grad_query + matmul(normed_all.T, d_queries)
        grad_key = grad_key + matmul(normed_all.T, d_keys)
        grad_value = grad_value + matmul(normed_all.T, d_values)
        grad_bq = grad_bq + jnp.sum(d_queries.astype(jnp.float32), axis=0)
        grad_bv = grad_bv + jnp.sum(d_values.astype(jnp.float32), axis=0)
        normed_term = (
            matmul(d_queries, wq_all.T) + matmul(d_keys, wk_all.T) + matmul(d_values, wv_all.T)
        )
        d_normed = lax.psum_scatter(
            normed_term.astype(jnp.bfloat16), "tp", scatter_dimension=0, tiled=True
        ).astype(jnp.float32)
        _, norm_one_back = jax.vjp(layer_norm, row_input, ln1_gain, ln1_bias)
        d_input_norm, d_gain_one, d_bias_one = norm_one_back(d_normed)
        grad_g1 = grad_g1 + d_gain_one
        grad_c1 = grad_c1 + d_bias_one
        input_grads.append(d_hidden + d_input_norm)
    bias_first_full = lax.dynamic_update_slice(
        jnp.zeros((FF,), jnp.float32), grad_first_bias, (tp_index * units,)
    )
    grad_query, grad_key, grad_value, grad_out, grad_first, grad_second = (
        lax.psum_scatter(
            grad_query.astype(jnp.bfloat16), ("fsdp", "ctx"), scatter_dimension=0, tiled=True
        ).astype(jnp.float32),
        lax.psum_scatter(
            grad_key.astype(jnp.bfloat16), ("fsdp", "ctx"), scatter_dimension=0, tiled=True
        ).astype(jnp.float32),
        lax.psum_scatter(
            grad_value.astype(jnp.bfloat16), ("fsdp", "ctx"), scatter_dimension=0, tiled=True
        ).astype(jnp.float32),
        lax.psum_scatter(
            grad_out.astype(jnp.bfloat16), ("fsdp", "ctx"), scatter_dimension=1, tiled=True
        ).astype(jnp.float32),
        lax.psum_scatter(
            grad_first.astype(jnp.bfloat16), ("fsdp", "ctx"), scatter_dimension=0, tiled=True
        ).astype(jnp.float32),
        lax.psum_scatter(
            grad_second.astype(jnp.bfloat16), ("fsdp", "ctx"), scatter_dimension=1, tiled=True
        ).astype(jnp.float32),
    )
    bq_full = lax.dynamic_update_slice(jnp.zeros((D,), jnp.float32), grad_bq, (tp_index * columns,))
    bv_full = lax.dynamic_update_slice(jnp.zeros((D,), jnp.float32), grad_bv, (tp_index * columns,))
    grad_g1, grad_c1, bq_full, bv_full, grad_bo, grad_g2, grad_c2, bias_first_full, grad_bs = (
        lax.psum(
            (
                grad_g1,
                grad_c1,
                bq_full,
                bv_full,
                grad_bo,
                grad_g2,
                grad_c2,
                bias_first_full,
                grad_bs,
            ),
            ("fsdp", "ctx", "tp"),
        )
    )
    return (
        jnp.stack(outputs, 0),
        jnp.stack(input_grads, 0),
        grad_g1,
        grad_c1,
        grad_query,
        bq_full,
        grad_key,
        grad_value,
        bv_full,
        grad_out,
        grad_bo,
        grad_g2,
        grad_c2,
        grad_first,
        bias_first_full,
        grad_second,
        grad_bs,
    )


def solution(mesh):
    return jax.shard_map(
        shards,
        mesh=mesh,
        in_specs=(
            P("fsdp", ("ctx", "tp"), None),
            P("fsdp", "ctx"),
            P(),
            P(),
            P("fsdp", "tp"),
            P(),
            P("fsdp", "tp"),
            P("fsdp", "tp"),
            P(),
            P("tp", "fsdp"),
            P(),
            P(),
            P(),
            P("fsdp", "tp"),
            P(),
            P("tp", "fsdp"),
            P(),
            P("fsdp", ("ctx", "tp"), None),
        ),
        out_specs=(
            P("fsdp", ("ctx", "tp"), None),
            P("fsdp", ("ctx", "tp"), None),
            P(),
            P(),
            P(("fsdp", "ctx"), "tp"),
            P(),
            P(("fsdp", "ctx"), "tp"),
            P(("fsdp", "ctx"), "tp"),
            P(),
            P("tp", ("fsdp", "ctx")),
            P(),
            P(),
            P(),
            P(("fsdp", "ctx"), "tp"),
            P(),
            P("tp", ("fsdp", "ctx")),
            P(),
        ),
        check_vma=False,
    )
```

profile of v0, /device:TPU:0, one launch (start us, length us, event | category | flops | bytes accessed | tf_op | source)
XLA Modules:
  0.0 2532.8 jit_solution(4475514019620308846)
XLA Ops:
  136.3 48.1 %reduce-scatter.31.cloned.1.call-done = bf16[256,1152]{1,0:T(8,128)(2,1)} async-done(((bf16[1024,1152]{1,0:T(8,128)(2,1)}), bf16[256,1152]{1,0:T(8,128)(2,1)}) %reduce-scatter.31.cloned.1.call-update) | async-done | bytes 589840 | tf_op jit(solution)/shard_map/reduce_scatter | solution.py:119
  187.1 50.1 %all-gather.55.cloned.1.call-done = bf16[1024,1152]{1,0:T(8,128)(2,1)} async-done(((bf16[256,1152]{1,0:T(8,128)(2,1)}), bf16[1024,1152]{1,0:T(8,128)(2,1)}) %all-gather.55.cloned.1.call-update) | async-done | bytes 2359312 | tf_op jit(solution)/shard_map/all_gather | solution.py:83
  309.0 48.1 %reduce-scatter.39.cloned.1.call-done = bf16[256,1152]{1,0:T(8,128)(2,1)} async-done(((bf16[1024,1152]{1,0:T(8,128)(2,1)}), bf16[256,1152]{1,0:T(8,128)(2,1)}) %reduce-scatter.39.cloned.1.call-update) | async-done | bytes 589840 | tf_op jit(solution)/shard_map/reduce_scatter | solution.py:119
  369.1 44.7 %all-gather.63.cloned.1.call-done = bf16[1024,1152]{1,0:T(8,128)(2,1)} async-done(((bf16[256,1152]{1,0:T(8,128)(2,1)}), bf16[1024,1152]{1,0:T(8,128)(2,1)}) %all-gather.63.cloned.1.call-update) | async-done | bytes 2359312 | tf_op jit(solution)/shard_map/all_gather | solution.py:83
  420.9 44.2 %all-gather.47.cloned.1.call-done = bf16[1024,1152]{1,0:T(8,128)(2,1)} async-done(((bf16[256,1152]{1,0:T(8,128)(2,1)}), bf16[1024,1152]{1,0:T(8,128)(2,1)}) %all-gather.47.cloned.1.call-update) | async-done | bytes 2359312 | tf_op jit(solution)/shard_map/all_gather | solution.py:83
  491.2 51.9 %all-gather.41.cloned.1.call-done = bf16[1024,1152]{1,0:T(8,128)(2,1)} async-done(((bf16[256,1152]{1,0:T(8,128)(2,1)}), bf16[1024,1152]{1,0:T(8,128)(2,1)}) %all-gather.41.cloned.1.call-update) | async-done | bytes 2359312 | tf_op jit(solution)/shard_map/all_gather | solution.py:126
  550.8 43.3 %all-gather.79.cloned.1.call-done = bf16[1,1024,1152]{2,1,0:T(8,128)(2,1)} async-done(((bf16[1,256,1152]{2,1,0:T(8,128)(2,1)}), bf16[1,1024,1152]{2,1,0:T(8,128)(2,1)}) %all-gather.79.cloned.1.call-update) | async-done | bytes 2359312 | tf_op jit(solution)/shard_map/all_gather | solution.py:127
  638.4 33.6 %all-gather.61.cloned.1.call-done = bf16[1024,1152]{1,0:T(8,128)(2,1)} async-done(((bf16[256,1152]{1,0:T(8,128)(2,1)}), bf16[1024,1152]{1,0:T(8,128)(2,1)}) %all-gather.61.cloned.1.call-update) | async-done | bytes 2359312 | tf_op jit(solution)/shard_map/all_gather | solution.py:126
  679.7 43.1 %all-gather.83.cloned.1.call-done = bf16[1,1024,1152]{2,1,0:T(8,128)(2,1)} async-done(((bf16[1,256,1152]{2,1,0:T(8,128)(2,1)}), bf16[1,1024,1152]{2,1,0:T(8,128)(2,1)}) %all-gather.83.cloned.1.call-update) | async-done | bytes 2359312 | tf_op jit(solution)/shard_map/all_gather | solution.py:127
  869.7 50.5 %reduce-scatter.63.cloned.1.call-done = bf16[256,1152]{1,0:T(8,128)(2,1)} async-done(((bf16[1024,1152]{1,0:T(8,128)(2,1)}), bf16[256,1152]{1,0:T(8,128)(2,1)}) %reduce-scatter.63.cloned.1.call-update) | async-done | bytes 589840 | tf_op jit(solution)/shard_map/reduce_scatter | solution.py:146
  920.1 49.9 %reduce-scatter.43.cloned.1.call-done = bf16[256,1152]{1,0:T(8,128)(2,1)} async-done(((bf16[1024,1152]{1,0:T(8,128)(2,1)}), bf16[256,1152]{1,0:T(8,128)(2,1)}) %reduce-scatter.43.cloned.1.call-update) | async-done | bytes 589840 | tf_op jit(solution)/shard_map/reduce_scatter | solution.py:119
  970.0 49.7 %reduce-scatter.35.cloned.1.call-done = bf16[256,1152]{1,0:T(8,128)(2,1)} async-done(((bf16[1024,1152]{1,0:T(8,128)(2,1)}), bf16[256,1152]{1,0:T(8,128)(2,1)}) %reduce-scatter.35.cloned.1.call-update) | async-done | bytes 589840 | tf_op jit(solution)/shard_map/reduce_scatter | solution.py:119
  1023.4 46.1 %reduce-scatter.41.cloned.1.call-done = bf16[256,1152]{1,0:T(8,128)(2,1)} async-done(((bf16[1024,1152]{1,0:T(8,128)(2,1)}), bf16[256,1152]{1,0:T(8,128)(2,1)}) %reduce-scatter.41.cloned.1.call-update) | async-done | bytes 589840 | tf_op jit(solution)/shard_map/reduce_scatter | solution.py:132
  1080.2 39.1 %reduce-scatter.33.cloned.1.call-done = bf16[256,1152]{1,0:T(8,128)(2,1)} async-done(((bf16[1024,1152]{1,0:T(8,128)(2,1)}), bf16[256,1152]{1,0:T(8,128)(2,1)}) %reduce-scatter.33.cloned.1.call-update) | async-done | bytes 589840 | tf_op jit(solution)/shard_map/reduce_scatter | solution.py:132
  1127.7 43.0 %all-gather.75.cloned.1.call-done = bf16[1024,1152]{1,0:T(8,128)(2,1)} async-done(((bf16[256,1152]{1,0:T(8,128)(2,1)}), bf16[1024,1152]{1,0:T(8,128)(2,1)}) %all-gather.75.cloned.1.call-update) | async-done | bytes 2359312 | tf_op jit(solution)/shard_map/all_gather | solution.py:162
  1289.6 34.9 %all-gather.53.cloned.1.call-done = bf16[1024,1152]{1,0:T(8,128)(2,1)} async-done(((bf16[256,1152]{1,0:T(8,128)(2,1)}), bf16[1024,1152]{1,0:T(8,128)(2,1)}) %all-gather.53.cloned.1.call-update) | async-done | bytes 2359312 | tf_op jit(solution)/shard_map/all_gather | solution.py:126
  1332.1 43.2 %all-gather.81.cloned.1.call-done = bf16[1,1024,1152]{2,1,0:T(8,128)(2,1)} async-done(((bf16[1,256,1152]{2,1,0:T(8,128)(2,1)}), bf16[1,1024,1152]{2,1,0:T(8,128)(2,1)}) %all-gather.81.cloned.1.call-update) | async-done | bytes 2359312 | tf_op jit(solution)/shard_map/all_gather | solution.py:127
  1473.1 49.9 %reduce-scatter.55.cloned.1.call-done = bf16[256,1152]{1,0:T(8,128)(2,1)} async-done(((bf16[1024,1152]{1,0:T(8,128)(2,1)}), bf16[256,1152]{1,0:T(8,128)(2,1)}) %reduce-scatter.55.cloned.1.call-update) | async-done | bytes 589840 | tf_op jit(solution)/shard_map/reduce_scatter | solution.py:146
  1523.0 49.7 %reduce-scatter.69.cloned.1.call-done = bf16[256,1152]{1,0:T(8,128)(2,1)} async-done(((bf16[1024,1152]{1,0:T(8,128)(2,1)}), bf16[256,1152]{1,0:T(8,128)(2,1)}) %reduce-scatter.69.cloned.1.call-update) | async-done | bytes 589840 | tf_op jit(solution)/shard_map/reduce_scatter | solution.py:208
  1576.8 45.6 %reduce-scatter.37.cloned.1.call-done = bf16[256,1152]{1,0:T(8,128)(2,1)} async-done(((bf16[1024,1152]{1,0:T(8,128)(2,1)}), bf16[256,1152]{1,0:T(8,128)(2,1)}) %reduce-scatter.37.cloned.1.call-update) | async-done | bytes 589840 | tf_op jit(solution)/shard_map/reduce_scatter | solution.py:132
  1625.6 47.3 %reduce-scatter.45.cloned.1.call-done = bf16[256,1152]{1,0:T(8,128)(2,1)} async-done(((bf16[1024,1152]{1,0:T(8,128)(2,1)}), bf16[256,1152]{1,0:T(8,128)(2,1)}) %reduce-scatter.45.cloned.1.call-update) | async-done | bytes 589840 | tf_op jit(solution)/shard_map/reduce_scatter | solution.py:132
  1681.9 48.1 %all-gather.71.cloned.1.call-done = bf16[1024,1152]{1,0:T(8,128)(2,1)} async-done(((bf16[256,1152]{1,0:T(8,128)(2,1)}), bf16[1024,1152]{1,0:T(8,128)(2,1)}) %all-gather.71.cloned.1.call-update) | async-done | bytes 2359312 | tf_op jit(solution)/shard_map/all_gather | solution.py:162
  1783.6 48.8 %all-gather.73.cloned.1.call-done = bf16[1024,1152]{1,0:T(8,128)(2,1)} async-done(((bf16[256,1152]{1,0:T(8,128)(2,1)}), bf16[1024,1152]{1,0:T(8,128)(2,1)}) %all-gather.73.cloned.1.call-update) | async-done | bytes 2359312 | tf_op jit(solution)/shard_map/all_gather | solution.py:162
  1891.4 28.6 %multiply_convert_fusion.3 = bf16[4,1024,2048]{2,1,0:T(8,128)(2,1)} fusion(f32[4,1024,2048]{2,1,0:T(8,128)} %get-tuple-element.137, f32[4,1024]{1,0:T(4,128)S(1)} %get-tuple-element.136, f32[4,1024,2048]{2,1,0:T(8,128)} %get-tuple-element.127, f32[4,1024]{1,0:T(4,128)S(1)} %copy-done.125), kind=kLoop, calls=%fused_computation.10 | loop fusion | flops 33554432 | bytes 83918848 | tf_op jit(solution)/shard_map/convert_element_type | solution.py:177
  1951.7 28.3 %multiply_convert_fusion.2 = bf16[4,1024,2048]{2,1,0:T(8,128)(2,1)} fusion(f32[4,1024,2048]{2,1,0:T(8,128)} %get-tuple-element.139, f32[4,1024]{1,0:T(4,128)S(1)} %get-tuple-element.138, f32[4,1024,2048]{2,1,0:T(8,128)} %get-tuple-element.131, f32[4,1024]{1,0:T(4,128)S(1)} %copy-done.130), kind=kLoop, calls=%fused_computation.8 | loop fusion | flops 33554432 | bytes 83918848 | tf_op jit(solution)/shard_map/convert_element_type | solution.py:177
  2209.9 31.4 %reduce-scatter.79.cloned.1.call-done = bf16[144,288]{1,0:T(8,128)(2,1)} async-done(((bf16[1152,288]{1,0:T(8,128)(2,1)}), bf16[144,288]{1,0:T(8,128)(2,1)}) %reduce-scatter.79.cloned.1.call-update) | async-done | bytes 82960 | tf_op jit(solution)/shard_map/reduce_scatter | solution.py:220
  2247.4 32.2 %reduce-scatter.83.cloned.1.call-done = bf16[144,288]{1,0:T(8,128)(2,1)} async-done(((bf16[1152,288]{1,0:T(8,128)(2,1)}), bf16[144,288]{1,0:T(8,128)(2,1)}) %reduce-scatter.83.cloned.1.call-update) | async-done | bytes 82960 | tf_op jit(solution)/shard_map/reduce_scatter | solution.py:226
  2281.3 36.9 %reduce-scatter.81.cloned.1.call-done = bf16[144,288]{1,0:T(8,128)(2,1)} async-done(((bf16[1152,288]{1,0:T(8,128)(2,1)}), bf16[144,288]{1,0:T(8,128)(2,1)}) %reduce-scatter.81.cloned.1.call-update) | async-done | bytes 82960 | tf_op jit(solution)/shard_map/reduce_scatter | solution.py:223
  2319.8 48.8 %reduce-scatter.53.cloned.1.call-done = bf16[256,1152]{1,0:T(8,128)(2,1)} async-done(((bf16[1024,1152]{1,0:T(8,128)(2,1)}), bf16[256,1152]{1,0:T(8,128)(2,1)}) %reduce-scatter.53.cloned.1.call-update) | async-done | bytes 589840 | tf_op jit(solution)/shard_map/reduce_scatter | solution.py:208
  2368.6 49.9 %reduce-scatter.61.cloned.1.call-done = bf16[256,1152]{1,0:T(8,128)(2,1)} async-done(((bf16[1024,1152]{1,0:T(8,128)(2,1)}), bf16[256,1152]{1,0:T(8,128)(2,1)}) %reduce-scatter.61.cloned.1.call-update) | async-done | bytes 589840 | tf_op jit(solution)/shard_map/reduce_scatter | solution.py:208
  2418.5 49.9 %reduce-scatter.77.cloned.1.call-done = bf16[256,1152]{1,0:T(8,128)(2,1)} async-done(((bf16[1024,1152]{1,0:T(8,128)(2,1)}), bf16[256,1152]{1,0:T(8,128)(2,1)}) %reduce-scatter.77.cloned.1.call-update) | async-done | bytes 589840 | tf_op jit(solution)/shard_map/reduce_scatter | solution.py:208
  2483.4 42.4 %all-reduce = (f32[1152]{0:T(1024)}, f32[1152]{0:T(1024)}, f32[1152]{0:T(1024)}, f32[1152]{0:T(1024)}, f32[1152]{0:T(1024)}, /*index=5*/f32[1152]{0:T(1024)}, f32[1152]{0:T(1024)}, f32[4304]{0:T(1024)}, f32[1152]{0:T(1024)}) all-reduce(f32[1152]{0:T(1024)S(1)} %copy-done.115, ...), channel_id=1, replica_groups=mesh['fsdp'=4,'ctx'=2,'tp'=4] {'fsdp','ctx','tp'}, use_global_device_ids=true, to_apply=%region_72.73 | all-reduce | flops 13520 | bytes 108160 | tf_op jit(solution)/shard_map/psum | solution.py:242
  (779 shorter events, 1113.7 us)
Async XLA Ops:
  365.6 228.5 %all-gather.79.cloned.1.call-start = ((), (), s32[]{:S(2)}) async-start(), calls=%async_computation.82 | async-start | bytes 2949120 | tf_op jit(solution)/shard_map/all_gather | solution.py:127
  367.1 253.0 %all-gather.45.cloned.1.call-start = ((), (), s32[]{:S(2)}) async-start(), calls=%async_computation.36 | async-start | bytes 3317760 | tf_op jit(solution)/shard_map/all_gather | solution.py:51
  367.6 304.4 %all-gather.61.cloned.1.call-start = ((), (), s32[]{:S(2)}) async-start(), calls=%async_computation.48 | async-start | bytes 2949120 | tf_op jit(solution)/shard_map/all_gather | solution.py:126
  368.2 354.6 %all-gather.83.cloned.1.call-start = ((), (), s32[]{:S(2)}) async-start(), calls=%async_computation.84 | async-start | bytes 2949120 | tf_op jit(solution)/shard_map/all_gather | solution.py:127
  368.8 380.5 %all-gather.67.cloned.1.call-start = ((), (), s32[]{:S(2)}) async-start(), calls=%async_computation.52 | async-start | bytes 1769472 | tf_op jit(solution)/shard_map/all_gather | solution.py:89
  417.3 352.8 %all-gather.65.cloned.1.call-start = ((), (), s32[]{:S(2)}) async-start(), calls=%async_computation.51 | async-start | bytes 1769472 | tf_op jit(solution)/shard_map/all_gather | solution.py:90
  420.8 380.8 %all-gather.51.cloned.1.call-start = ((), (), s32[]{:S(2)}) async-start(), calls=%async_computation.40 | async-start | bytes 1769472 | tf_op jit(solution)/shard_map/all_gather | solution.py:89
  468.6 352.8 %all-gather.49.cloned.1.call-start = ((), (), s32[]{:S(2)}) async-start(), calls=%async_computation.39 | async-start | bytes 1769472 | tf_op jit(solution)/shard_map/all_gather | solution.py:90
  473.0 396.7 %reduce-scatter.47.cloned.1.call-start = ((), (), s32[]{:S(2)}) async-start(), calls=%async_computation.56 | async-start | bytes 2949120 | tf_op jit(solution)/shard_map/reduce_scatter | solution.py:146
  637.9 282.2 %reduce-scatter.63.cloned.1.call-start = ((), (), s32[]{:S(2)}) async-start(), calls=%async_computation.66 | async-start | bytes 2949120 | tf_op jit(solution)/shard_map/reduce_scatter | solution.py:146
  739.0 231.0 %reduce-scatter.43.cloned.1.call-start = ((), (), s32[]{:S(2)}) async-start(), calls=%async_computation.53 | async-start | bytes 2949120 | tf_op jit(solution)/shard_map/reduce_scatter | solution.py:119
  791.1 228.7 %reduce-scatter.35.cloned.1.call-start = ((), (), s32[]{:S(2)}) async-start(), calls=%async_computation.41 | async-start | bytes 2949120 | tf_op jit(solution)/shard_map/reduce_scatter | solution.py:119
  840.8 228.8 %reduce-scatter.41.cloned.1.call-start = ((), (), s32[]{:S(2)}) async-start(), calls=%async_computation.49 | async-start | bytes 2949120 | tf_op jit(solution)/shard_map/reduce_scatter | solution.py:132
  849.9 269.5 %reduce-scatter.33.cloned.1.call-start = ((), (), s32[]{:S(2)}) async-start(), calls=%async_computation.37 | async-start | bytes 2949120 | tf_op jit(solution)/shard_map/reduce_scatter | solution.py:132
  858.8 311.9 %all-gather.75.cloned.1.call-start = ((), (), s32[]{:S(2)}) async-start(), calls=%async_computation.67 | async-start | bytes 2949120 | tf_op jit(solution)/shard_map/all_gather | solution.py:162
  1126.3 198.1 %all-gather.53.cloned.1.call-start = ((), (), s32[]{:S(2)}) async-start(), calls=%async_computation.42 | async-start | bytes 2949120 | tf_op jit(solution)/shard_map/all_gather | solution.py:126
  1126.9 248.4 %all-gather.81.cloned.1.call-start = ((), (), s32[]{:S(2)}) async-start(), calls=%async_computation.83 | async-start | bytes 2949120 | tf_op jit(solution)/shard_map/all_gather | solution.py:127
  1127.7 279.6 %reduce-scatter.65.cloned.1.call-start = ((), (), s32[]{:S(2)}) async-start(), calls=%async_computation.68 | async-start | bytes 1769472 | tf_op jit(solution)/shard_map/reduce_scatter | solution.py:191
  1233.2 189.0 %reduce-scatter.67.cloned.1.call-start = ((), (), s32[]{:S(2)}) async-start(), calls=%async_computation.69 | async-start | bytes 1769472 | tf_op jit(solution)/shard_map/reduce_scatter | solution.py:194
  1249.8 223.3 %reduce-scatter.71.cloned.1.call-start = ((), (), s32[]{:S(2)}) async-start(), calls=%async_computation.71 | async-start | bytes 2949120 | tf_op jit(solution)/shard_map/reduce_scatter | solution.py:146
  1289.3 233.7 %reduce-scatter.55.cloned.1.call-start = ((), (), s32[]{:S(2)}) async-start(), calls=%async_computation.61 | async-start | bytes 2949120 | tf_op jit(solution)/shard_map/reduce_scatter | solution.py:146
  1427.8 194.6 %reduce-scatter.37.cloned.1.call-start = ((), (), s32[]{:S(2)}) async-start(), calls=%async_computation.43 | async-start | bytes 2949120 | tf_op jit(solution)/shard_map/reduce_scatter | solution.py:132
  1436.1 236.8 %reduce-scatter.45.cloned.1.call-start = ((), (), s32[]{:S(2)}) async-start(), calls=%async_computation.55 | async-start | bytes 2949120 | tf_op jit(solution)/shard_map/reduce_scatter | solution.py:132
  1445.1 285.0 %all-gather.71.cloned.1.call-start = ((), (), s32[]{:S(2)}) async-start(), calls=%async_computation.57 | async-start | bytes 2949120 | tf_op jit(solution)/shard_map/all_gather | solution.py:162
  1681.4 462.1 %reduce-scatter.51.cloned.1.call-start = ((), (), s32[]{:S(2)}) async-start(), calls=%async_computation.59 | async-start | bytes 1769472 | tf_op jit(solution)/shard_map/reduce_scatter | solution.py:194
  1749.3 398.6 %reduce-scatter.59.cloned.1.call-start = ((), (), s32[]{:S(2)}) async-start(), calls=%async_computation.64 | async-start | bytes 1769472 | tf_op jit(solution)/shard_map/reduce_scatter | solution.py:194
  1869.3 285.4 %reduce-scatter.75.cloned.1.call-start = ((), (), s32[]{:S(2)}) async-start(), calls=%async_computation.74 | async-start | bytes 1769472 | tf_op jit(solution)/shard_map/reduce_scatter | solution.py:194
  1891.4 268.1 %reduce-scatter.49.cloned.1.call-start = ((), (), s32[]{:S(2)}) async-start(), calls=%async_computation.58 | async-start | bytes 1769472 | tf_op jit(solution)/shard_map/reduce_scatter | solution.py:191
  1951.6 212.3 %reduce-scatter.57.cloned.1.call-start = ((), (), s32[]{:S(2)}) async-start(), calls=%async_computation.63 | async-start | bytes 1769472 | tf_op jit(solution)/shard_map/reduce_scatter | solution.py:191
  2175.5 193.1 %reduce-scatter.53.cloned.1.call-start = ((), (), s32[]{:S(2)}) async-start(), calls=%async_computation.60 | async-start | bytes 2949120 | tf_op jit(solution)/shard_map/reduce_scatter | solution.py:208
  2182.2 236.3 %reduce-scatter.61.cloned.1.call-start = ((), (), s32[]{:S(2)}) async-start(), calls=%async_computation.65 | async-start | bytes 2949120 | tf_op jit(solution)/shard_map/reduce_scatter | solution.py:208
  2189.5 278.8 %reduce-scatter.77.cloned.1.call-start = ((), (), s32[]{:S(2)}) async-start(), calls=%async_computation.75 | async-start | bytes 2949120 | tf_op jit(solution)/shard_map/reduce_scatter | solution.py:208
  (246 other events, 9267.9 us)
Sparse Core Ops, SparseCore 0:
  11.2 53.1 all-gather.34
  136.3 48.0 reduce-scatter.30
  187.2 49.9 all-gather.54
  309.1 48.0 reduce-scatter.38
  363.8 49.9 all-gather.62
  415.8 49.2 all-gather.46
  492.7 50.4 all-gather.40
  544.8 49.2 all-gather.78
  621.5 50.4 all-gather.60
  673.5 49.2 all-gather.82
  821.6 48.0 reduce-scatter.46
  872.5 47.5 reduce-scatter.62
  922.4 47.5 reduce-scatter.42
  972.2 47.5 reduce-scatter.34
  1022.0 47.5 reduce-scatter.40
  1071.8 47.5 reduce-scatter.32
  1120.7 49.9 all-gather.74
  1172.9 49.2 all-gather.68
  1223.8 49.2 all-gather.84
  1275.1 49.2 all-gather.52
  1326.0 49.2 all-gather.80
  1425.0 48.0 reduce-scatter.70
  1475.4 47.5 reduce-scatter.54
  1525.1 47.5 reduce-scatter.68
  1574.9 47.5 reduce-scatter.36
  1625.3 47.5 reduce-scatter.44
  1680.0 49.9 all-gather.70
  1731.6 49.2 all-gather.76
  1783.1 49.2 all-gather.72
  2320.5 48.0 reduce-scatter.52
  2370.9 47.5 reduce-scatter.60
  2420.8 47.5 reduce-scatter.76
  (24 shorter events, 618.2 us)
where the time goes:
time: 2540 us; the launch traced here: 2530 us
  waiting for transfers between devices  1480 us (58%)
  matrix products  702 us (28%)
  other arithmetic  204 us (8%)
  blocking collectives  100 us (4%)
    dot_general x72, matrix products, matmul(): return jnp.dot(left, right, preferred_element_type=jnp.float32)  320 us
    reduce_scatter x4, waiting for transfers between devices, shards(): lax.psum_scatter(normed_term.astype(jnp.bfloat16), 'tp', scatter_dimensio...  198 us
    reduce_scatter x4, waiting for transfers between devices, shards(): lax.psum_scatter(matmul(attended, wo_all).astype(jnp.bfloat16), 'tp', sca...  196 us
    reduce_scatter x4, waiting for transfers between devices, shards(): lax.psum_scatter(matmul(active, second_use).astype(jnp.bfloat16), 'tp', s...  178 us
    all_gather x4, waiting for transfers between devices, shards(): d_attention_all = lax.all_gather(d_attention, 'tp', axis=0, tiled=True)  163 us
    all_gather x4, waiting for transfers between devices, shards(): normed_all = lax.all_gather(normed, 'tp', axis=0, tiled=True)  161 us
    all_gather x4, waiting for transfers between devices, shards(): lax.all_gather(row_cot, 'tp', axis=0, tiled=True)  145 us
    reduce_scatter x4, waiting for transfers between devices, shards(): lax.psum_scatter(matmul(d_before, first_use.T).astype(jnp.bfloat16), 'tp'...  138 us
  transfers between devices with their start and end apart: 56, of which 41 were waited for; matrix products, arithmetic and copies ran while one was open for 33% of the time, Pallas kernels for 0%

commit v1 on v0

v1 whole, which is shorter than its diff:
```python
import functools

import jax
import jax.numpy as jnp
from jax import lax
from jax.experimental import pallas as pl
from jax.experimental.pallas import tpu as pltpu
from jax.sharding import PartitionSpec as P

HD = 72
EPSILON = 1e-06
LOG2E = 1.4426950408889634
NEG = -1e30
F32 = jnp.float32
BF16 = jnp.bfloat16


def dot(left, right, left_dim, right_dim):
    return lax.dot_general(
        left, right, (((left_dim,), (right_dim,)), ((), ())), preferred_element_type=F32
    )


def forward_kernel(nq, nk, bq, bk, count, index, q_ref, k_ref, v_ref, qid_ref, kid_ref, o_ref, lse_ref, kt):
    factor = HD ** (-0.5) * LOG2E
    kt[...] = k_ref[...].astype(F32).T.astype(BF16)
    for qb in range(nq):
        cols = pl.ds(qb * bq, bq)
        q = q_ref[:, cols]
        qid = qid_ref[:, cols]

        def body(n, carry):
            top, total, acc = carry
            off = pl.multiple_of(index[qb * nk + n] * bk, bk)
            s = dot(kt[pl.ds(off, bk), :], q, 1, 0) * factor
            s = jnp.where(kid_ref[pl.ds(off, bk), :] == qid, s, NEG)
            new = jnp.maximum(top, jnp.max(s, axis=0, keepdims=True))
            p = jnp.exp2(s - new)
            alpha = jnp.exp2(top - new)
            total = total * alpha + jnp.sum(p, axis=0, keepdims=True)
            acc = acc * alpha + dot(v_ref[:, pl.ds(off, bk)], p.astype(BF16), 1, 0)
            return new, total, acc

        top, total, acc = lax.fori_loop(
            0,
            count[qb],
            body,
            (jnp.full((1, bq), 4 * NEG, F32), jnp.zeros((1, bq), F32), jnp.zeros((HD, bq), F32)),
        )
        o_ref[:, cols] = (acc / total).astype(BF16)
        lse_ref[:, cols] = top + jnp.log2(total)


def backward_kernel(
    nq, nk, bq, bk, count, index, q_ref, k_ref, v_ref, do_ref, o_ref, lse_ref, qid_ref, kid_ref,
    dq_ref, dk_ref, dv_ref, kt, vt, dk_acc, dv_acc
):
    factor = HD ** (-0.5) * LOG2E
    kt[...] = k_ref[...].astype(F32).T.astype(BF16)
    vt[...] = v_ref[...].astype(F32).T.astype(BF16)
    dk_acc[...] = jnp.zeros_like(dk_acc)
    dv_acc[...] = jnp.zeros_like(dv_acc)
    for qb in range(nq):
        cols = pl.ds(qb * bq, bq)
        q = q_ref[:, cols]
        do = do_ref[:, cols]
        qid = qid_ref[:, cols]
        lse = lse_ref[:, cols]
        delta = jnp.sum(do.astype(F32) * o_ref[:, cols].astype(F32), axis=0, keepdims=True)

        def body(n, dq):
            off = pl.multiple_of(index[qb * nk + n] * bk, bk)
            rows = pl.ds(off, bk)
            s = dot(kt[rows, :], q, 1, 0) * factor
            p = jnp.exp2(jnp.where(kid_ref[rows, :] == qid, s, NEG) - lse)
            dp = dot(vt[rows, :], do, 1, 0)
            ds = (p * (dp - delta)).astype(BF16)
            dv_acc[:, rows] += dot(do, p.astype(BF16), 1, 1)
            dk_acc[:, rows] += dot(q, ds, 1, 1)
            return dq + dot(k_ref[:, rows], ds, 1, 0)

        dq = lax.fori_loop(0, count[qb], body, jnp.zeros((HD, bq), F32))
        dq_ref[:, cols] = (dq * HD ** (-0.5)).astype(BF16)
    dk_ref[...] = (dk_acc[...] * HD ** (-0.5)).astype(BF16)
    dv_ref[...] = dv_acc[...].astype(BF16)


def attention_forward(count, index, qt, kvt, qid, kid, bq, bk):
    width, tokens = qt.shape
    context = kvt.shape[1]
    heads = width // HD
    nq, nk = tokens // bq, context // bk
    q_spec = pl.BlockSpec((HD, tokens), lambda h, *_: (h, 0))
    k_spec = pl.BlockSpec((HD, context), lambda h, *_: (h, 0))
    v_spec = pl.BlockSpec((HD, context), lambda h, *_: (heads + h, 0))
    whole = lambda shape: pl.BlockSpec(shape, lambda h, *_: (0, 0))
    lse_spec = pl.BlockSpec((None, 1, tokens), lambda h, *_: (h, 0, 0))
    return pl.pallas_call(
        functools.partial(forward_kernel, nq, nk, bq, bk),
        out_shape=(
            jax.ShapeDtypeStruct((width, tokens), BF16),
            jax.ShapeDtypeStruct((heads, 1, tokens), F32),
        ),
        grid_spec=pltpu.PrefetchScalarGridSpec(
            num_scalar_prefetch=2,
            grid=(heads,),
            in_specs=[q_spec, k_spec, v_spec, whole((1, tokens)), whole((context, 1))],
            out_specs=(q_spec, lse_spec),
            scratch_shapes=[pltpu.VMEM((context, HD), BF16)],
        ),
        compiler_params=pltpu.CompilerParams(vmem_limit_bytes=48 << 20),
        cost_estimate=pl.CostEstimate(
            flops=tokens * context * width * 8, bytes_accessed=width * (tokens + context) * 4,
            transcendentals=tokens * context * heads // 2,
        ),
        name="attention_forward",
    )(count, index, qt, kvt, kvt, qid, kid)


def attention_backward(count, index, qt, kvt, dot_, ot, lse, qid, kid, bq, bk):
    width, tokens = qt.shape
    context = kvt.shape[1]
    heads = width // HD
    nq, nk = tokens // bq, context // bk
    q_spec = pl.BlockSpec((HD, tokens), lambda h, *_: (h, 0))
    k_spec = pl.BlockSpec((HD, context), lambda h, *_: (h, 0))
    v_spec = pl.BlockSpec((HD, context), lambda h, *_: (heads + h, 0))
    whole = lambda shape: pl.BlockSpec(shape, lambda h, *_: (0, 0))
    lse_spec = pl.BlockSpec((None, 1, tokens), lambda h, *_: (h, 0, 0))
    return pl.pallas_call(
        functools.partial(backward_kernel, nq, nk, bq, bk),
        out_shape=(
            jax.ShapeDtypeStruct((width, tokens), BF16),
            jax.ShapeDtypeStruct((width, context), BF16),
            jax.ShapeDtypeStruct((width, context), BF16),
        ),
        grid_spec=pltpu.PrefetchScalarGridSpec(
            num_scalar_prefetch=2,
            grid=(heads,),
            in_specs=[
                q_spec, k_spec, v_spec, q_spec, q_spec, lse_spec, whole((1, tokens)), whole((context, 1)),
            ],
            out_specs=(q_spec, k_spec, k_spec),
            scratch_shapes=[
                pltpu.VMEM((context, HD), BF16),
                pltpu.VMEM((context, HD), BF16),
                pltpu.VMEM((HD, context), F32),
                pltpu.VMEM((HD, context), F32),
            ],
        ),
        compiler_params=pltpu.CompilerParams(vmem_limit_bytes=48 << 20),
        cost_estimate=pl.CostEstimate(
            flops=tokens * context * width * 20, bytes_accessed=width * (tokens + context) * 8,
            transcendentals=tokens * context * heads // 2,
        ),
        name="attention_backward",
    )(count, index, qt, kvt, kvt, dot_, ot, lse, qid, kid)


def active_blocks(qid, kid, bq, bk):
    q = qid.reshape(-1, bq)
    k = kid.reshape(-1, bk)
    q_low, q_high = jnp.min(q, 1)[:, None], jnp.max(q, 1)[:, None]
    k_low, k_high = jnp.min(k, 1)[None, :], jnp.max(k, 1)[None, :]
    active = (q_low <= k_high) & (k_low <= q_high)
    slots = jnp.arange(k.shape[0], dtype=jnp.int32)
    before = (slots[:, None] < slots[None, :])[None]
    place = jnp.sum((active[:, :, None] & before).astype(jnp.int32), axis=1)
    hit = active[:, None, :] & (place[:, None, :] == slots[None, :, None])
    index = jnp.sum(jnp.where(hit, slots[None, None, :], 0), axis=2)
    return jnp.sum(active.astype(jnp.int32), axis=1), index.reshape(-1)


def norm_stats(values):
    centred = values - jnp.mean(values, axis=-1, keepdims=True)
    inverse = lax.rsqrt(jnp.mean(centred * centred, axis=-1, keepdims=True) + EPSILON)
    return centred * inverse, inverse


def norm_back(grad, scaled, inverse, gain):
    wide = grad * gain
    return inverse * (
        wide
        - jnp.mean(wide, axis=-1, keepdims=True)
        - scaled * jnp.mean(wide * scaled, axis=-1, keepdims=True)
    )


def gelu_pair(pre):
    c = 0.7978845608028654
    square = pre * pre
    t = jnp.tanh(c * pre * (1.0 + 0.044715 * square))
    value = 0.5 * pre * (1.0 + t)
    slope = 0.5 * (1.0 + t) + 0.5 * pre * (1.0 - t * t) * c * (1.0 + 3 * 0.044715 * square)
    return value, slope


def shards(
    sizes,
    tokens,
    picture,
    ln1_gain,
    ln1_bias,
    w_query,
    b_query,
    w_key,
    w_value,
    b_value,
    w_output,
    b_output,
    ln2_gain,
    ln2_bias,
    w_first,
    b_first,
    w_second,
    b_second,
    cotangent,
):
    tp, ctx = sizes["tp"], sizes["ctx"]
    rows, span, width = tokens.shape
    group = tp // rows
    place = lax.axis_index("tp")
    mine = place % rows
    row = place // group
    part = place % group

    def out_permutation(k):
        return [(s * rows + j, ((j + k) % rows) * group + s) for s in range(group) for j in range(rows)]

    def gather_row(blocks):
        got = []
        for k in range(rows):
            piece = lax.dynamic_index_in_dim(blocks, (mine + k) % rows, 0, keepdims=False)
            pairs = out_permutation(k)
            if any(a != b for a, b in pairs):
                piece = lax.ppermute(piece, "tp", pairs)
            got.append(piece)
        return got

    def scatter_row(values):
        out = jnp.zeros((rows, span) + values.shape[1:], values.dtype)
        for k in range(rows):
            piece = values[k * span : (k + 1) * span]
            pairs = [(b, a) for a, b in out_permutation(k)]
            if any(a != b for a, b in pairs):
                piece = lax.ppermute(piece, "tp", pairs)
            out = lax.dynamic_update_index_in_dim(out, piece, (mine + k) % rows, 0)
        return out

    def peers(step):
        s_step, c_step = step % group, step // group
        return s_step, c_step

    def fetch(value, step):
        s_step, c_step = peers(step)
        if s_step:
            pairs = [(r * group + (s + s_step) % group, r * group + s) for r in range(rows) for s in range(group)]
            value = lax.ppermute(value, "tp", pairs)
        if c_step:
            value = lax.ppermute(value, "ctx", [((c + c_step) % ctx, c) for c in range(ctx)])
        return value

    def give(value, step):
        s_step, c_step = peers(step)
        if s_step:
            pairs = [(r * group + s, r * group + (s + s_step) % group) for r in range(rows) for s in range(group)]
            value = lax.ppermute(value, "tp", pairs)
        if c_step:
            value = lax.ppermute(value, "ctx", [(c, (c + c_step) % ctx) for c in range(ctx)])
        return value

    steps = group * ctx

    heads_dev = w_query.shape[1]
    both = ("tp", "fsdp")
    qkvo = lax.all_gather(
        jnp.concatenate([w_query, w_key, w_value, w_output.T], axis=1), both, axis=0, tiled=True
    ).reshape(tp, width, 4, heads_dev)
    qkvo = qkvo.transpose(2, 0, 3, 1).reshape(4, tp * heads_dev, width)
    wq, wkv, wo = qkvo[0], qkvo[1:3].reshape(2 * tp * heads_dev, width), qkvo[3]
    units = w_first.shape[1]
    first = lax.all_gather(w_first, both, axis=0, tiled=True).reshape(tp, width, units)
    second = lax.all_gather(w_second.T, both, axis=0, tiled=True).reshape(tp, width, units)

    x16 = jnp.concatenate(gather_row(tokens), axis=0)
    count = rows * span
    ids = lax.dynamic_index_in_dim(picture, row, 0, keepdims=False).reshape(tp, span)
    order = part * rows + (row - jnp.arange(rows)) % rows
    ids = jnp.take(ids, order, axis=0).reshape(count)
    cot = jnp.concatenate(gather_row(cotangent), axis=0)
    x_all16 = jnp.concatenate([x16] + [fetch(x16, i) for i in range(1, steps)], axis=0)
    kid = jnp.concatenate([ids] + [fetch(ids, i) for i in range(1, steps)], axis=0)
    block = 256 if count % 256 == 0 else count
    blocks, index = active_blocks(ids, kid, block, block)
    qid, kid = ids[None, :], kid[:, None]

    x_all = x_all16.astype(F32)
    scaled_all, inverse_all = norm_stats(x_all)
    n1 = (scaled_all * ln1_gain + ln1_bias).astype(BF16)
    qt = (dot(wq, n1[:count], 1, 1) + b_query[:, None]).astype(BF16)
    kv_bias = jnp.concatenate([jnp.zeros_like(b_value), b_value])
    kvt = (dot(wkv, n1, 1, 1) + kv_bias[:, None]).astype(BF16)
    ot, lse = attention_forward(blocks, index, qt, kvt, qid, kid, block, block)
    h = x_all[:count] + (dot(ot, wo, 0, 0) + b_output)

    scaled2, inverse2 = norm_stats(h)
    n2 = (scaled2 * ln2_gain + ln2_bias).astype(BF16)
    y = h + b_second
    d_n2 = jnp.zeros_like(h)
    g_first, g_second, g_first_bias = [], [], []
    for t in range(tp):
        pre = dot(n2, first[t], 1, 0) + b_first[t * units : (t + 1) * units]
        value, slope = gelu_pair(pre)
        act = value.astype(BF16)
        y = y + dot(act, second[t], 1, 1)
        d_pre = (dot(cot, second[t], 1, 0) * slope).astype(BF16)
        d_n2 = d_n2 + dot(d_pre, first[t], 1, 1)
        g_second.append(dot(cot, act, 0, 0).astype(BF16))
        g_first.append(dot(n2, d_pre, 0, 0).astype(BF16))
        g_first_bias.append(jnp.sum(d_pre.astype(F32), axis=0))
    every = ("tp", "fsdp", "ctx")

    def scatter_grad(parts):
        return lax.psum_scatter(
            jnp.concatenate(parts, axis=0), every, scatter_dimension=0, tiled=True
        ).astype(F32)

    g_second = scatter_grad(g_second).T
    g_first = scatter_grad(g_first)
    output = scatter_row(y.astype(BF16))
    cot32 = cot.astype(F32)
    g_g2 = jnp.sum(d_n2 * scaled2, axis=0)
    g_c2 = jnp.sum(d_n2, axis=0)
    d_h = cot32 + norm_back(d_n2, scaled2, inverse2, ln2_gain)
    g_bs = jnp.sum(cot32, axis=0)

    d_att = d_h.astype(BF16)
    g_bo = jnp.sum(d_att.astype(F32), axis=0)
    d_ot = dot(wo, d_att, 1, 1).astype(BF16)
    dqt, dkt, dvt = attention_backward(blocks, index, qt, kvt, d_ot, ot, lse, qid, kid, block, block)
    d_all = dot(dkt, wkv[: tp * heads_dev], 0, 0) + dot(dvt, wkv[tp * heads_dev :], 0, 0)
    d_n1 = d_all[:count] + dot(dqt, wq, 0, 0)
    for i in range(1, steps):
        d_n1 = d_n1 + give(d_all[i * count : (i + 1) * count].astype(BF16), i).astype(F32)
    g_query = dot(n1[:count], dqt, 0, 1)
    g_key = dot(n1, dkt, 0, 1)
    g_value = dot(n1, dvt, 0, 1)
    g_out = dot(d_att, ot, 0, 1)
    g_bq = jnp.sum(dqt.astype(F32), axis=1)
    g_bv = jnp.sum(dvt.astype(F32), axis=1)

    def split(grad):
        return grad.astype(BF16).reshape(width, tp, heads_dev).transpose(1, 0, 2).reshape(tp * width, heads_dev)

    g_out = scatter_grad([split(g_out)]).T
    g_query, g_key, g_value = (scatter_grad([split(v)]) for v in (g_query, g_key, g_value))

    scaled1, inverse1 = scaled_all[:count], inverse_all[:count]
    g_g1 = jnp.sum(d_n1 * scaled1, axis=0)
    g_c1 = jnp.sum(d_n1, axis=0)
    grad_tokens = d_h + norm_back(d_n1, scaled1, inverse1, ln1_gain)
    grad_tokens = scatter_row(grad_tokens.astype(BF16)).astype(F32)

    small = lax.psum(
        (g_g1, g_c1, g_bq, g_bv, g_bo, g_g2, g_c2, jnp.concatenate(g_first_bias), g_bs),
        ("fsdp", "ctx", "tp"),
    )
    g_g1, g_c1, g_bq, g_bv, g_bo, g_g2, g_c2, g_bf, g_bs = small
    return (
        output, grad_tokens, g_g1, g_c1, g_query, g_bq, g_key, g_value, g_bv, g_out, g_bo,
        g_g2, g_c2, g_first, g_bf, g_second, g_bs,
    )


def solution(mesh):
    rows_spec = P("fsdp", ("ctx", "tp"), None)
    column, line = P("fsdp", "tp"), P("tp", "fsdp")
    column_out, line_out = P(("fsdp", "ctx"), "tp"), P("tp", ("fsdp", "ctx"))
    return jax.shard_map(
        functools.partial(shards, dict(mesh.shape)),
        mesh=mesh,
        in_specs=(
            rows_spec, P("fsdp", "ctx"), P(), P(), column, P(), column, column, P(), line, P(),
            P(), P(), column, P(), line, P(), rows_spec,
        ),
        out_specs=(
            rows_spec, rows_spec, P(), P(), column_out, P(), column_out, column_out, P(), line_out,
            P(), P(), P(), column_out, P(), line_out, P(),
        ),
        check_vma=False,
    )
```

time: 2540 us -> 1420 us (0.56)
  waiting for transfers between devices: 1480 us -> 543 us
  matrix products: 702 us -> 260 us
  Pallas kernels: 0 us -> 222 us
  other arithmetic: 204 us -> 52 us
  local copies, waits for them, and re-layouts: 24.4 us -> 139 us
  blocking collectives: 100 us -> 151 us
    reduce_scatter x30 -> x4, waiting for transfers between devices: 819 us -> 115 us  [scatter_grad(): lax.psum_scatter(jnp.concatenate(parts, axis=0), every, scatter_dimension...]
    all_gather x26 -> x3, waiting for transfers between devices: 650 us -> 21.5 us  [the longest x1 21.5 us: shards(): lax.all_gather(jnp.concatenate([w_query, w_key, w_value, w_output.T], axi...]
    dot_general x92 -> x35, matrix products: 624 us -> 260 us  [dot(): lax.dot_general(left, right, (((left_dim,), (right_dim,)), ((), ())), pre...]
    unnamed x56 -> x11, waiting for transfers between devices: 7.33 us -> 291 us
    pallas_call x0 -> x2, Pallas kernels: none -> 222 us  [the longest x1 114 us: attention_backward(): pl.pallas_call(functools.partial(backward_kernel, nq, nk, bq, bk), out_sh...]
    ppermute x0 -> x15, waiting for transfers between devices: none -> 115 us  [the longest x6 56.4 us: gather_row(): piece = lax.ppermute(piece, 'tp', pairs)]
    convert_element_type x14 -> x7, other arithmetic: 130 us -> 20.7 us  [the longest x2 6.98 us: shards(): grad_tokens = scatter_row(grad_tokens.astype(BF16)).astype(F32)]
    psum x1, blocking collectives: 42.4 us -> 151 us  [shards(): lax.psum((g_g1, g_c1, g_bq, g_bv, g_bo, g_g2, g_c2, jnp.concatenate(g_fir...]
  transfers between devices with their start and end apart: 56 -> 24, of which waited for: 41 -> 10; matrix products, arithmetic and copies ran while one was open for 33% -> 25% of each run, Pallas kernels for 0% -> 8%
where the time goes in v1:
time: 1420 us; the launch traced here: 1410 us
  waiting for transfers between devices  543 us (38%)
  matrix products  260 us (18%)
  Pallas kernels  222 us (16%)
  blocking collectives  151 us (11%)
  local copies, waits for them, and re-layouts  139 us (10%)
  other arithmetic  52 us (4%)
  starting transfers between devices  31.9 us (2%)
  between operations  15.4 us (1%)
    unnamed x11, waiting for transfers between devices  291 us
    dot_general x35, matrix products, dot(): lax.dot_general(left, right, (((left_dim,), (right_dim,)), ((), ())), pre...  260 us
    psum x1, blocking collectives, shards(): lax.psum((g_g1, g_c1, g_bq, g_bv, g_bo, g_g2, g_c2, jnp.concatenate(g_fir...  151 us
    reduce_scatter x4, waiting for transfers between devices, scatter_grad(): lax.psum_scatter(jnp.concatenate(parts, axis=0), every, scatter_dimension...  115 us
    pallas_call x1, Pallas kernels, attention_backward(): pl.pallas_call(functools.partial(backward_kernel, nq, nk, bq, bk), out_sh...  114 us
    pallas_call x1, Pallas kernels, attention_forward(): pl.pallas_call(functools.partial(forward_kernel, nq, nk, bq, bk), out_sha...  108 us
    ppermute x6, waiting for transfers between devices, gather_row(): piece = lax.ppermute(piece, 'tp', pairs)  56.4 us
    unnamed x153, local copies, waits for them, and re-layouts  46.7 us
  transfers between devices with their start and end apart: 24, of which 10 were waited for; matrix products, arithmetic and copies ran while one was open for 25% of the time, Pallas kernels for 8%

profile of v1, /device:TPU:0, one launch (start us, length us, event | category | flops | bytes accessed | tf_op | source)
XLA Modules:
  0.0 1413.1 jit_solution(12876104329089899275)
XLA Ops:
  22.5 16.7 %collective-permute-done = bf16[256,1152]{1,0:T(8,128)(2,1)S(1)} collective-permute-done((bf16[256,1152]{1,0:T(8,128)(2,1)}, bf16[256,1152]{1,0:T(8,128)(2,1)S(1)}, u32[]{:S(2)}, u32[]{:S(2)}) %collective-permute-start) | collective-permute-done | bytes 589856 | tf_op jit(solution)/shard_map/ppermute | solution.py:236
  39.2 39.6 %collective-permute-done.1 = bf16[256,1152]{1,0:T(8,128)(2,1)S(1)} collective-permute-done((bf16[256,1152]{1,0:T(8,128)(2,1)}, bf16[256,1152]{1,0:T(8,128)(2,1)S(1)}, u32[]{:S(2)}, u32[]{:S(2)}) %collective-permute-start.1) | collective-permute-done | bytes 589856 | tf_op jit(solution)/shard_map/ppermute | solution.py:236
  86.2 17.2 %collective-permute-start.10 = (bf16[256,1152]{1,0:T(8,128)(2,1)}, bf16[256,1152]{1,0:T(8,128)(2,1)}, u32[]{:S(2)}, u32[]{:S(2)}) collective-permute-start(bf16[256,1152]{1,0:T(8,128)(2,1)} %get-tuple-element.152), channel_id=1, source_target_pairs={{0,3},{1,0},{2,1},{3,2},{4,7},{5,4},{6,5},{7,6},{8,11},{9,8},{10,9... | collective-permute-start | bytes 1769480 | tf_op jit(solution)/shard_map/ppermute | solution.py:236
  104.1 29.8 %collective-permute-done.4 = s32[1024]{0:T(1024)S(1)} collective-permute-done((s32[1024]{0:T(1024)S(1)}, s32[1024]{0:T(1024)S(1)}, u32[]{:S(2)}, u32[]{:S(2)}) %collective-permute-start.4) | collective-permute-done | bytes 4128 | tf_op jit(solution)/shard_map/ppermute | solution.py:260
  156.0 21.5 %all-gather.4.cloned.1.call-done = bf16[4608,1152]{1,0:T(8,128)(2,1)} async-done(((bf16[288,1152]{1,0:T(8,128)(2,1)}), bf16[4608,1152]{1,0:T(8,128)(2,1)}) %all-gather.4.cloned.1.call-update) | async-done | bytes 10616848 | tf_op jit(solution)/shard_map/all_gather | solution.py:276
  177.4 15.4 %copy.87 = bf16[4608,1152]{0,1:T(8,128)(2,1)} copy(bf16[4608,1152]{1,0:T(8,128)(2,1)} %all-gather.4.cloned.1.call-done) | data formatting | bytes 21233664 | tf_op jit(solution)/shard_map/all_gather | solution.py:276
  192.8 14.7 %reshape.353 = bf16[4,1152,4,288]{1,0,3,2:T(4,128)(2,1)} reshape(bf16[4608,1152]{0,1:T(8,128)(2,1)} %copy.87) | data formatting | bytes 21233664 | tf_op jit(solution)/shard_map/reshape | solution.py:278
  229.8 14.6 %add_convert_fusion.k_ref.v_ref = bf16[2304,2048]{1,0:T(8,128)(2,1)} fusion(bf16[2304,1152]{1,0:T(8,128)(2,1)S(1)} %bitcast.123, bf16[2048,1152]{1,0:T(8,128)(2,1)S(1)} %bitcast.127, f32[2304]{0:T(1024)S(1)} %concatenate.38), kind=kOutput, calls=%fused_computation.1 | convolution fusion | flops 10881073152 | bytes 19473408 | tf_op jit(solution)/shard_map/dot_general | solution.py:19
  244.4 108.4 %attention_forward.1 = (bf16[1152,1024]{1,0:T(8,128)(2,1)S(1)}, f32[16,1,1024]{2,1,0:T(1,128)S(1)}) custom-call(s32[4]{0:T(128)S(1)} %get-tuple-element.135.count, s32[32]{0:T(128)S(1)} %reshape.352.index, bf16[1152,1024]{1,0:T(8,128)(2,1)S(1)} %add_convert_fusion.5.q_ref, bf16[2304,2048]{1,0:T(8,128)(2,1)} %add_convert_fusion.k_ref.v_ref, ...), custom_call_target="tpu_custom_call" | custom-call | flops 19327352832 | bytes 14155776 | tf_op jit(solution)/shard_map/attention_forward/pallas_call | solution.py:98
  385.8 10.6 convert_reduce_fusion.5
  396.5 9.5 convert_reduce_fusion.6
  409.8 9.9 convert_reduce_fusion.8
  425.1 10.8 convert_reduce_fusion.7
  443.4 11.9 multiply_reduce_fusion.1
  465.7 113.6 %attention_backward.1 = (bf16[1152,1024]{1,0:T(8,128)(2,1)S(1)}, bf16[1152,2048]{1,0:T(8,128)(2,1)}, bf16[1152,2048]{1,0:T(8,128)(2,1)}) custom-call(s32[4]{0:T(128)S(1)} %get-tuple-element.135.count, s32[32]{0:T(128)S(1)} %reshape.352.index, bf16[1152,1024]{1,0:T(8,128)(2,1)S(1)} %copy-done.7, bf16[2304,2048]{1,0:T(8,128)(2,1)} %add_convert_fusion.k_ref.v_ref, ...), custom_call_target="tpu_custom_call" | custom-call | flops 48318382080 | bytes 28311552 | tf_op jit(solution)/shard_map/attention_backward/pallas_call | solution.py:130
  585.8 9.5 convolution_convert_fusion.11
  598.4 10.6 convolution_convert_fusion.10
  648.4 14.3 %copy.101 = bf16[4608,1076]{1,0:T(8,128)(2,1)} copy(bf16[4608,1076]{0,1:T(8,128)(2,1)} %pad_maximum_fusion) | data formatting | bytes 19832832
  694.8 14.3 %copy.103 = bf16[4608,1076]{1,0:T(8,128)(2,1)} copy(bf16[4608,1076]{0,1:T(8,128)(2,1)} %pad_maximum_fusion.1) | data formatting | bytes 19832832
  709.1 11.0 fusion.46
  721.9 10.7 convolution_add_fusion
  734.3 13.4 fusion.10
  747.7 7.9 fusion.16
  755.6 8.0 fusion.22
  763.6 9.8 add_convert_fusion.3
  788.6 24.0 %collective-permute-done.6 = bf16[256,1152]{1,0:T(8,128)(2,1)} collective-permute-done((bf16[256,1152]{1,0:T(8,128)(2,1)S(1)}, bf16[256,1152]{1,0:T(8,128)(2,1)}, u32[]{:S(2)}, u32[]{:S(2)}) %collective-permute-start.6) | collective-permute-done | bytes 589856 | tf_op jit(solution)/shard_map/ppermute | solution.py:246
  814.5 9.9 multiply_reduce_fusion.2
  834.4 150.8 %all-reduce.1 = (f32[1152]{0:T(1024)}, f32[1152]{0:T(1024)}, f32[1152]{0:T(1024)}, f32[1152]{0:T(1024)}, f32[1152]{0:T(1024)}, /*index=5*/f32[1152]{0:T(1024)}, f32[1152]{0:T(1024)}, f32[4304]{0:T(1024)}, f32[1152]{0:T(1024)}) all-reduce(f32[1152]{0:T(1024)} %get-tuple-element.112, ...), channel_id=1, replica_groups=mesh['fsdp'=4,'ctx'=2,'tp'=4] {'fsdp','ctx','tp'}, use_global_device_ids=true, to_apply=%region_16.17 | all-reduce | flops 13520 | bytes 108160 | tf_op jit(solution)/shard_map/psum | solution.py:364
  993.4 8.8 reduce-scatter.15.cloned.1.call-done
  1003.8 106.0 %reduce-scatter.17.cloned.1.call-done = bf16[144,288]{1,0:T(8,128)(2,1)} async-done(((bf16[4608,288]{1,0:T(8,128)(2,1)}), bf16[144,288]{1,0:T(8,128)(2,1)}) %reduce-scatter.17.cloned.1.call-update) | async-done | bytes 82960 | tf_op jit(solution)/shard_map/reduce_scatter | solution.py:324
  1111.4 145.4 %reduce-scatter.19.cloned.1.call-done = bf16[144,1076]{1,0:T(8,128)(2,1)} async-done(((bf16[4608,1076]{1,0:T(8,128)(2,1)}), bf16[144,1076]{1,0:T(8,128)(2,1)}) %reduce-scatter.19.cloned.1.call-update) | async-done | bytes 309904
  1259.0 144.6 %reduce-scatter.21.cloned.1.call-done = bf16[144,1076]{1,0:T(8,128)(2,1)} async-done(((bf16[4608,1076]{1,0:T(8,128)(2,1)}), bf16[144,1076]{1,0:T(8,128)(2,1)}) %reduce-scatter.21.cloned.1.call-update) | async-done | bytes 309904
  (307 shorter events, 254.6 us)
Async XLA Ops:
  7.2 74.8 %copy-start = (s32[4,1024]{1,0:T(4,128)S(1)}, s32[4,1024]{1,0:T(4,128)}, u32[]{:S(2)}) copy-start(s32[4,1024]{1,0:T(4,128)} %param.19) | copy-start | bytes 49156
  7.2 170.2 %all-gather.4.cloned.1.call-start = ((), (), s32[]{:S(2)}) async-start(), calls=%async_computation.6 | async-start | bytes 11280384 | tf_op jit(solution)/shard_map/all_gather | solution.py:276
  10.7 353.2 %all-gather.6.cloned.1.call-start = ((), (), s32[]{:S(2)}) async-start(), calls=%async_computation.7 | async-start | bytes 11280384 | tf_op jit(solution)/shard_map/all_gather | solution.py:282
  11.5 374.3 %all-gather.8.cloned.1.call-start = ((), (), s32[]{:S(2)}) async-start(), calls=%async_computation.8 | async-start | bytes 11280384 | tf_op jit(solution)/shard_map/all_gather | solution.py:283
  12.2 978.0 %reduce-scatter.11.cloned.1.call-start = ((), (), s32[]{:S(2)}) async-start(), calls=%async_computation.9 | async-start | bytes 3649536 | tf_op jit(solution)/shard_map/reduce_scatter | solution.py:324
  13.5 25.7 %collective-permute-start = (bf16[256,1152]{1,0:T(8,128)(2,1)}, bf16[256,1152]{1,0:T(8,128)(2,1)S(1)}, u32[]{:S(2)}, u32[]{:S(2)}) collective-permute-start(bf16[256,1152]{1,0:T(8,128)(2,1)} %get-tuple-element.158), channel_id=1, source_target_pairs={{0,1},{1,2},{2,3},{3,0},{4,5},{5,6},{6,7},{7,4},{8,9},{9,10},{10,1... | collective-permute-start | bytes 1769480 | tf_op jit(solution)/shard_map/ppermute | solution.py:236
  16.5 62.3 %collective-permute-start.1 = (bf16[256,1152]{1,0:T(8,128)(2,1)}, bf16[256,1152]{1,0:T(8,128)(2,1)S(1)}, u32[]{:S(2)}, u32[]{:S(2)}) collective-permute-start(bf16[256,1152]{1,0:T(8,128)(2,1)} %get-tuple-element.159), channel_id=1, source_target_pairs={{0,2},{1,3},{2,0},{3,1},{4,6},{5,7},{6,4},{7,5},{8,10},{9,11},{10,... | collective-permute-start | bytes 1769480 | tf_op jit(solution)/shard_map/ppermute | solution.py:236
  19.1 59.7 %collective-permute-start.2 = (bf16[256,1152]{1,0:T(8,128)(2,1)S(1)}, bf16[256,1152]{1,0:T(8,128)(2,1)S(1)}, u32[]{:S(2)}, u32[]{:S(2)}) collective-permute-start(bf16[256,1152]{1,0:T(8,128)(2,1)S(1)} %get-tuple-element.157), channel_id=1, source_target_pairs={{0,3},{1,0},{2,1},{3,2},{4,7},{5,4},{6,5},{7,6},{8,11},{9,8},{10,9... | collective-permute-start | bytes 1769480 | tf_op jit(solution)/shard_map/ppermute | solution.py:236
  78.8 25.2 %copy-start.33 = (f32[1152]{0:T(1024)S(1)}, f32[1152]{0:T(1024)}, u32[]{:S(2)}) copy-start(f32[1152]{0:T(1024)} %param.26) | copy-start | bytes 13828
  80.4 57.1 %collective-permute-start.3 = (bf16[1024,1152]{1,0:T(8,128)(2,1)}, bf16[1024,1152]{1,0:T(8,128)(2,1)}, u32[]{:S(2)}, u32[]{:S(2)}) collective-permute-start(bf16[1024,1152]{1,0:T(8,128)(2,1)} %pad_maximum_fusion.2), channel_id=1, source_target_pairs={{4,0},{0,4},{5,1},{1,5},{6,2},{2,6},{7,3},{3,7},{12,8},{8,12},{13,... | collective-permute-start | bytes 7077896 | tf_op jit(solution)/shard_map/ppermute | solution.py:260
  82.8 51.1 %collective-permute-start.4 = (s32[1024]{0:T(1024)S(1)}, s32[1024]{0:T(1024)S(1)}, u32[]{:S(2)}, u32[]{:S(2)}) collective-permute-start(s32[1024]{0:T(1024)S(1)} %bitcast.147), channel_id=1, source_target_pairs={{4,0},{0,4},{5,1},{1,5},{6,2},{2,6},{7,3},{3,7},{12,8},{8,12},{13,... | collective-permute-start | bytes 12296 | tf_op jit(solution)/shard_map/ppermute | solution.py:260
  86.2 299.6 %collective-permute-start.10 = (bf16[256,1152]{1,0:T(8,128)(2,1)}, bf16[256,1152]{1,0:T(8,128)(2,1)}, u32[]{:S(2)}, u32[]{:S(2)}) collective-permute-start(bf16[256,1152]{1,0:T(8,128)(2,1)} %get-tuple-element.152), channel_id=1, source_target_pairs={{0,3},{1,0},{2,1},{3,2},{4,7},{5,4},{6,5},{7,6},{8,11},{9,8},{10,9... | collective-permute-start | bytes 1769480 | tf_op jit(solution)/shard_map/ppermute | solution.py:236
  103.4 282.4 %collective-permute-start.9 = (bf16[256,1152]{1,0:T(8,128)(2,1)}, bf16[256,1152]{1,0:T(8,128)(2,1)}, u32[]{:S(2)}, u32[]{:S(2)}) collective-permute-start(bf16[256,1152]{1,0:T(8,128)(2,1)} %get-tuple-element.153), channel_id=1, source_target_pairs={{0,2},{1,3},{2,0},{3,1},{4,6},{5,7},{6,4},{7,5},{8,10},{9,11},{10,... | collective-permute-start | bytes 1769480 | tf_op jit(solution)/shard_map/ppermute | solution.py:236
  103.4 282.4 %collective-permute-start.8 = (bf16[256,1152]{1,0:T(8,128)(2,1)}, bf16[256,1152]{1,0:T(8,128)(2,1)}, u32[]{:S(2)}, u32[]{:S(2)}) collective-permute-start(bf16[256,1152]{1,0:T(8,128)(2,1)} %get-tuple-element.151), channel_id=1, source_target_pairs={{0,1},{1,2},{2,3},{3,0},{4,5},{5,6},{6,7},{7,4},{8,9},{9,10},{10,1... | collective-permute-start | bytes 1769480 | tf_op jit(solution)/shard_map/ppermute | solution.py:236
  244.4 108.5 %copy-start.15 = (bf16[1,4,288,1152]{3,2,1,0:T(8,128)(2,1)S(1)}, bf16[1,4,288,1152]{3,2,1,0:T(8,128)(2,1)}, u32[]{:S(2)}) copy-start(bf16[1,4,288,1152]{3,2,1,0:T(8,128)(2,1)} %copy.91) | copy-start | bytes 7962628
  244.4 108.5 %copy-start.36 = (f32[1152]{0:T(1024)S(1)}, f32[1152]{0:T(1024)}, u32[]{:S(2)}) copy-start(f32[1152]{0:T(1024)} %param.28) | copy-start | bytes 13828
  461.0 118.3 %slice-start.8 = ((s8[4718592]{0:T(1024)(128)(4,1)}), s8[524288]{0:T(1024)(128)(4,1)S(1)}, s32[]{:S(2)}) async-start(s8[4718592]{0:T(1024)(128)(4,1)} %bitcast.128), calls=%async_computation.23 | async-start | bytes 1048576
  465.7 113.6 %slice-start.9 = ((s8[4718592]{0:T(1024)(128)(4,1)}), s8[4194304]{0:T(1024)(128)(4,1)S(1)}, s32[]{:S(2)}) async-start(s8[4718592]{0:T(1024)(128)(4,1)} %bitcast.128), calls=%async_computation.24 | async-start | bytes 8388608
  585.8 406.0 %reduce-scatter.13.cloned.1.call-start = ((), (), s32[]{:S(2)}) async-start(), calls=%async_computation.10 | async-start | bytes 3649536 | tf_op jit(solution)/shard_map/reduce_scatter | solution.py:324
  598.4 403.8 %reduce-scatter.15.cloned.1.call-start = ((), (), s32[]{:S(2)}) async-start(), calls=%async_computation.11 | async-start | bytes 3649536 | tf_op jit(solution)/shard_map/reduce_scatter | solution.py:324
  613.9 495.9 %reduce-scatter.17.cloned.1.call-start = ((), (), s32[]{:S(2)}) async-start(), calls=%async_computation.12 | async-start | bytes 3649536 | tf_op jit(solution)/shard_map/reduce_scatter | solution.py:324
  631.1 625.7 %reduce-scatter.19.cloned.1.call-start = ((), (), s32[]{:S(2)}) async-start(), calls=%async_computation.13 | async-start | bytes 10948608
  662.7 741.0 %reduce-scatter.21.cloned.1.call-start = ((), (), s32[]{:S(2)}) async-start(), calls=%async_computation.14 | async-start | bytes 10948608
  734.3 80.3 %collective-permute-start.11 = (bf16[1024,1152]{1,0:T(8,128)(2,1)}, bf16[1024,1152]{1,0:T(8,128)(2,1)}, u32[]{:S(2)}, u32[]{:S(2)}) collective-permute-start(bf16[1024,1152]{1,0:T(8,128)(2,1)} %slice.235), channel_id=1, source_target_pairs={{0,4},{4,0},{1,5},{5,1},{2,6},{6,2},{3,7},{7,3},{8,12},{12,8},{9,1... | collective-permute-start | bytes 7077896 | tf_op jit(solution)/shard_map/ppermute | solution.py:269
  774.4 12.4 collective-permute-start.5
  776.3 38.3 %copy-start.31 = (f32[1152]{0:T(1024)S(1)}, f32[1152]{0:T(1024)}, u32[]{:S(2)}) copy-start(f32[1152]{0:T(1024)} %param.20) | copy-start | bytes 13828
  776.3 36.3 %collective-permute-start.6 = (bf16[256,1152]{1,0:T(8,128)(2,1)S(1)}, bf16[256,1152]{1,0:T(8,128)(2,1)}, u32[]{:S(2)}, u32[]{:S(2)}) collective-permute-start(bf16[256,1152]{1,0:T(8,128)(2,1)S(1)} %get-tuple-element.155), channel_id=1, source_target_pairs={{2,0},{3,1},{0,2},{1,3},{6,4},{7,5},{4,6},{5,7},{10,8},{11,9},{8,1... | collective-permute-start | bytes 1769480 | tf_op jit(solution)/shard_map/ppermute | solution.py:246
  778.6 51.6 %collective-permute-start.7 = (bf16[256,1152]{1,0:T(8,128)(2,1)S(1)}, bf16[256,1152]{1,0:T(8,128)(2,1)}, u32[]{:S(2)}, u32[]{:S(2)}) collective-permute-start(bf16[256,1152]{1,0:T(8,128)(2,1)S(1)} %get-tuple-element.154), channel_id=1, source_target_pairs={{3,0},{0,1},{1,2},{2,3},{7,4},{4,5},{5,6},{6,7},{11,8},{8,9},{9,10... | collective-permute-start | bytes 1769480 | tf_op jit(solution)/shard_map/ppermute | solution.py:246
  830.1 155.1 %collective-permute-start.12 = (bf16[256,1152]{1,0:T(8,128)(2,1)}, bf16[256,1152]{1,0:T(8,128)(2,1)}, u32[]{:S(2)}, u32[]{:S(2)}) collective-permute-start(bf16[256,1152]{1,0:T(8,128)(2,1)} %get-tuple-element.149), channel_id=1, source_target_pairs={{1,0},{2,1},{3,2},{0,3},{5,4},{6,5},{7,6},{4,7},{9,8},{10,9},{11,1... | collective-permute-start | bytes 1769480 | tf_op jit(solution)/shard_map/ppermute | solution.py:246
  832.1 154.4 %collective-permute-start.13 = (bf16[256,1152]{1,0:T(8,128)(2,1)}, bf16[256,1152]{1,0:T(8,128)(2,1)S(1)}, u32[]{:S(2)}, u32[]{:S(2)}) collective-permute-start(bf16[256,1152]{1,0:T(8,128)(2,1)} %get-tuple-element.148), channel_id=1, source_target_pairs={{2,0},{3,1},{0,2},{1,3},{6,4},{7,5},{4,6},{5,7},{10,8},{11,9},{8,1... | collective-permute-start | bytes 1769480 | tf_op jit(solution)/shard_map/ppermute | solution.py:246
  834.4 152.2 %collective-permute-start.14 = (bf16[256,1152]{1,0:T(8,128)(2,1)S(1)}, bf16[256,1152]{1,0:T(8,128)(2,1)}, u32[]{:S(2)}, u32[]{:S(2)}) collective-permute-start(bf16[256,1152]{1,0:T(8,128)(2,1)S(1)} %get-tuple-element.147), channel_id=1, source_target_pairs={{3,0},{0,1},{1,2},{2,3},{7,4},{4,5},{5,6},{6,7},{11,8},{8,9},{9,10... | collective-permute-start | bytes 1769480 | tf_op jit(solution)/shard_map/ppermute | solution.py:246
  987.7 418.4 %copy-start.1 = (s32[4,1024]{1,0:T(4,128)S(1)}, s32[4,1024]{1,0:T(4,128)}, u32[]{:S(2)}) copy-start(s32[4,1024]{1,0:T(4,128)} %param.19) | copy-start | bytes 49156
  (63 other events, 547.9 us)
Sparse Core Ops, SparseCore 0:
  10.9 166.4 all-gather.3
  179.7 88.5 all-gather.5
  270.6 87.2 all-gather.7
  585.9 153.7 reduce-scatter.10
  744.9 149.0 reduce-scatter.12
  899.3 102.8 reduce-scatter.14
  1007.6 102.1 reduce-scatter.16
  1115.9 140.8 reduce-scatter.18
  1262.8 140.7 reduce-scatter.20

commit v2 on v1

v2 whole, which is shorter than its diff:
```python
import functools

import jax
import jax.numpy as jnp
from jax import lax
from jax.experimental import pallas as pl
from jax.experimental.pallas import tpu as pltpu
from jax.sharding import PartitionSpec as P

HD = 72
PICS = 4
EPSILON = 1e-06
LOG2E = 1.4426950408889634
NEG = -1e30
F32 = jnp.float32
BF16 = jnp.bfloat16
MESH = pl.DeviceIdType.MESH


def dot(left, right, left_dim, right_dim):
    return lax.dot_general(
        left, right, (((left_dim,), (right_dim,)), ((), ())), preferred_element_type=F32
    )


def load_augmented(h, q_ref, k_ref, qm_ref, km_ref, kt, qa):
    rows = slice(h * HD, (h + 1) * HD)
    kt[h] = jnp.concatenate([k_ref[rows, :].astype(F32), km_ref[...]], axis=0).T.astype(BF16)
    qa[h] = jnp.concatenate([q_ref[rows, :].astype(F32), qm_ref[...]], axis=0).astype(BF16)


def forward_kernel(nq, nk, block, heads, count, index, q_ref, k_ref, v_ref, qm_ref, km_ref, o_ref, lse_ref, kt, qa):
    for h in range(heads):
        load_augmented(h, q_ref, k_ref, qm_ref, km_ref, kt, qa)
    for qb in range(nq):
        cols = pl.ds(qb * block, block)
        q = [qa[h, :, cols] for h in range(heads)]

        def body(n, carry):
            off = pl.multiple_of(index[qb * nk + n] * block, block)
            scores = [dot(kt[h, pl.ds(off, block), :], q[h], 1, 0) for h in range(heads)]
            out = []
            for h in range(heads):
                top, total, acc = carry[h]
                new = jnp.maximum(top, jnp.max(scores[h], axis=0, keepdims=True))
                p = jnp.exp2(scores[h] - new)
                alpha = jnp.exp2(top - new)
                total = total * alpha + jnp.sum(p, axis=0, keepdims=True)
                acc = acc * alpha + dot(v_ref[h * HD : (h + 1) * HD, pl.ds(off, block)], p.astype(BF16), 1, 0)
                out.append((new, total, acc))
            return tuple(out)

        start = (jnp.full((1, block), 4 * NEG, F32), jnp.zeros((1, block), F32), jnp.zeros((HD, block), F32))
        done = lax.fori_loop(0, count[qb], body, (start,) * heads)
        for h in range(heads):
            top, total, acc = done[h]
            o_ref[h * HD : (h + 1) * HD, cols] = (acc / total).astype(BF16)
            lse_ref[h, :, cols] = top + jnp.log2(total)


def backward_kernel(
    nq, nk, block, heads, count, index, q_ref, k_ref, v_ref, do_ref, o_ref, lse_ref, qm_ref, km_ref,
    dq_ref, dk_ref, dv_ref, kt, vt, qa, dk_acc, dv_acc
):
    for h in range(heads):
        load_augmented(h, q_ref, k_ref, qm_ref, km_ref, kt, qa)
        vt[h] = v_ref[h * HD : (h + 1) * HD, :].astype(F32).T.astype(BF16)
    dk_acc[...] = jnp.zeros_like(dk_acc)
    dv_acc[...] = jnp.zeros_like(dv_acc)
    for qb in range(nq):
        cols = pl.ds(qb * block, block)
        lines = [slice(h * HD, (h + 1) * HD) for h in range(heads)]
        q = [qa[h, :, cols] for h in range(heads)]
        do = [do_ref[lines[h], cols] for h in range(heads)]
        lse = [lse_ref[h, :, cols] for h in range(heads)]
        delta = [
            jnp.sum(do[h].astype(F32) * o_ref[lines[h], cols].astype(F32), axis=0, keepdims=True)
            for h in range(heads)
        ]

        def body(n, carry):
            rows = pl.ds(pl.multiple_of(index[qb * nk + n] * block, block), block)
            scores = [dot(kt[h, rows, :], q[h], 1, 0) for h in range(heads)]
            d_probs = [dot(vt[h, rows, :], do[h], 1, 0) for h in range(heads)]
            out = []
            for h in range(heads):
                p = jnp.exp2(scores[h] - lse[h])
                ds = (p * (d_probs[h] - delta[h])).astype(BF16)
                dv_acc[h, :, rows] += dot(do[h], p.astype(BF16), 1, 1)
                dk_acc[h, :, rows] += dot(q[h][:HD], ds, 1, 1)
                out.append(carry[h] + dot(k_ref[lines[h], rows], ds, 1, 0))
            return tuple(out)

        dq = lax.fori_loop(0, count[qb], body, (jnp.zeros((HD, block), F32),) * heads)
        for h in range(heads):
            dq_ref[lines[h], cols] = (dq[h] * HD ** (-0.5)).astype(BF16)
    for h in range(heads):
        dk_ref[h * HD : (h + 1) * HD, :] = (dk_acc[h] * (1.0 / LOG2E)).astype(BF16)
        dv_ref[h * HD : (h + 1) * HD, :] = dv_acc[h].astype(BF16)


def attention_specs(tokens, context, total, heads):
    q_spec = pl.BlockSpec((HD * heads, tokens), lambda h, *_: (h, 0))
    k_spec = pl.BlockSpec((HD * heads, context), lambda h, *_: (h, 0))
    v_spec = pl.BlockSpec((HD * heads, context), lambda h, *_: (total // heads + h, 0))
    lse_spec = pl.BlockSpec((heads, 1, tokens), lambda h, *_: (h, 0, 0))
    masks = [pl.BlockSpec((8, tokens), lambda h, *_: (0, 0)), pl.BlockSpec((8, context), lambda h, *_: (0, 0))]
    return q_spec, k_spec, v_spec, lse_spec, masks


def attention_forward(count, index, qt, kvt, qm, km, block, heads=8):
    width, tokens = qt.shape
    context, total = kvt.shape[1], width // HD
    q_spec, k_spec, v_spec, lse_spec, masks = attention_specs(tokens, context, total, heads)
    return pl.pallas_call(
        functools.partial(forward_kernel, tokens // block, context // block, block, heads),
        out_shape=(
            jax.ShapeDtypeStruct((width, tokens), BF16),
            jax.ShapeDtypeStruct((total, 1, tokens), F32),
        ),
        grid_spec=pltpu.PrefetchScalarGridSpec(
            num_scalar_prefetch=2,
            grid=(total // heads,),
            in_specs=[q_spec, k_spec, v_spec] + masks,
            out_specs=(q_spec, lse_spec),
            scratch_shapes=[pltpu.VMEM((heads, context, HD + 8), BF16), pltpu.VMEM((heads, HD + 8, tokens), BF16)],
        ),
        compiler_params=pltpu.CompilerParams(vmem_limit_bytes=56 << 20),
        cost_estimate=pl.CostEstimate(
            flops=tokens * context * width * 12, bytes_accessed=width * (tokens + context) * 4,
            transcendentals=tokens * context * total // 2,
        ),
        name="attention_forward",
    )(count, index, qt, kvt, kvt, qm, km)


def attention_backward(count, index, qt, kvt, d_ot, ot, lse, qm, km, block, heads=8):
    width, tokens = qt.shape
    context, total = kvt.shape[1], width // HD
    q_spec, k_spec, v_spec, lse_spec, masks = attention_specs(tokens, context, total, heads)
    return pl.pallas_call(
        functools.partial(backward_kernel, tokens // block, context // block, block, heads),
        out_shape=(
            jax.ShapeDtypeStruct((width, tokens), BF16),
            jax.ShapeDtypeStruct((width, context), BF16),
            jax.ShapeDtypeStruct((width, context), BF16),
        ),
        grid_spec=pltpu.PrefetchScalarGridSpec(
            num_scalar_prefetch=2,
            grid=(total // heads,),
            in_specs=[q_spec, k_spec, v_spec, q_spec, q_spec, lse_spec] + masks,
            out_specs=(q_spec, k_spec, k_spec),
            scratch_shapes=[
                pltpu.VMEM((heads, context, HD + 8), BF16),
                pltpu.VMEM((heads, context, HD), BF16),
                pltpu.VMEM((heads, HD + 8, tokens), BF16),
                pltpu.VMEM((heads, HD, context), F32),
                pltpu.VMEM((heads, HD, context), F32),
            ],
        ),
        compiler_params=pltpu.CompilerParams(vmem_limit_bytes=56 << 20),
        cost_estimate=pl.CostEstimate(
            flops=tokens * context * width * 20, bytes_accessed=width * (tokens + context) * 8,
            transcendentals=tokens * context * total // 2,
        ),
        name="attention_backward",
    )(count, index, qt, kvt, kvt, d_ot, ot, lse, qm, km)


def active_blocks(qid, kid, bq, bk):
    q = qid.reshape(-1, bq)
    k = kid.reshape(-1, bk)
    q_low, q_high = jnp.min(q, 1)[:, None], jnp.max(q, 1)[:, None]
    k_low, k_high = jnp.min(k, 1)[None, :], jnp.max(k, 1)[None, :]
    active = (q_low <= k_high) & (k_low <= q_high)
    slots = jnp.arange(k.shape[0], dtype=jnp.int32)
    before = (slots[:, None] < slots[None, :])[None]
    place = jnp.sum((active[:, :, None] & before).astype(jnp.int32), axis=1)
    hit = active[:, None, :] & (place[:, None, :] == slots[None, :, None])
    index = jnp.sum(jnp.where(hit, slots[None, None, :], 0), axis=2)
    return jnp.sum(active.astype(jnp.int32), axis=1), index.reshape(-1)


def norm_stats(values):
    centred = values - jnp.mean(values, axis=-1, keepdims=True)
    inverse = lax.rsqrt(jnp.mean(centred * centred, axis=-1, keepdims=True) + EPSILON)
    return centred * inverse, inverse


def norm_back(grad, scaled, inverse, gain):
    wide = grad * gain
    return inverse * (
        wide
        - jnp.mean(wide, axis=-1, keepdims=True)
        - scaled * jnp.mean(wide * scaled, axis=-1, keepdims=True)
    )


def gelu_pair(pre):
    c = 0.7978845608028654
    square = pre * pre
    t = jnp.tanh(c * pre * (1.0 + 0.044715 * square))
    value = 0.5 * pre * (1.0 + t)
    slope = 0.5 * (1.0 + t) + 0.5 * pre * (1.0 - t * t) * c * (1.0 + 3 * 0.044715 * square)
    return value, slope


def bits_of(size):
    assert size & (size - 1) == 0
    return size.bit_length() - 1


def exchange(value, axis, size, flip):
    return lax.ppermute(value, axis, [(i, i ^ flip) for i in range(size)])


def butterfly(value, sizes):
    for axis, size in sizes.items():
        for bit in range(bits_of(size)):
            value = value + exchange(value, axis, size, 1 << bit)
    return value


def halve(grad, sizes, ctx_first):
    fsdp, ctx = sizes["fsdp"], sizes["ctx"]
    nf, nc = bits_of(fsdp), bits_of(ctx)
    total = grad.reshape((2,) * (nf + nc) + (-1, grad.shape[-1])).astype(F32)
    f_stages = [("fsdp", fsdp, bit) for bit in range(nf)]
    c_stages = [("ctx", ctx, bit) for bit in range(nc)]
    stages = f_stages[:1] + (c_stages + f_stages[1:] if ctx_first else f_stages[1:] + c_stages)
    left = [("fsdp", bit) for bit in reversed(range(nf))] + [("ctx", bit) for bit in reversed(range(nc))]
    for axis, size, bit in stages:
        dim = left.index((axis, bit))
        mine = (lax.axis_index(axis) >> bit) & 1
        send = lax.dynamic_index_in_dim(total, 1 - mine, dim, keepdims=False).astype(BF16)
        keep = lax.dynamic_index_in_dim(total, mine, dim, keepdims=False)
        total = keep + exchange(send, axis, size, 1 << bit).astype(F32)
        left.pop(dim)
    return total


def scatter_units(parts, tp):
    place = lax.axis_index("tp")
    stack = jnp.stack([p.astype(BF16) for p in parts])
    total = lax.dynamic_index_in_dim(jnp.stack(parts), place, 0, keepdims=False)
    for k in range(1, tp):
        piece = lax.dynamic_index_in_dim(stack, place ^ k, 0, keepdims=False)
        total = total + exchange(piece, "tp", tp, k).astype(F32)
    return total


def closing_kernel(kinds, moved, tp, refs):
    jobs = len(kinds)
    grads, (vec, gt) = refs[:jobs], refs[jobs : jobs + 2]
    rest = list(refs[jobs + 2 :])

    def take(n):
        out = rest[:n]
        del rest[:n]
        return out

    units = sorted({slot for part, slot in kinds if part is not None})
    heads = sorted({slot for part, slot in kinds if part is None})
    out_units, out_heads = take(len(units)), take(len(heads))
    vec_out, gt_out = take(2)
    arrived = take(jobs)
    widths = [g.shape[-1] for g in grads]
    pools = {w: take(2) for w in sorted(set(widths))}
    slots = [widths[:j].count(widths[j]) % 2 for j in range(jobs)]
    own = [pools[widths[j]][0].at[slots[j]] for j in range(jobs)]
    come = [pools[widths[j]][1].at[slots[j]] for j in range(jobs)]
    keep, send2, recv2, send3, recv3 = (take(jobs) for _ in range(5))
    last_units, last_heads, piece_heads = take(len(units)), take(len(heads)), take(len(heads))
    (vec_in,) = take(1)
    s1, r1, s2, r2, s3, r3, l1, l2 = take(8)
    s4, r4, sv, rv, sg, rg, lg = take(7)

    f, c, z = lax.axis_index("fsdp"), lax.axis_index("ctx"), lax.axis_index("tp")
    x, core = f // 2, f % 2
    near, across = f + 1 - 2 * core, f + 2 - 4 * x
    other_c = 1 - c

    barrier = pltpu.get_barrier_semaphore()
    for where in ({"fsdp": near}, {"fsdp": across}, {"ctx": other_c}):
        pl.semaphore_signal(barrier, inc=1, device_id=where, device_id_type=MESH)
    for k in range(1, tp):
        pl.semaphore_signal(barrier, inc=1, device_id={"tp": lax.rem(z + k, tp)}, device_id_type=MESH)
    pl.semaphore_wait(barrier, 2 + tp)

    def remote(src, dst, send, recv, where):
        return pltpu.make_async_remote_copy(
            src_ref=src, dst_ref=dst, send_sem=send, recv_sem=recv, device_id=where, device_id_type=MESH
        )

    for k in range(tp if moved else 0):
        @pl.when(z != k)
        def _():
            remote(gt.at[k], gt_out.at[z], sg.at[k], rg.at[z], {"tp": k}).start()

        @pl.when(z == k)
        def _():
            pltpu.make_async_copy(gt.at[k], gt_out.at[z], lg).start()

    first = [remote(grads[j].at[:, 1 - core], arrived[j], s1.at[j], r1.at[j], {"fsdp": near}) for j in range(jobs)]
    mine = [pltpu.make_async_copy(grads[j].at[:, core], own[j], l1.at[j]) for j in range(jobs)]
    theirs = [pltpu.make_async_copy(arrived[j], come[j], l2.at[j]) for j in range(jobs)]
    for copy in first:
        copy.start()

    def turn(j):
        return j % 2 == 0

    second, third = [], []
    for j in range(jobs):
        where2 = {"fsdp": across} if turn(j) else {"ctx": other_c}
        where3 = {"ctx": other_c} if turn(j) else {"fsdp": across}
        second.append(remote(send2[j], recv2[j], s2.at[j], r2.at[j], where2))
        third.append(remote(send3[j], recv3[j], s3.at[j], r3.at[j], where3))

    def rows_loop(rows, body):
        tile = 48

        @pl.loop(0, rows // tile)
        def _(i):
            body(pl.ds(pl.multiple_of(i * tile, 16), tile))

    def stage1(j):
        mine[j].wait()
        theirs[j].wait()
        rows = send3[j].shape[0]
        for i in range(2):

            def body(r, i=i):
                if turn(j):
                    out_at, in_at = (1 - x, i), (x, i)
                else:
                    out_at, in_at = (i, 1 - c), (i, c)
                send2[j][i, r] = (own[j][out_at[0], out_at[1], r].astype(F32) + come[j][out_at[0], out_at[1], r].astype(F32)).astype(BF16)
                keep[j][i, r] = (own[j][in_at[0], in_at[1], r].astype(F32) + come[j][in_at[0], in_at[1], r].astype(F32)).astype(BF16)

            rows_loop(rows, body)
        second[j].start()

    def stage2(j):
        second[j].wait()
        at = c if turn(j) else x

        def body(r):
            send3[j][r] = (keep[j][1 - at, r].astype(F32) + recv2[j][1 - at, r].astype(F32)).astype(BF16)
            keep[j][at, r] = (keep[j][at, r].astype(F32) + recv2[j][at, r].astype(F32)).astype(BF16)

        rows_loop(send3[j].shape[0], body)
        third[j].start()

    def stage3(j):
        third[j].wait()
        at = c if turn(j) else x
        part, slot = kinds[j]
        if part is None:
            width = piece_heads[slot].shape[-1]

            def body(r):
                total = keep[j][at, r].astype(F32) + recv3[j][r].astype(F32)
                for t in range(tp):
                    piece_heads[slot][t, r] = total[:, t * width : (t + 1) * width].astype(BF16)

            rows_loop(send3[j].shape[0], body)
            for t in range(tp):
                @pl.when(z != t)
                def _():
                    remote(piece_heads[slot].at[t], last_heads[slot].at[z], s4.at[j, t], r4.at[len(units) + slot, z], {"tp": t}).start()
        else:

            def body(r):
                send3[j][r] = (keep[j][at, r].astype(F32) + recv3[j][r].astype(F32)).astype(BF16)

            rows_loop(send3[j].shape[0], body)

            @pl.when(z != part)
            def _():
                remote(send3[j], last_units[slot].at[z], s4.at[j, part], r4.at[slot, z], {"tp": part}).start()

    flips = [{"fsdp": near}, {"fsdp": across}, {"ctx": other_c}]
    bit = 1
    while bit < tp:
        flips.append({"tp": z + bit - 2 * bit * lax.rem(lax.div(z, bit), 2)})
        bit *= 2
    swaps = [remote(vec_out, vec_in.at[i], sv.at[i], rv.at[i], where) for i, where in enumerate(flips)]
    vec_out[...] = vec[...]
    swaps[0].start()

    def small(i):
        swaps[i].wait()
        vec_out[...] = vec_out[...] + vec_in[i]
        if i + 1 < len(swaps):
            swaps[i + 1].start()

    mine[0].start()
    first[0].wait()
    theirs[0].start()
    lag = 2
    for step in range(jobs + 2 * lag):
        if step + 1 < jobs:
            mine[step + 1].start()
            first[step + 1].wait()
            theirs[step + 1].start()
        if step < jobs:
            stage1(step)
        if 0 <= step - lag < jobs:
            stage2(step - lag)
        if 0 <= step - 2 * lag < jobs:
            stage3(step - 2 * lag)
        if step % 2 == 0 and step // 2 < len(swaps):
            small(step // 2)
    for i in range((jobs + 2 * lag + 1) // 2, len(swaps)):
        small(i)

    for j, (part, slot) in enumerate(kinds):
        for t in range(tp):
            if part is None:
                @pl.when(z != t)
                def _():
                    remote(piece_heads[slot].at[t], last_heads[slot].at[z], s4.at[j, t], r4.at[len(units) + slot, z], {"tp": t}).wait_send()
                    remote(piece_heads[slot].at[t], last_heads[slot].at[t], s4.at[j, t], r4.at[len(units) + slot, t], {"tp": t}).wait_recv()
            elif t == part:
                @pl.when(z != t)
                def _():
                    remote(send3[j], last_units[slot].at[z], s4.at[j, t], r4.at[slot, z], {"tp": t}).wait_send()

                @pl.when(z == t)
                def _():
                    for other in range(tp):
                        if other != t:
                            remote(send3[j], last_units[slot].at[other], s4.at[j, t], r4.at[slot, other], {"tp": t}).wait_recv()
                    last_units[slot][t] = send3[j][...]
    for slot in heads:
        last_heads[slot][z] = piece_heads[slot][z]
    for slots, last, out in ((units, last_units, out_units), (heads, last_heads, out_heads)):
        for slot in slots:

            def body(r, last=last, out=out, slot=slot):
                total = last[slot][0, r].astype(F32)
                for t in range(1, tp):
                    total = total + last[slot][t, r].astype(F32)
                out[slot][r] = total

            rows_loop(out[slot].shape[0], body)
    for k in range(tp if moved else 0):
        @pl.when(z != k)
        def _():
            remote(gt.at[k], gt_out.at[z], sg.at[k], rg.at[z], {"tp": k}).wait_send()
            remote(gt.at[k], gt_out.at[k], sg.at[k], rg.at[k], {"tp": k}).wait_recv()

        @pl.when(z == k)
        def _():
            pltpu.make_async_copy(gt.at[k], gt_out.at[z], lg).wait()


def closing(unit_grads, head_grads, vector, token_grads, tp):
    kinds, operands = [], []
    for t in range(tp if unit_grads else 0):
        for slot, parts in enumerate(unit_grads):
            kinds.append((t, slot))
            operands.append(parts[t])
    for slot, grad in enumerate(head_grads):
        kinds.append((None, slot))
        operands.append(grad)
    operands = [g.reshape((2, 2, 2, g.shape[0] // 8, g.shape[1])) for g in operands]
    rows = operands[0].shape[3]
    jobs = len(kinds)
    vmem, hbm = pl.BlockSpec(memory_space=pltpu.VMEM), pl.BlockSpec(memory_space=pl.ANY)
    heads_w = head_grads[0].shape[1] // tp
    units_w = unit_grads[0][0].shape[1] if unit_grads else 0
    out_shape = (
        [jax.ShapeDtypeStruct((rows, units_w), F32)] * len(unit_grads)
        + [jax.ShapeDtypeStruct((rows, heads_w), F32)] * len(head_grads)
        + [jax.ShapeDtypeStruct(vector.shape, F32), jax.ShapeDtypeStruct(token_grads.shape, token_grads.dtype)]
        + [jax.ShapeDtypeStruct((2, 2, rows, g.shape[-1]), BF16) for g in operands]
    )
    out_specs = [vmem] * (len(unit_grads) + len(head_grads) + 1) + [hbm] * (1 + jobs)
    widths = [g.shape[-1] for g in operands]
    scratch = [pltpu.VMEM((2, 2, 2, rows, w), BF16) for w in sorted(set(widths)) for _ in range(2)]
    scratch += [pltpu.VMEM((2, rows, w), BF16) for w in widths] * 3
    scratch += [pltpu.VMEM((rows, w), BF16) for w in widths] * 2
    scratch += [pltpu.VMEM((tp, rows, units_w), BF16)] * len(unit_grads)
    scratch += [pltpu.VMEM((tp, rows, heads_w), BF16)] * (2 * len(head_grads))
    swaps = 3 + bits_of(tp)
    scratch += [pltpu.VMEM((swaps,) + vector.shape, F32)]
    scratch += [pltpu.SemaphoreType.DMA((jobs,))] * 8
    scratch += [pltpu.SemaphoreType.DMA((jobs, tp)), pltpu.SemaphoreType.DMA((len(unit_grads) + len(head_grads), tp))]
    scratch += [pltpu.SemaphoreType.DMA((swaps,))] * 2 + [pltpu.SemaphoreType.DMA((tp,))] * 2 + [pltpu.SemaphoreType.DMA]
    outs = pl.pallas_call(
        lambda *refs: closing_kernel(kinds, True, tp, refs),
        out_shape=out_shape,
        in_specs=[hbm] * jobs + [vmem, hbm],
        out_specs=out_specs,
        scratch_shapes=scratch,
        compiler_params=pltpu.CompilerParams(collective_id=1, has_side_effects=True, vmem_limit_bytes=62 << 20),
        name="closing",
    )(*operands, vector, token_grads)
    n_u, n_h = len(unit_grads), len(head_grads)
    return outs[:n_u], outs[n_u : n_u + n_h], outs[n_u + n_h], outs[n_u + n_h + 1]


def shards(
    sizes,
    tokens,
    picture,
    ln1_gain,
    ln1_bias,
    w_query,
    b_query,
    w_key,
    w_value,
    b_value,
    w_output,
    b_output,
    ln2_gain,
    ln2_bias,
    w_first,
    b_first,
    w_second,
    b_second,
    cotangent,
):
    tp, ctx = sizes["tp"], sizes["ctx"]
    rows, span, width = tokens.shape
    group = tp // rows
    place = lax.axis_index("tp")
    mine = place % rows
    row = place // group
    part = place % group

    def out_permutation(k):
        return [(s * rows + j, ((j + k) % rows) * group + s) for s in range(group) for j in range(rows)]

    def gather_row(blocks):
        got = []
        for k in range(rows):
            piece = lax.dynamic_index_in_dim(blocks, (mine + k) % rows, 0, keepdims=False)
            pairs = out_permutation(k)
            if any(a != b for a, b in pairs):
                piece = lax.ppermute(piece, "tp", pairs)
            got.append(piece)
        return got

    def scatter_row(values):
        out = jnp.zeros((rows, span) + values.shape[1:], values.dtype)
        for k in range(rows):
            piece = values[k * span : (k + 1) * span]
            pairs = [(b, a) for a, b in out_permutation(k)]
            if any(a != b for a, b in pairs):
                piece = lax.ppermute(piece, "tp", pairs)
            out = lax.dynamic_update_index_in_dim(out, piece, (mine + k) % rows, 0)
        return out

    def peers(step):
        s_step, c_step = step % group, step // group
        return s_step, c_step

    def fetch(value, step):
        s_step, c_step = peers(step)
        if s_step:
            pairs = [(r * group + (s + s_step) % group, r * group + s) for r in range(rows) for s in range(group)]
            value = lax.ppermute(value, "tp", pairs)
        if c_step:
            value = lax.ppermute(value, "ctx", [((c + c_step) % ctx, c) for c in range(ctx)])
        return value

    def give(value, step):
        s_step, c_step = peers(step)
        if s_step:
            pairs = [(r * group + s, r * group + (s + s_step) % group) for r in range(rows) for s in range(group)]
            value = lax.ppermute(value, "tp", pairs)
        if c_step:
            value = lax.ppermute(value, "ctx", [(c, (c + c_step) % ctx) for c in range(ctx)])
        return value

    steps = group * ctx

    heads_dev = w_query.shape[1]
    both = ("tp", "fsdp")
    qkvo = lax.all_gather(
        jnp.concatenate([w_query, w_key, w_value, w_output.T], axis=1), both, axis=0, tiled=True
    ).reshape(tp, width, 4, heads_dev)
    qkvo = qkvo.transpose(2, 0, 3, 1).reshape(4, tp * heads_dev, width)
    wq, wkv, wo = qkvo[0], qkvo[1:3].reshape(2 * tp * heads_dev, width), qkvo[3]
    units = w_first.shape[1]
    first = lax.all_gather(w_first, both, axis=0, tiled=True).reshape(tp, width, units)
    second = lax.all_gather(w_second.T, both, axis=0, tiled=True).reshape(tp, width, units)

    x16 = jnp.concatenate(gather_row(tokens), axis=0)
    count = rows * span
    ids = lax.dynamic_index_in_dim(picture, row, 0, keepdims=False).reshape(tp, span)
    order = part * rows + (row - jnp.arange(rows)) % rows
    ids = jnp.take(ids, order, axis=0).reshape(count)
    cot = jnp.concatenate(gather_row(cotangent), axis=0)
    x_all16 = jnp.concatenate([x16] + [fetch(x16, i) for i in range(1, steps)], axis=0)
    kid = jnp.concatenate([ids] + [fetch(ids, i) for i in range(1, steps)], axis=0)
    block = 256 if count % 256 == 0 else count
    blocks, index = active_blocks(ids, kid, block, block)
    numbers = jnp.arange(8)[:, None]
    qm = jnp.where((numbers < PICS) & (ids[None, :] != numbers), NEG, 0.0).astype(F32)
    km = (kid[None, :] == numbers).astype(F32)

    x_all = x_all16.astype(F32)
    scaled_all, inverse_all = norm_stats(x_all)
    n1 = (scaled_all * ln1_gain + ln1_bias).astype(BF16)
    qt = ((dot(wq, n1[:count], 1, 1) + b_query[:, None]) * (HD ** (-0.5) * LOG2E)).astype(BF16)
    kv_bias = jnp.concatenate([jnp.zeros_like(b_value), b_value])
    kvt = (dot(wkv, n1, 1, 1) + kv_bias[:, None]).astype(BF16)
    ot, lse = attention_forward(blocks, index, qt, kvt, qm, km, block)
    h = x_all[:count] + (dot(ot, wo, 0, 0) + b_output)

    scaled2, inverse2 = norm_stats(h)
    n2 = (scaled2 * ln2_gain + ln2_bias).astype(BF16)
    y = h + b_second
    d_n2 = jnp.zeros_like(h)
    g_first, g_second, g_first_bias = [], [], []
    for t in range(tp):
        pre = dot(n2, first[t], 1, 0) + b_first[t * units : (t + 1) * units]
        value, slope = gelu_pair(pre)
        act = value.astype(BF16)
        y = y + dot(act, second[t], 1, 1)
        d_pre = (dot(cot, second[t], 1, 0) * slope).astype(BF16)
        d_n2 = d_n2 + dot(d_pre, first[t], 1, 1)
        g_second.append(dot(cot, act, 0, 0).astype(BF16))
        g_first.append(dot(n2, d_pre, 0, 0).astype(BF16))
        g_first_bias.append(jnp.sum(d_pre.astype(F32), axis=0))
    output = scatter_row(y.astype(BF16))
    cot32 = cot.astype(F32)
    g_g2 = jnp.sum(d_n2 * scaled2, axis=0)
    g_c2 = jnp.sum(d_n2, axis=0)
    d_h = cot32 + norm_back(d_n2, scaled2, inverse2, ln2_gain)
    g_bs = jnp.sum(cot32, axis=0)

    d_att = d_h.astype(BF16)
    g_bo = jnp.sum(d_att.astype(F32), axis=0)
    d_ot = dot(wo, d_att, 1, 1).astype(BF16)
    dqt, dkt, dvt = attention_backward(blocks, index, qt, kvt, d_ot, ot, lse, qm, km, block)
    d_all = dot(dkt, wkv[: tp * heads_dev], 0, 0) + dot(dvt, wkv[tp * heads_dev :], 0, 0)
    d_n1 = d_all[:count] + dot(dqt, wq, 0, 0)
    for i in range(1, steps):
        d_n1 = d_n1 + give(d_all[i * count : (i + 1) * count].astype(BF16), i).astype(F32)
    g_query = dot(n1[:count], dqt, 0, 1)
    g_key = dot(n1, dkt, 0, 1)
    g_value = dot(n1, dvt, 0, 1)
    g_out = dot(d_att, ot, 0, 1)
    g_bq = jnp.sum(dqt.astype(F32), axis=1)
    g_bv = jnp.sum(dvt.astype(F32), axis=1)

    scaled1, inverse1 = scaled_all[:count], inverse_all[:count]
    g_g1 = jnp.sum(d_n1 * scaled1, axis=0)
    g_c1 = jnp.sum(d_n1, axis=0)
    grad_tokens = (d_h + norm_back(d_n1, scaled1, inverse1, ln1_gain)).astype(BF16)
    small = [g_g1, g_c1, g_bq, g_bv, g_bo, g_g2, g_c2, jnp.concatenate(g_first_bias), g_bs]
    vector = jnp.concatenate(small)
    vector = jnp.pad(vector, (0, -vector.shape[0] % 1024)).reshape(-1, 128)
    head_grads = [g.astype(BF16) for g in (g_query, g_key, g_value, g_out)]
    if sizes["fsdp"] == 4 and ctx == 2 and group == 1 and bits_of(tp):
        natural = jnp.zeros((rows, span, width), BF16)
        for k in range(rows):
            piece = grad_tokens[k * span : (k + 1) * span]
            natural = lax.dynamic_update_index_in_dim(natural, piece, (place - k) % rows, 0)
        (g_first, g_second), heads_out, vector, grad_tokens = closing(
            [g_first, g_second], head_grads, vector, natural, tp
        )
        g_query, g_key, g_value, g_out = heads_out
    else:
        g_first, g_second = (
            scatter_units([halve(g, sizes, i % 2 == 0) for g in parts], tp)
            for i, parts in enumerate((g_first, g_second))
        )
        halved = [halve(g, sizes, i % 2 == 0) for i, g in enumerate(head_grads)]
        g_query, g_key, g_value, g_out = (
            scatter_units([g[:, t * heads_dev : (t + 1) * heads_dev] for t in range(tp)], tp) for g in halved
        )
        vector = butterfly(vector, sizes)
        grad_tokens = scatter_row(grad_tokens)
    grad_tokens = grad_tokens.astype(F32)
    g_out, g_second = g_out.T, g_second.T
    vector = vector.reshape(-1)
    ends = [sum(p.shape[0] for p in small[:i]) for i in range(len(small) + 1)]
    g_g1, g_c1, g_bq, g_bv, g_bo, g_g2, g_c2, g_bf, g_bs = (vector[i:j] for i, j in zip(ends, ends[1:]))
    return (
        output, grad_tokens, g_g1, g_c1, g_query, g_bq, g_key, g_value, g_bv, g_out, g_bo,
        g_g2, g_c2, g_first, g_bf, g_second, g_bs,
    )


def solution(mesh):
    rows_spec = P("fsdp", ("ctx", "tp"), None)
    column, line = P("fsdp", "tp"), P("tp", "fsdp")
    column_out, line_out = P(("fsdp", "ctx"), "tp"), P("tp", ("fsdp", "ctx"))
    return jax.shard_map(
        functools.partial(shards, dict(mesh.shape)),
        mesh=mesh,
        in_specs=(
            rows_spec, P("fsdp", "ctx"), P(), P(), column, P(), column, column, P(), line, P(),
            P(), P(), column, P(), line, P(), rows_spec,
        ),
        out_specs=(
            rows_spec, rows_spec, P(), P(), column_out, P(), column_out, column_out, P(), line_out,
            P(), P(), P(), column_out, P(), line_out, P(),
        ),
        check_vma=False,
    )
```

time: 1420 us -> 938 us (0.66)
  waiting for transfers between devices: 543 us -> 101 us
  blocking collectives: 151 us -> 0 us
  Pallas kernels: 222 us -> 293 us
  starting transfers between devices: 31.9 us -> 94.5 us
  other arithmetic: 52 us -> 37.7 us
    unnamed x11 -> x3, waiting for transfers between devices: 291 us -> 1.39 us
    psum x1 -> x0, blocking collectives: 151 us -> none  [shards(): lax.psum((g_g1, g_c1, g_bq, g_bv, g_bo, g_g2, g_c2, jnp.concatenate(g_fir...]
    reduce_scatter x4 -> x0, waiting for transfers between devices: 115 us -> none  [scatter_grad(): lax.psum_scatter(jnp.concatenate(parts, axis=0), every, scatter_dimension...]
    pallas_call x2 -> x3, Pallas kernels: 222 us -> 293 us  [the longest x1 171 us: closing(): pl.pallas_call(lambda *refs: closing_kernel(kinds, True, tp, refs), out_s...]
    ppermute x6, starting transfers between devices: 24.7 us -> 89.8 us  [gather_row(): piece = lax.ppermute(piece, 'tp', pairs)]
    all_gather x1, waiting for transfers between devices: 0.02 us -> 46.2 us  [shards(): lax.all_gather(w_second.T, both, axis=0, tiled=True)]
    ppermute x6, waiting for transfers between devices: 56.4 us -> 16.1 us  [gather_row(): piece = lax.ppermute(piece, 'tp', pairs)]
    convert_element_type x0 -> x8, local copies, waits for them, and re-layouts: none -> 34.5 us  [the longest x4 21.4 us: shards(): g_second.append(dot(cot, act, 0, 0).astype(BF16))]
  transfers between devices with their start and end apart: 24 -> 15, of which waited for: 10 -> 3; matrix products, arithmetic and copies ran while one was open for 25% -> 25% of each run, Pallas kernels for 8% -> 13%
where the time goes in v2:
time: 938 us; the launch traced here: 921 us
  Pallas kernels  293 us (31%)
  matrix products  248 us (26%)
  local copies, waits for them, and re-layouts  131 us (14%)
  waiting for transfers between devices  101 us (11%)
  starting transfers between devices  94.5 us (10%)
  other arithmetic  37.7 us (4%)
  between operations  14.8 us (2%)
    dot_general x35, matrix products, dot(): lax.dot_general(left, right, (((left_dim,), (right_dim,)), ((), ())), pre...  248 us
    pallas_call x1, Pallas kernels, closing(): pl.pallas_call(lambda *refs: closing_kernel(kinds, True, tp, refs), out_s...  171 us
    ppermute x6, starting transfers between devices, gather_row(): piece = lax.ppermute(piece, 'tp', pairs)  89.8 us
    pallas_call x1, Pallas kernels, attention_backward(): pl.pallas_call(functools.partial(backward_kernel, tokens // block, contex...  76.7 us
    all_gather x1, waiting for transfers between devices, shards(): lax.all_gather(w_second.T, both, axis=0, tiled=True)  46.2 us
    pallas_call x1, Pallas kernels, attention_forward(): pl.pallas_call(functools.partial(forward_kernel, tokens // block, context...  46 us
    ppermute x2, waiting for transfers between devices, fetch(): lax.ppermute(value, 'ctx', [((c + c_step) % ctx, c) for c in range(ctx)])  37.4 us
    convert_element_type x4, local copies, waits for them, and re-layouts, shards(): g_second.append(dot(cot, act, 0, 0).astype(BF16))  21.4 us
  transfers between devices with their start and end apart: 15, of which 3 were waited for; matrix products, arithmetic and copies ran while one was open for 25% of the time, Pallas kernels for 13%

profile of v2, /device:TPU:0, one launch (start us, length us, event | category | flops | bytes accessed | tf_op | source)
XLA Modules:
  0.0 920.7 jit_solution(8079995062139431067)
XLA Ops:
  28.4 16.1 %collective-permute-done = bf16[256,1152]{1,0:T(8,128)(2,1)S(1)} collective-permute-done((bf16[256,1152]{1,0:T(8,128)(2,1)}, bf16[256,1152]{1,0:T(8,128)(2,1)S(1)}, u32[]{:S(2)}, u32[]{:S(2)}) %collective-permute-start) | collective-permute-done | bytes 589856 | tf_op jit(solution)/shard_map/ppermute | solution.py:543
  44.6 56.7 %collective-permute-start.9 = (bf16[256,1152]{1,0:T(8,128)(2,1)}, bf16[256,1152]{1,0:T(8,128)(2,1)}, u32[]{:S(2)}, u32[]{:S(2)}) collective-permute-start(bf16[256,1152]{1,0:T(8,128)(2,1)} %get-tuple-element.72), channel_id=1, source_target_pairs={{0,2},{1,3},{2,0},{3,1},{4,6},{5,7},{6,4},{7,5},{8,10},{9,11},{10,... | collective-permute-start | bytes 1769480 | tf_op jit(solution)/shard_map/ppermute | solution.py:543
  101.2 27.0 %collective-permute-start.8 = (bf16[256,1152]{1,0:T(8,128)(2,1)}, bf16[256,1152]{1,0:T(8,128)(2,1)}, u32[]{:S(2)}, u32[]{:S(2)}) collective-permute-start(bf16[256,1152]{1,0:T(8,128)(2,1)} %get-tuple-element.70), channel_id=1, source_target_pairs={{0,1},{1,2},{2,3},{3,0},{4,5},{5,6},{6,7},{7,4},{8,9},{9,10},{10,1... | collective-permute-start | bytes 1769480 | tf_op jit(solution)/shard_map/ppermute | solution.py:543
  136.2 37.4 %collective-permute-done.3 = bf16[1024,1152]{1,0:T(8,128)(2,1)} collective-permute-done((bf16[1024,1152]{1,0:T(8,128)(2,1)}, bf16[1024,1152]{1,0:T(8,128)(2,1)}, u32[]{:S(2)}, u32[]{:S(2)}) %collective-permute-start.3) | collective-permute-done | bytes 2359328 | tf_op jit(solution)/shard_map/ppermute | solution.py:567
  176.9 6.6 convert_element_type.129
  185.7 6.3 subtract_multiply_fusion
  192.0 15.3 %copy.89 = bf16[4608,1152]{0,1:T(8,128)(2,1)} copy(bf16[4608,1152]{1,0:T(8,128)(2,1)} %all-gather.4.cloned.1.call-done) | data formatting | bytes 21233664 | tf_op jit(solution)/shard_map/all_gather | solution.py:583
  207.3 14.6 %reshape.374 = bf16[4,1152,4,288]{1,0,3,2:T(4,128)(2,1)} reshape(bf16[4608,1152]{0,1:T(8,128)(2,1)} %copy.89) | data formatting | bytes 21233664 | tf_op jit(solution)/shard_map/reshape | solution.py:585
  221.9 7.6 slice.225
  243.9 14.8 %add_convert_fusion.k_ref.v_ref = bf16[2304,2048]{1,0:T(8,128)(2,1)} fusion(bf16[2304,1152]{1,0:T(8,128)(2,1)S(1)} %bitcast.134, bf16[2048,1152]{1,0:T(8,128)(2,1)S(1)} %bitcast.138, f32[2304]{0:T(1024)S(1)} %concatenate.32), kind=kOutput, calls=%fused_computation.1 | convolution fusion | flops 10881073152 | bytes 19473408 | tf_op jit(solution)/shard_map/dot_general | solution.py:21
  258.7 46.0 %attention_forward.1 = (bf16[1152,1024]{1,0:T(8,128)(2,1)}, f32[16,1,1024]{2,1,0:T(1,128)}) custom-call(s32[4]{0:T(128)} %get-tuple-element.57.count, s32[32]{0:T(128)} %reshape.373.index, bf16[1152,1024]{1,0:T(8,128)(2,1)} %multiply_convert_fusion.q_ref, bf16[2304,2048]{1,0:T(8,128)(2,1)} %add_convert_fusion.k_ref.v_ref, ...), custom_call_target="tpu_custom_call" | custom-call | flops 28991029248 | bytes 14155776 | tf_op jit(solution)/shard_map/attention_forward/pallas_call | solution.py:115
  304.7 7.2 fusion.50
  314.8 6.5 convolution_add_fusion.4
  321.3 46.2 %all-gather.8.cloned.1.call-done = bf16[4608,1076]{1,0:T(8,128)(2,1)} async-done(((bf16[288,1076]{1,0:T(8,128)(2,1)}), bf16[4608,1076]{1,0:T(8,128)(2,1)}) %all-gather.8.cloned.1.call-update) | async-done | bytes 9916432 | tf_op jit(solution)/shard_map/all_gather | solution.py:590
  367.5 9.8 %convert_reduce_fusion.8 = (f32[1076]{0:T(1024)}, bf16[1024,1076]{0,1:T(8,128)(2,1)S(1)}) fusion(f32[1024,1076]{0,1:T(8,128)} %convolution_add_fusion.4, bf16[4608,1076]{1,0:T(8,128)(2,1)} %all-gather.8.cloned.1.call-done, bf16[256,1152]{1,0:T(8,128)(2,1)} %collective-permute-done.10, bf16[256,1152]{1,0:T(8,128)(2,1)} %collective-permute-done.9, ...), kind=kOutput, calls=%fused_computation.50 | convolution fusion | flops 2570075136 | bytes 11645136 | tf_op jit(solution)/shard_map/dot_general | solution.py:21
  387.7 8.7 convert_reduce_fusion.7
  405.6 8.7 convert_reduce_fusion.6
  423.3 8.7 convert_reduce_fusion.5
  451.0 9.7 %multiply_reduce_fusion.2 = (f32[1152]{0:T(1024)}, f32[1024]{0:T(1024)S(1)}, f32[1024]{0:T(1024)S(1)}, f32[1152]{0:T(1024)}, f32[1024,1152]{1,0:T(8,128)S(1)}) fusion(f32[1024,1152]{1,0:T(8,128)S(1)} %bitcast.123, f32[1024]{0:T(1024)S(1)} %add_rsqrt_fusion.1, f32[1024]{0:T(1024)S(1)} %broadcast_multiply_fusion.5, f32[1152]{0:T(1024)S(1)} %copy-done.31, ...), kind=kOutput, calls=%fused_computation.32 | convolution fusion | flops 2552754176 | bytes 28481024 | tf_op jit(solution)/shard_map/dot_general | solution.py:21
  495.7 11.7 %add_convert_fusion.3 = bf16[1024,1152]{1,0:T(8,128)(2,1)S(1)} fusion(f32[1024,1152]{1,0:T(8,128)} %fusion.10, f32[1024,1152]{1,0:T(8,128)} %fusion.16, f32[1024,1152]{1,0:T(8,128)} %fusion.22, f32[1024,1152]{1,0:T(8,128)S(1)} %bitcast.123, f32[1152]{0:T(1024)S(1)} %copy-done.51, bf16[4608,1076]{1,0:T(8,128)(2,1)} %all-gather.8.cloned.1.call-done, ...), kind=kOutput, calls=%fused_computation.38 | convolution fusion | flops 2555596800 | bytes 28316160 | tf_op jit(solution)/shard_map/dot_general | solution.py:21
  511.5 76.7 %attention_backward.1 = (bf16[1152,1024]{1,0:T(8,128)(2,1)}, bf16[1152,2048]{1,0:T(8,128)(2,1)}, bf16[1152,2048]{1,0:T(8,128)(2,1)}) custom-call(s32[4]{0:T(128)} %get-tuple-element.57.count, s32[32]{0:T(128)} %reshape.373.index, bf16[1152,1024]{1,0:T(8,128)(2,1)} %multiply_convert_fusion.q_ref, bf16[2304,2048]{1,0:T(8,128)(2,1)} %add_convert_fusion.k_ref.v_ref, ...), custom_call_target="tpu_custom_call" | custom-call | flops 48318382080 | bytes 28311552 | tf_op jit(solution)/shard_map/attention_backward/pallas_call | solution.py:141
  588.2 6.6 convolution_convert_fusion.1
  594.8 7.9 convolution_convert_fusion.11
  602.7 7.8 convolution_convert_fusion.10
  610.9 9.4 %fusion.51 = f32[2048,1152]{1,0:T(8,128)} fusion(bf16[1152,2048]{1,0:T(8,128)(2,1)S(1)} %copy-done.59, bf16[1152,1152]{1,0:T(8,128)(2,1)S(1)} %bitcast.149), kind=kOutput, calls=%fused_computation.174 | convolution fusion | flops 5435817984 | bytes 16809984 | tf_op jit(solution)/shard_map/dot_general | solution.py:21
  620.7 10.1 %convolution_add_fusion = f32[2048,1152]{1,0:T(8,128)S(1)} fusion(f32[2048,1152]{1,0:T(8,128)} %fusion.51, bf16[1152,2048]{1,0:T(8,128)(2,1)S(1)} %bitcast.136, bf16[1152,1152]{1,0:T(8,128)(2,1)S(1)} %bitcast.150), kind=kOutput, calls=%fused_computation.5 | convolution fusion | flops 5438177280 | bytes 26247168 | tf_op jit(solution)/shard_map/dot_general | solution.py:21
  632.5 10.1 %convolution_convert_fusion.8 = bf16[1152,1076]{0,1:T(8,128)(2,1)} fusion(f32[1024,1076]{0,1:T(8,128)S(1)} %bitcast.170, bf16[256,1152]{1,0:T(8,128)(2,1)} %collective-permute-done.10, bf16[256,1152]{1,0:T(8,128)(2,1)} %collective-permute-done.9, bf16[256,1152]{1,0:T(8,128)(2,1)} %collective-permute-done.8, bf16[256,1152]{1,0:T(8,128)(2,1)S(1)} %copy-done.18), kind=kOutput, calls=%fused_computation.15 | convolution fusion | flops 2559195648 | bytes 9245696 | tf_op jit(solution)/shard_map/dot_general | solution.py:21
  642.6 6.4 convolution_convert_fusion.6
  649.0 7.6 convolution_convert_fusion.4
  656.5 6.7 convolution_convert_fusion.2
  707.0 11.7 %multiply_reduce_fusion.1 = (f32[1024]{0:T(1024)S(1)}, f32[1152]{0:T(1024)S(1)}, f32[1024]{0:T(1024)S(1)}, f32[1152]{0:T(1024)S(1)}, f32[1024,1152]{1,0:T(8,128)}) fusion(f32[2048,1152]{1,0:T(8,128)} %get-tuple-element.66, f32[1152]{0:T(1024)S(1)} %copy-done.37, bf16[1024,1152]{1,0:T(8,128)(2,1)} %collective-permute-done.11, ...), kind=kOutput, calls=%fused_computation.31 | convolution fusion | flops 2729701376 | bytes 21550592 | tf_op jit(solution)/shard_map/dot_general | solution.py:21
  730.4 170.6 %closing.1 = (f32[144,1076]{1,0:T(8,128)}, f32[144,1076]{1,0:T(8,128)}, f32[144,288]{1,0:T(8,128)}, f32[144,288]{1,0:T(8,128)}, f32[144,288]{1,0:T(8,128)}, /*in...) custom-call(bf16[2,2,2,144,1076]{4,3,2,1,0:T(8,128)(2,1)} %bitcast.1, ...), custom_call_target="tpu_custom_call" | custom-call | tf_op jit(solution)/shard_map/closing/pallas_call | solution.py:492
  (314 shorter events, 208.6 us)
Async XLA Ops:
  7.2 184.7 %all-gather.4.cloned.1.call-start = ((), (), s32[]{:S(2)}) async-start(), calls=%async_computation | async-start | bytes 11280384 | tf_op jit(solution)/shard_map/all_gather | solution.py:583
  10.7 304.1 %all-gather.6.cloned.1.call-start = ((), (), s32[]{:S(2)}) async-start(), calls=%async_computation.1 | async-start | bytes 11280384 | tf_op jit(solution)/shard_map/all_gather | solution.py:589
  11.5 356.0 %all-gather.8.cloned.1.call-start = ((), (), s32[]{:S(2)}) async-start(), calls=%async_computation.2 | async-start | bytes 11280384 | tf_op jit(solution)/shard_map/all_gather | solution.py:590
  13.1 118.1 %collective-permute-start.4 = (s32[1024]{0:T(1024)S(1)}, s32[1024]{0:T(1024)S(1)}, u32[]{:S(2)}, u32[]{:S(2)}) collective-permute-start(s32[1024]{0:T(1024)S(1)} %bitcast.157), channel_id=1, source_target_pairs={{4,0},{0,4},{5,1},{1,5},{6,2},{2,6},{7,3},{3,7},{12,8},{8,12},{13,... | collective-permute-start | bytes 12296 | tf_op jit(solution)/shard_map/ppermute | solution.py:567
  17.4 27.2 %collective-permute-start = (bf16[256,1152]{1,0:T(8,128)(2,1)}, bf16[256,1152]{1,0:T(8,128)(2,1)S(1)}, u32[]{:S(2)}, u32[]{:S(2)}) collective-permute-start(bf16[256,1152]{1,0:T(8,128)(2,1)} %get-tuple-element.77), channel_id=1, source_target_pairs={{0,1},{1,2},{2,3},{3,0},{4,5},{5,6},{6,7},{7,4},{8,9},{9,10},{10,1... | collective-permute-start | bytes 1769480 | tf_op jit(solution)/shard_map/ppermute | solution.py:543
  18.9 82.3 %collective-permute-start.1 = (bf16[256,1152]{1,0:T(8,128)(2,1)}, bf16[256,1152]{1,0:T(8,128)(2,1)S(1)}, u32[]{:S(2)}, u32[]{:S(2)}) collective-permute-start(bf16[256,1152]{1,0:T(8,128)(2,1)} %get-tuple-element.78), channel_id=1, source_target_pairs={{0,2},{1,3},{2,0},{3,1},{4,6},{5,7},{6,4},{7,5},{8,10},{9,11},{10,... | collective-permute-start | bytes 1769480 | tf_op jit(solution)/shard_map/ppermute | solution.py:543
  21.5 106.7 %collective-permute-start.2 = (bf16[256,1152]{1,0:T(8,128)(2,1)}, bf16[256,1152]{1,0:T(8,128)(2,1)S(1)}, u32[]{:S(2)}, u32[]{:S(2)}) collective-permute-start(bf16[256,1152]{1,0:T(8,128)(2,1)} %get-tuple-element.76), channel_id=1, source_target_pairs={{0,3},{1,0},{2,1},{3,2},{4,7},{5,4},{6,5},{7,6},{8,11},{9,8},{10,9... | collective-permute-start | bytes 1769480 | tf_op jit(solution)/shard_map/ppermute | solution.py:543
  25.8 434.9 %copy-start.17 = (bf16[256,1152]{1,0:T(8,128)(2,1)}, bf16[256,1152]{1,0:T(8,128)(2,1)S(1)}, u32[]{:S(2)}) copy-start(bf16[256,1152]{1,0:T(8,128)(2,1)S(1)} %get-tuple-element.69) | copy-start | bytes 1769476
  25.8 104.7 %copy-start.32 = (f32[4304]{0:T(1024)S(1)}, f32[4304]{0:T(1024)}, u32[]{:S(2)}) copy-start(f32[4304]{0:T(1024)} %param.32) | copy-start | bytes 51652
  25.8 105.4 %copy-start.45 = (f32[1152]{0:T(1024)S(1)}, f32[1152]{0:T(1024)}, u32[]{:S(2)}) copy-start(f32[1152]{0:T(1024)} %param.26) | copy-start | bytes 13828
  25.8 295.5 %collective-permute-start.10 = (bf16[256,1152]{1,0:T(8,128)(2,1)}, bf16[256,1152]{1,0:T(8,128)(2,1)}, u32[]{:S(2)}, u32[]{:S(2)}) collective-permute-start(bf16[256,1152]{1,0:T(8,128)(2,1)} %get-tuple-element.71), channel_id=1, source_target_pairs={{0,3},{1,0},{2,1},{3,2},{4,7},{5,4},{6,5},{7,6},{8,11},{9,8},{10,9... | collective-permute-start | bytes 1769480 | tf_op jit(solution)/shard_map/ppermute | solution.py:543
  44.6 276.7 %collective-permute-start.9 = (bf16[256,1152]{1,0:T(8,128)(2,1)}, bf16[256,1152]{1,0:T(8,128)(2,1)}, u32[]{:S(2)}, u32[]{:S(2)}) collective-permute-start(bf16[256,1152]{1,0:T(8,128)(2,1)} %get-tuple-element.72), channel_id=1, source_target_pairs={{0,2},{1,3},{2,0},{3,1},{4,6},{5,7},{6,4},{7,5},{8,10},{9,11},{10,... | collective-permute-start | bytes 1769480 | tf_op jit(solution)/shard_map/ppermute | solution.py:543
  101.2 220.0 %collective-permute-start.8 = (bf16[256,1152]{1,0:T(8,128)(2,1)}, bf16[256,1152]{1,0:T(8,128)(2,1)}, u32[]{:S(2)}, u32[]{:S(2)}) collective-permute-start(bf16[256,1152]{1,0:T(8,128)(2,1)} %get-tuple-element.70), channel_id=1, source_target_pairs={{0,1},{1,2},{2,3},{3,0},{4,5},{5,6},{6,7},{7,4},{8,9},{9,10},{10,1... | collective-permute-start | bytes 1769480 | tf_op jit(solution)/shard_map/ppermute | solution.py:543
  129.8 43.9 %collective-permute-start.3 = (bf16[1024,1152]{1,0:T(8,128)(2,1)}, bf16[1024,1152]{1,0:T(8,128)(2,1)}, u32[]{:S(2)}, u32[]{:S(2)}) collective-permute-start(bf16[1024,1152]{1,0:T(8,128)(2,1)} %pad_maximum_fusion), channel_id=1, source_target_pairs={{4,0},{0,4},{5,1},{1,5},{6,2},{2,6},{7,3},{3,7},{12,8},{8,12},{13,... | collective-permute-start | bytes 7077896 | tf_op jit(solution)/shard_map/ppermute | solution.py:567
  238.0 66.6 %copy-start.11 = (bf16[1,4,288,1152]{3,2,1,0:T(8,128)(2,1)}, bf16[1,4,288,1152]{3,2,1,0:T(8,128)(2,1)S(1)}, u32[]{:S(2)}) copy-start(bf16[1,4,288,1152]{3,2,1,0:T(8,128)(2,1)S(1)} %copy.92) | copy-start | bytes 7962628
  258.7 46.0 %copy-start.50 = (f32[1152]{0:T(1024)S(1)}, f32[1152]{0:T(1024)}, u32[]{:S(2)}) copy-start(f32[1152]{0:T(1024)} %param.28) | copy-start | bytes 13828
  460.7 15.5 %slice-start.25 = ((s8[4423680]{0:T(1024)(128)(4,1)}), s8[229376]{0:T(1024)(128)(4,1)S(1)}, s32[]{:S(2)}) async-start(s8[4423680]{0:T(1024)(128)(4,1)} %bitcast.175), calls=%async_computation.28 | async-start | bytes 458752
  466.7 16.8 %slice-start.21 = ((s8[4423680]{0:T(1024)(128)(4,1)}), s8[4194304]{0:T(1024)(128)(4,1)S(1)}, s32[]{:S(2)}) async-start(s8[4423680]{0:T(1024)(128)(4,1)} %bitcast.171), calls=%async_computation.24 | async-start | bytes 8388608
  471.3 12.2 %slice-start.22 = ((s8[4423680]{0:T(1024)(128)(4,1)}), s8[229376]{0:T(1024)(128)(4,1)S(1)}, s32[]{:S(2)}) async-start(s8[4423680]{0:T(1024)(128)(4,1)} %bitcast.171), calls=%async_computation.25 | async-start | bytes 458752
  477.5 12.0 %slice-start.17 = ((s8[4423680]{0:T(1024)(128)(4,1)}), s8[4194304]{0:T(1024)(128)(4,1)S(1)}, s32[]{:S(2)}) async-start(s8[4423680]{0:T(1024)(128)(4,1)} %bitcast.167), calls=%async_computation.20 | async-start | bytes 8388608
  495.7 92.4 %slice-start.6 = ((s8[4718592]{0:T(1024)(128)(4,1)}), s8[4194304]{0:T(1024)(128)(4,1)S(1)}, s32[]{:S(2)}) async-start(s8[4718592]{0:T(1024)(128)(4,1)} %bitcast.139), calls=%async_computation.9 | async-start | bytes 8388608
  510.0 191.1 %collective-permute-start.5 = (bf16[256,1152]{1,0:T(8,128)(2,1)}, bf16[256,1152]{1,0:T(8,128)(2,1)}, u32[]{:S(2)}, u32[]{:S(2)}) collective-permute-start(bf16[256,1152]{1,0:T(8,128)(2,1)} %get-tuple-element.75), channel_id=1, source_target_pairs={{1,0},{2,1},{3,2},{0,3},{5,4},{6,5},{7,6},{4,7},{9,8},{10,9},{11,1... | collective-permute-start | bytes 1769480 | tf_op jit(solution)/shard_map/ppermute | solution.py:553
  511.5 76.7 %slice-start.7 = ((s8[4718592]{0:T(1024)(128)(4,1)}), s8[524288]{0:T(1024)(128)(4,1)S(1)}, s32[]{:S(2)}) async-start(s8[4718592]{0:T(1024)(128)(4,1)} %bitcast.139), calls=%async_computation.10 | async-start | bytes 1048576
  588.2 14.5 %slice-start.2 = ((s8[4718592]{0:T(1024)(128)(4,1)}), s8[4194304]{0:T(1024)(128)(4,1)S(1)}, s32[]{:S(2)}) async-start(s8[4718592]{0:T(1024)(128)(4,1)} %bitcast.135), calls=%async_computation.5 | async-start | bytes 8388608
  620.3 12.1 %slice-start.19 = ((s8[4423680]{0:T(1024)(128)(4,1)}), s8[4194304]{0:T(1024)(128)(4,1)S(1)}, s32[]{:S(2)}) async-start(s8[4423680]{0:T(1024)(128)(4,1)} %bitcast.169), calls=%async_computation.22 | async-start | bytes 8388608
  632.4 74.5 %collective-permute-start.11 = (bf16[1024,1152]{1,0:T(8,128)(2,1)}, bf16[1024,1152]{1,0:T(8,128)(2,1)}, u32[]{:S(2)}, u32[]{:S(2)}) collective-permute-start(bf16[1024,1152]{1,0:T(8,128)(2,1)} %slice.317), channel_id=1, source_target_pairs={{0,4},{4,0},{1,5},{5,1},{2,6},{6,2},{3,7},{7,3},{8,12},{12,8},{9,1... | collective-permute-start | bytes 7077896 | tf_op jit(solution)/shard_map/ppermute | solution.py:576
  642.6 14.0 %slice-start.15 = ((s8[4423680]{0:T(1024)(128)(4,1)}), s8[4194304]{0:T(1024)(128)(4,1)S(1)}, s32[]{:S(2)}) async-start(s8[4423680]{0:T(1024)(128)(4,1)} %bitcast.165), calls=%async_computation.18 | async-start | bytes 8388608
  664.7 38.3 %collective-permute-start.6 = (bf16[256,1152]{1,0:T(8,128)(2,1)}, bf16[256,1152]{1,0:T(8,128)(2,1)}, u32[]{:S(2)}, u32[]{:S(2)}) collective-permute-start(bf16[256,1152]{1,0:T(8,128)(2,1)} %get-tuple-element.74), channel_id=1, source_target_pairs={{2,0},{3,1},{0,2},{1,3},{6,4},{7,5},{4,6},{5,7},{10,8},{11,9},{8,1... | collective-permute-start | bytes 1769480 | tf_op jit(solution)/shard_map/ppermute | solution.py:553
  666.5 38.4 %collective-permute-start.7 = (bf16[256,1152]{1,0:T(8,128)(2,1)S(1)}, bf16[256,1152]{1,0:T(8,128)(2,1)}, u32[]{:S(2)}, u32[]{:S(2)}) collective-permute-start(bf16[256,1152]{1,0:T(8,128)(2,1)S(1)} %get-tuple-element.73), channel_id=1, source_target_pairs={{3,0},{0,1},{1,2},{2,3},{7,4},{4,5},{5,6},{6,7},{11,8},{8,9},{9,10... | collective-permute-start | bytes 1769480 | tf_op jit(solution)/shard_map/ppermute | solution.py:553
  706.9 11.9 %copy-start.34 = (f32[1152]{0:T(1024)S(1)}, f32[1152]{0:T(1024)}, u32[]{:S(2)}) copy-start(f32[1152]{0:T(1024)} %get-tuple-element.55) | copy-start | bytes 13828
  706.9 11.8 %copy-start.35 = (f32[1152]{0:T(1024)S(1)}, f32[1152]{0:T(1024)}, u32[]{:S(2)}) copy-start(f32[1152]{0:T(1024)} %get-tuple-element.68) | copy-start | bytes 13828
  707.0 12.5 %slice-start.8 = ((f32[2048]{0:T(1024)}), f32[1024]{0:T(1024)S(1)}, s32[]{:S(2)}) async-start(f32[2048]{0:T(1024)} %copy-done.33), calls=%async_computation.11 | async-start | bytes 8192 | tf_op jit(solution)/shard_map/slice | solution.py:652
  (70 other events, 469.0 us)
Sparse Core Ops, SparseCore 0:
  10.9 177.9 all-gather.3
  191.1 87.0 all-gather.5
  280.5 86.9 all-gather.7

commit v3 on v2

--- a/solution.py
+++ b/solution.py
@@ -247,6 +247,390 @@
         piece = lax.dynamic_index_in_dim(stack, place ^ k, 0, keepdims=False)
         total = total + exchange(piece, "tp", tp, k).astype(F32)
     return total
+
+
+def opening_kernel(
+    tp, tokens, shard, ff_in, x_all, wt, ff, pieces,
+    st, rt, sy, ry, sz, rz, sx, rx, sn, rn, own, fsz, frz, fsx, frx, fsy, fry, fsn, frn
+):
+    f, c, z = lax.axis_index("fsdp"), lax.axis_index("ctx"), lax.axis_index("tp")
+    near, across = f + 1 - 2 * (f % 2), f + 2 - 4 * (f // 2)
+    other_c = 1 - c
+
+    barrier = pltpu.get_barrier_semaphore()
+    for where in ({"fsdp": near}, {"fsdp": across}, {"ctx": other_c}):
+        pl.semaphore_signal(barrier, inc=1, device_id=where, device_id_type=MESH)
+    for k in range(1, tp):
+        pl.semaphore_signal(barrier, inc=1, device_id={"tp": lax.rem(z + k, tp)}, device_id_type=MESH)
+    start = pltpu.make_async_copy(shard, pieces.at[z, f], own.at[0])
+    start.start()
+    mine = [pltpu.make_async_copy(ff_in.at[m], ff.at[m, z, f], own.at[1 + m]) for m in range(2)]
+    for copy in mine:
+        copy.start()
+    start.wait()
+    pl.semaphore_wait(barrier, 2 + tp)
+
+    def remote(src, dst, send, recv, where):
+        return pltpu.make_async_remote_copy(
+            src_ref=src, dst_ref=dst, send_sem=send, recv_sem=recv, device_id=where, device_id_type=MESH
+        )
+
+    def along(t, side):
+        return remote(pieces.at[t, f], pieces.at[t, f], sz.at[t, side], rz.at[t], {"tp": z + 1 if side else z - 1})
+
+    def cross(t):
+        return remote(pieces.at[t, f], pieces.at[t, f], sx.at[t], rx.at[t], {"fsdp": across})
+
+    def beside(t, i):
+        source = across if i else f
+        return remote(pieces.at[t, source], pieces.at[t, source], sn.at[t, i], rn.at[t, i], {"fsdp": near})
+
+    def token(k, row):
+        return remote(tokens.at[k], x_all.at[0, row], st.at[k], rt.at[row], {"tp": k})
+
+    def half(t):
+        return remote(x_all.at[0, t], x_all.at[1, t], sy.at[t], ry.at[t], {"ctx": other_c})
+
+    def ff_along(t, side):
+        part = ff.at[c, t, f]
+        return remote(part, part, fsz.at[t, side], frz.at[t], {"tp": z + 1 if side else z - 1})
+
+    def ff_cross(m, t):
+        part = ff.at[m, t, f]
+        return remote(part, part, fsx.at[m, t], frx.at[m, t], {"fsdp": across})
+
+    def ff_half(t, i):
+        part = ff.at[c, t, across if i else f]
+        return remote(part, part, fsy.at[t, i], fry.at[t, i], {"ctx": other_c})
+
+    def ff_beside(m, t, i):
+        part = ff.at[m, t, across if i else f]
+        return remote(part, part, fsn.at[m, t, i], frn.at[m, t, i], {"fsdp": near})
+
+    def passes(t, right, left):
+        @pl.when((t <= z) & (z < tp - 1))
+        def _():
+            right(t)
+
+        @pl.when((t >= z) & (z > 0))
+        def _():
+            left(t)
+
+    def onward(t):
+        passes(t, lambda t: along(t, 1).start(), lambda t: along(t, 0).start())
+        cross(t).start()
+        beside(t, 0).start()
+
+    def ff_pass(t):
+        passes(t, lambda t: ff_along(t, 1).start(), lambda t: ff_along(t, 0).start())
+
+    def arrivals(d, wait, then):
+        for t, there in ((z - d, z >= d), (z + d, z + d < tp)):
+            @pl.when(there)
+            def _():
+                wait(t)
+                then(t)
+
+    onward(z)
+    local = pltpu.make_async_copy(tokens.at[z], x_all.at[0, z], own.at[0])
+    local.start()
+    for k in range(1, tp):
+        token(z ^ k, z).start()
+    for m in range(2):
+        mine[m].wait()
+        ff_cross(m, z).start()
+        ff_beside(m, z, 0).start()
+    local.wait()
+    half(z).start()
+    for d in range(1, tp):
+        arrivals(d, lambda t: along(t, 0).wait_recv(), onward)
+        block = z ^ d
+        token(block, block).wait_recv()
+        half(block).start()
+        cross(z ^ (d - 1)).wait_recv()
+        beside(z ^ (d - 1), 1).start()
+        if d == 1:
+            ff_pass(z)
+    cross(z ^ (tp - 1)).wait_recv()
+    beside(z ^ (tp - 1), 1).start()
+
+    depth = shard.shape[0]
+    columns = shard.shape[1] // 4
+
+    def turn(t):
+        for i in range(2):
+            beside(t, i).wait_recv()
+        for g in range(4):
+            for w in range(4):
+                piece = pieces[t, g, :, w * columns : (w + 1) * columns].astype(F32).T.astype(BF16)
+                wt[w, pl.ds(pl.multiple_of(t * columns, 32), columns), g * depth : (g + 1) * depth] = piece
+
+    def ff_onward(t):
+        ff_pass(t)
+        ff_cross(c, t).start()
+        ff_half(t, 0).start()
+        ff_beside(c, t, 0).start()
+
+    def ff_second(t):
+        ff_cross(c, t).wait_recv()
+        ff_half(t, 1).start()
+        ff_beside(c, t, 1).start()
+
+    for d in range(1, tp):
+        arrivals(d, lambda t: ff_along(t, 0).wait_recv(), ff_onward)
+        if d == 1:
+            for m in range(2):
+                ff_cross(m, z).wait_recv()
+                ff_beside(m, z, 1).start()
+        else:
+            arrivals(d - 1, lambda t: None, ff_second)
+        turn(z ^ (d - 1))
+    turn(z ^ (tp - 1))
+    arrivals(tp - 1, lambda t: None, ff_second)
+    for d in range(1, tp):
+
+        def handed(t):
+            for i in range(2):
+                ff_half(t, i).wait_recv()
+                ff_beside(1 - c, t, i).start()
+
+        arrivals(d, lambda t: None, handed)
+
+    for k in range(tp):
+        t = z ^ k
+        passes(t, lambda t: along(t, 1).wait_send(), lambda t: along(t, 0).wait_send())
+        passes(t, lambda t: ff_along(t, 1).wait_send(), lambda t: ff_along(t, 0).wait_send())
+        cross(t).wait_send()
+        beside(t, 0).wait_send()
+        beside(t, 1).wait_send()
+        if k:
+            token(t, z).wait_send()
+        half(t).wait()
+        for m in range(2):
+            if k == 0:
+                ff_cross(m, t).wait_send()
+            for i in range(2):
+                ff_beside(m, t, i).wait()
+        if k:
+            ff_cross(c, t).wait_send()
+            for i in range(2):
+                ff_half(t, i).wait_send()
+
+
+def opening(tokens, shard, ff_in, tp):
+    rows, span, width = tokens.shape
+    vmem, hbm = pl.BlockSpec(memory_space=pltpu.VMEM), pl.BlockSpec(memory_space=pl.ANY)
+    depth, columns = shard.shape[0], shard.shape[1] // 4
+    dma = pltpu.SemaphoreType.DMA
+    return pl.pallas_call(
+        functools.partial(opening_kernel, tp),
+        out_shape=(
+            jax.ShapeDtypeStruct((2, rows, span, width), BF16),
+            jax.ShapeDtypeStruct((4, tp * columns, 4 * depth), BF16),
+            jax.ShapeDtypeStruct((2, tp, 4) + ff_in.shape[1:], BF16),
+        ),
+        in_specs=[hbm, hbm, hbm],
+        out_specs=(hbm, vmem, hbm),
+        scratch_shapes=[pltpu.VMEM((tp, 4, depth, 4 * columns), BF16)]
+        + [dma((tp,))] * 4
+        + [dma((tp, 2)), dma((tp,)), dma((tp,)), dma((tp,)), dma((tp, 2)), dma((tp, 2)), dma((3,))]
+        + [dma((tp, 2)), dma((tp,)), dma((2, tp)), dma((2, tp)), dma((tp, 2)), dma((tp, 2))]
+        + [dma((2, tp, 2)), dma((2, tp, 2))],
+        compiler_params=pltpu.CompilerParams(collective_id=2, has_side_effects=True, vmem_limit_bytes=48 << 20),
+        name="opening",
+    )(tokens, shard, ff_in)
+
+
+def feed_kernel(
+    tp, n2, cot, bias, ff, y, dn2, g_first, g_second, g_bias,
+    n2t, cott, weights, act, d_pre, near_part, recv1, recv2, recv3, recvz,
+    lw, s1, r1, s2, r2, s3, r3, s4, r4
+):
+    f, c, z = lax.axis_index("fsdp"), lax.axis_index("ctx"), lax.axis_index("tp")
+    x, core = f // 2, f % 2
+    near, across, other_c = f + 1 - 2 * core, f + 2 - 4 * x, 1 - c
+    tokens, width = n2.shape
+    depth = width // 4
+    order = list(range(tp - 1, -1, -1))
+
+    def load(i):
+        return [pltpu.make_async_copy(ff.at[m, z ^ order[i]], weights.at[m], lw.at[m]) for m in range(2)]
+
+    for copy in load(0):
+        copy.start()
+
+    barrier = pltpu.get_barrier_semaphore()
+    for where in ({"fsdp": near}, {"fsdp": across}, {"ctx": other_c}):
+        pl.semaphore_signal(barrier, inc=1, device_id=where, device_id_type=MESH)
+    for k in range(1, tp):
+        pl.semaphore_signal(barrier, inc=1, device_id={"tp": z ^ k}, device_id_type=MESH)
+
+    @pl.loop(0, width // 128)
+    def _(i):
+        part = pl.ds(pl.multiple_of(i * 128, 128), 128)
+        n2t[part, :] = n2[:, part].astype(F32).T.astype(BF16)
+        cott[part, :] = cot[:, part].astype(F32).T.astype(BF16)
+
+    y[...] = jnp.zeros_like(y)
+    dn2[...] = jnp.zeros_like(dn2)
+    pl.semaphore_wait(barrier, 2 + tp)
+
+    def remote(src, dst, send, recv, where):
+        return pltpu.make_async_remote_copy(
+            src_ref=src, dst_ref=dst, send_sem=send, recv_sem=recv, device_id=where, device_id_type=MESH
+        )
+
+    def first(j, m):
+        return remote(near_part.at[m], recv1.at[j], s1.at[j], r1.at[j], {"fsdp": near})
+
+    def second(j, m):
+        if m == 0:
+            return remote(recv1.at[j, 1 - x], recv2.at[j], s2.at[j], r2.at[j], {"fsdp": across})
+        return remote(recv1.at[j, :, 1 - c], recv2.at[j], s2.at[j], r2.at[j], {"ctx": other_c})
+
+    def third(j, m):
+        if m == 0:
+            return remote(recv2.at[j, 1 - c], recv3.at[j], s3.at[j], r3.at[j], {"ctx": other_c})
+        return remote(recv2.at[j, 1 - x], recv3.at[j], s3.at[j], r3.at[j], {"fsdp": across})
+
+    def last(j, m, k):
+        return remote(recv3.at[j], recvz.at[m, k - 1], s4.at[m, k - 1], r4.at[m, k - 1], {"tp": z ^ k})
+
+    half = depth // 2
+    tile = 48
+
+    def stage2(i):
+        for m in range(2):
+            j = 2 * i + m
+            second(j, m).wait()
+
+            @pl.loop(0, half // tile)
+            def _(n):
+                r = pl.ds(pl.multiple_of(n * tile, 16), tile)
+                for a in range(2):
+                    kept = recv1[j, x, a, r] if m == 0 else recv1[j, a, c, r]
+                    recv2[j, a, r] = (kept.astype(F32) + recv2[j, a, r].astype(F32)).astype(BF16)
+
+            third(j, m).start()
+
+    def stage3(i):
+        for m in range(2):
+            j = 2 * i + m
+            third(j, m).wait()
+
+            @pl.loop(0, half // tile)
+            def _(n):
+                r = pl.ds(pl.multiple_of(n * tile, 16), tile)
+                recv3[j, r] = (recv2[j, c if m == 0 else x, r].astype(F32) + recv3[j, r].astype(F32)).astype(BF16)
+
+            if order[i]:
+                last(j, m, order[i]).start()
+
+    rows_tile = 256
+    for i in range(tp):
+        for copy in load(i):
+            copy.wait()
+        t = z ^ order[i]
+        g_bias[t] = jnp.zeros_like(g_bias[t])
+
+        @pl.loop(0, tokens // rows_tile)
+        def _(n):
+            r = pl.ds(pl.multiple_of(n * rows_tile, rows_tile), rows_tile)
+            value, slope = gelu_pair(dot(n2[r, :], weights[0], 1, 0) + bias[t])
+            act[r, :] = value.astype(BF16)
+            back = (dot(cot[r, :], weights[1], 1, 0) * slope).astype(BF16)
+            d_pre[r, :] = back
+            g_bias[t] += jnp.sum(back.astype(F32), axis=0, keepdims=True)
+            y[r, :] += dot(act[r, :], weights[1], 1, 1)
+            dn2[r, :] += dot(back, weights[0], 1, 1)
+
+        if i + 1 < tp:
+            for copy in load(i + 1):
+                copy.start()
+        if i:
+            stage2(i - 1)
+        sides = ((n2t, d_pre), (cott, act))
+        for m, (left, right) in enumerate(sides):
+            j = 2 * i + m
+            if i:
+                first(j - 2, m).wait_send()
+
+            @pl.loop(0, 2)
+            def _(a):
+                rows = pl.ds(pl.multiple_of((2 * a + 1 - core) * depth, 32), depth)
+                grad = dot(left[rows, :], right[...], 1, 0).astype(BF16)
+                for b in range(2):
+                    near_part[m, a, b] = grad[b * half : (b + 1) * half]
+
+            first(j, m).start()
+        if i:
+            stage3(i - 1)
+        for m, (left, right) in enumerate(sides):
+            j = 2 * i + m
+            first(j, m).wait_recv()
+
+            @pl.loop(0, 2)
+            def _(a):
+                rows = pl.ds(pl.multiple_of((2 * a + core) * depth, 32), depth)
+                grad = dot(left[rows, :], right[...], 1, 0)
+                for b in range(2):
+                    recv1[j, a, b] = (grad[b * half : (b + 1) * half] + recv1[j, a, b].astype(F32)).astype(BF16)
+
+            second(j, m).start()
+    stage2(tp - 1)
+    stage3(tp - 1)
+    for m, out in enumerate((g_first, g_second)):
+        first(2 * (tp - 1) + m, m).wait_send()
+        for k in range(1, tp):
+            last(2 * (tp - 1 - k) + m, m, k).wait()
+
+        @pl.loop(0, half // tile)
+        def _(n):
+            r = pl.ds(pl.multiple_of(n * tile, 16), tile)
+            total = recv3[2 * (tp - 1) + m, r].astype(F32)
+            for k in range(1, tp):
+                total = total + recvz[m, k - 1, r].astype(F32)
+            out[r] = total
+
+
+def feed(n2, cot, bias, ff, tp):
+    tokens, width = n2.shape
+    units, half = ff.shape[-1], width // 8
+    vmem, hbm = pl.BlockSpec(memory_space=pltpu.VMEM), pl.BlockSpec(memory_space=pl.ANY)
+    dma = pltpu.SemaphoreType.DMA
+    return pl.pallas_call(
+        functools.partial(feed_kernel, tp),
+        out_shape=(
+            jax.ShapeDtypeStruct((tokens, width), F32),
+            jax.ShapeDtypeStruct((tokens, width), F32),
+            jax.ShapeDtypeStruct((half, units), F32),
+            jax.ShapeDtypeStruct((half, units), F32),
+            jax.ShapeDtypeStruct((tp, 1, units), F32),
+        ),
+        in_specs=[vmem, vmem, vmem, hbm],
+        out_specs=(vmem,) * 5,
+        scratch_shapes=[
+            pltpu.VMEM((width, tokens), BF16),
+            pltpu.VMEM((width, tokens), BF16),
+            pltpu.VMEM((2, width, units), BF16),
+            pltpu.VMEM((tokens, units), BF16),
+            pltpu.VMEM((tokens, units), BF16),
+            pltpu.VMEM((2, 2, 2, half, units), BF16),
+            pltpu.VMEM((2 * tp, 2, 2, half, units), BF16),
+            pltpu.VMEM((2 * tp, 2, half, units), BF16),
+            pltpu.VMEM((2 * tp, half, units), BF16),
+            pltpu.VMEM((2, tp - 1, half, units), BF16),
+            dma((2,)),
+        ]
+        + [dma((2 * tp,))] * 6
+        + [dma((2, tp - 1))] * 2,
+        compiler_params=pltpu.CompilerParams(collective_id=3, has_side_effects=True, vmem_limit_bytes=63 << 20),
+        cost_estimate=pl.CostEstimate(
+            flops=12 * tokens * width * tp * units, bytes_accessed=4 * width * tp * units + 16 * tokens * width,
+            transcendentals=tokens * tp * units,
+        ),
+        name="feed",
+    )(n2, cot, bias, ff)
 
 
 def closing_kernel(kinds, moved, tp, refs):
@@ -545,14 +929,20 @@
         return got
 
     def scatter_row(values):
-        out = jnp.zeros((rows, span) + values.shape[1:], values.dtype)
+        out = jnp.zeros((rows,) + values[0].shape, values[0].dtype)
         for k in range(rows):
-            piece = values[k * span : (k + 1) * span]
+            piece = values[k]
             pairs = [(b, a) for a, b in out_permutation(k)]
             if any(a != b for a, b in pairs):
                 piece = lax.ppermute(piece, "tp", pairs)
             out = lax.dynamic_update_index_in_dim(out, piece, (mine + k) % rows, 0)
         return out
+
+    def in_order(pieces):
+        out = jnp.zeros((rows,) + pieces[0].shape, pieces[0].dtype)
+        for k in range(rows):
+            out = lax.dynamic_update_index_in_dim(out, pieces[k], (place - k) % rows, 0)
+        return out.reshape((-1,) + pieces[0].shape[1:])
 
     def peers(step):
         s_step, c_step = step % group, step // group
@@ -578,24 +968,34 @@
 
     steps = group * ctx
 
-    heads_dev = w_query.shape[1]
+    heads_dev, units = w_query.shape[1], w_first.shape[1]
     both = ("tp", "fsdp")
-    qkvo = lax.all_gather(
-        jnp.concatenate([w_query, w_key, w_value, w_output.T], axis=1), both, axis=0, tiled=True
-    ).reshape(tp, width, 4, heads_dev)
-    qkvo = qkvo.transpose(2, 0, 3, 1).reshape(4, tp * heads_dev, width)
+    shard = jnp.concatenate([w_query, w_key, w_value, w_output.T], axis=1)
+    paired = sizes["fsdp"] == 4 and ctx == 2 and group == 1 and bits_of(tp)
+    if paired:
+        x_all16, qkvo, both_ff = opening(tokens, shard, jnp.stack([w_first, w_second.T]), tp)
+        both_ff = both_ff.reshape(2, tp, width, units)
+        x_all16 = x_all16.reshape(2 * rows * span, width)
+    else:
+        first = lax.all_gather(w_first, both, axis=0, tiled=True).reshape(tp, width, units)
+        second = lax.all_gather(w_second.T, both, axis=0, tiled=True).reshape(tp, width, units)
+        qkvo = lax.all_gather(shard, both, axis=0, tiled=True).reshape(tp, width, 4, heads_dev)
+        qkvo = qkvo.transpose(2, 0, 3, 1).reshape(4, tp * heads_dev, width)
+        x16 = jnp.concatenate(gather_row(tokens), axis=0)
+        x_all16 = jnp.concatenate([x16] + [fetch(x16, i) for i in range(1, steps)], axis=0)
     wq, wkv, wo = qkvo[0], qkvo[1:3].reshape(2 * tp * heads_dev, width), qkvo[3]
-    units = w_first.shape[1]
-    first = lax.all_gather(w_first, both, axis=0, tiled=True).reshape(tp, width, units)
-    second = lax.all_gather(w_second.T, both, axis=0, tiled=True).reshape(tp, width, units)
-
-    x16 = jnp.concatenate(gather_row(tokens), axis=0)
     count = rows * span
     ids = lax.dynamic_index_in_dim(picture, row, 0, keepdims=False).reshape(tp, span)
-    order = part * rows + (row - jnp.arange(rows)) % rows
-    ids = jnp.take(ids, order, axis=0).reshape(count)
-    cot = jnp.concatenate(gather_row(cotangent), axis=0)
-    x_all16 = jnp.concatenate([x16] + [fetch(x16, i) for i in range(1, steps)], axis=0)
+    if not paired:
+        order = part * rows + (row - jnp.arange(rows)) % rows
+        ids = jnp.take(ids, order, axis=0)
+    ids = ids.reshape(count)
+    cotangent, x_all16 = lax.optimization_barrier((cotangent, x_all16))
+    cot = gather_row(cotangent)
+    if paired:
+        cot = in_order(cot)
+    else:
+        cot = jnp.concatenate(cot, axis=0)
     kid = jnp.concatenate([ids] + [fetch(ids, i) for i in range(1, steps)], axis=0)
     block = 256 if count % 256 == 0 else count
     blocks, index = active_blocks(ids, kid, block, block)
@@ -614,20 +1014,31 @@
 
     scaled2, inverse2 = norm_stats(h)
     n2 = (scaled2 * ln2_gain + ln2_bias).astype(BF16)
-    y = h + b_second
-    d_n2 = jnp.zeros_like(h)
-    g_first, g_second, g_first_bias = [], [], []
-    for t in range(tp):
-        pre = dot(n2, first[t], 1, 0) + b_first[t * units : (t + 1) * units]
-        value, slope = gelu_pair(pre)
-        act = value.astype(BF16)
-        y = y + dot(act, second[t], 1, 1)
-        d_pre = (dot(cot, second[t], 1, 0) * slope).astype(BF16)
-        d_n2 = d_n2 + dot(d_pre, first[t], 1, 1)
-        g_second.append(dot(cot, act, 0, 0).astype(BF16))
-        g_first.append(dot(n2, d_pre, 0, 0).astype(BF16))
-        g_first_bias.append(jnp.sum(d_pre.astype(F32), axis=0))
-    output = scatter_row(y.astype(BF16))
+    if paired:
+        y, d_n2, g_first, g_second, g_bf = feed(n2, cot, b_first.reshape(tp, 1, units), both_ff, tp)
+        g_bf = g_bf.reshape(-1)
+        y = h + b_second + y
+    else:
+        y = h + b_second
+        d_n2 = jnp.zeros_like(h)
+        g_first, g_second, g_first_bias = [], [], []
+        for t in range(tp):
+            pre = dot(n2, first[t], 1, 0) + b_first[t * units : (t + 1) * units]
+            value, slope = gelu_pair(pre)
+            act = value.astype(BF16)
+            y = y + dot(act, second[t], 1, 1)
+            d_pre = (dot(cot, second[t], 1, 0) * slope).astype(BF16)
+            d_n2 = d_n2 + dot(d_pre, first[t], 1, 1)
+            g_second.append(dot(cot, act, 0, 0).astype(BF16))
+            g_first.append(dot(n2, d_pre, 0, 0).astype(BF16))
+            g_first_bias.append(jnp.sum(d_pre.astype(F32), axis=0))
+        g_bf = jnp.concatenate(g_first_bias)
+    output = y.astype(BF16)
+    if paired:
+        output = output.reshape(rows, span, width)
+        output = scatter_row([lax.dynamic_index_in_dim(output, (place - k) % rows, 0, False) for k in range(rows)])
+    else:
+        output = scatter_row([output[k * span : (k + 1) * span] for k in range(rows)])
     cot32 = cot.astype(F32)
     g_g2 = jnp.sum(d_n2 * scaled2, axis=0)
     g_c2 = jnp.sum(d_n2, axis=0)
@@ -653,17 +1064,13 @@
     g_g1 = jnp.sum(d_n1 * scaled1, axis=0)
     g_c1 = jnp.sum(d_n1, axis=0)
     grad_tokens = (d_h + norm_back(d_n1, scaled1, inverse1, ln1_gain)).astype(BF16)
-    small = [g_g1, g_c1, g_bq, g_bv, g_bo, g_g2, g_c2, jnp.concatenate(g_first_bias), g_bs]
+    small = [g_g1, g_c1, g_bq, g_bv, g_bo, g_g2, g_c2, g_bf, g_bs]
     vector = jnp.concatenate(small)
     vector = jnp.pad(vector, (0, -vector.shape[0] % 1024)).reshape(-1, 128)
     head_grads = [g.astype(BF16) for g in (g_query, g_key, g_value, g_out)]
-    if sizes["fsdp"] == 4 and ctx == 2 and group == 1 and bits_of(tp):
-        natural = jnp.zeros((rows, span, width), BF16)
-        for k in range(rows):
-            piece = grad_tokens[k * span : (k + 1) * span]
-            natural = lax.dynamic_update_index_in_dim(natural, piece, (place - k) % rows, 0)
-        (g_first, g_second), heads_out, vector, grad_tokens = closing(
-            [g_first, g_second], head_grads, vector, natural, tp
+    if paired:
+        _, heads_out, vector, grad_tokens = closing(
+            [], head_grads, vector, grad_tokens.reshape(rows, span, width), tp
         )
         g_query, g_key, g_value, g_out = heads_out
     else:
@@ -676,7 +1083,7 @@
             scatter_units([g[:, t * heads_dev : (t + 1) * heads_dev] for t in range(tp)], tp) for g in halved
         )
         vector = butterfly(vector, sizes)
-        grad_tokens = scatter_row(grad_tokens)
+        grad_tokens = scatter_row([grad_tokens[k * span : (k + 1) * span] for k in range(rows)])
     grad_tokens = grad_tokens.astype(F32)
     g_out, g_second = g_out.T, g_second.T
     vector = vector.reshape(-1)

time: 938 us -> 815 us (0.87)
  Pallas kernels: 293 us -> 554 us
  matrix products: 248 us -> 100 us
  local copies, waits for them, and re-layouts: 131 us -> 36.6 us
  starting transfers between devices: 94.5 us -> 20.5 us
  waiting for transfers between devices: 101 us -> 32.8 us
  other arithmetic: 37.7 us -> 57.5 us
  between operations: 14.8 us -> 1.54 us
    pallas_call x0 -> x2, Pallas kernels: none -> 358 us  [the longest x1 208 us: opening(): pl.pallas_call(functools.partial(opening_kernel, tp), out_shape=(jax.Shap...]
    dot_general x35 -> x11, matrix products: 248 us -> 100 us  [dot(): lax.dot_general(left, right, (((left_dim,), (right_dim,)), ((), ())), pre...]
    ppermute x6 -> x3, starting transfers between devices: 89.8 us -> 3.84 us  [gather_row(): piece = lax.ppermute(piece, 'tp', pairs)]
    pallas_call x1, Pallas kernels: 171 us -> 93.7 us  [closing(): pl.pallas_call(lambda *refs: closing_kernel(kinds, True, tp, refs), out_s...]
    all_gather x3 -> x0, waiting for transfers between devices: 46.2 us -> none  [the longest x1 46.2 us: shards(): lax.all_gather(w_second.T, both, axis=0, tiled=True)]
    ppermute x2 -> x1, waiting for transfers between devices: 37.4 us -> 0.01 us  [fetch(): lax.ppermute(value, 'ctx', [((c + c_step) % ctx, c) for c in range(ctx)])]
    convert_element_type x8 -> x0, local copies, waits for them, and re-layouts: 34.5 us -> none  [the longest x4 21.4 us: shards(): g_second.append(dot(cot, act, 0, 0).astype(BF16))]
    ppermute x3, waiting for transfers between devices: 0.01 us -> 32.8 us  [scatter_row(): piece = lax.ppermute(piece, 'tp', pairs)]
  transfers between devices with their start and end apart: 15 -> 8, of which waited for: 3 -> 1; matrix products, arithmetic and copies ran while one was open for 25% -> 10% of each run, Pallas kernels for 13% -> 5%
where the time goes in v3:
time: 815 us; the launch traced here: 803 us
  Pallas kernels  554 us (68%)
  matrix products  100 us (12%)
  other arithmetic  57.5 us (7%)
  local copies, waits for them, and re-layouts  36.6 us (4%)
  waiting for transfers between devices  32.8 us (4%)
  starting transfers between devices  20.5 us (3%)
    pallas_call x1, Pallas kernels, opening(): pl.pallas_call(functools.partial(opening_kernel, tp), out_shape=(jax.Shap...  208 us
    pallas_call x1, Pallas kernels, feed(): pl.pallas_call(functools.partial(feed_kernel, tp), out_shape=(jax.ShapeDt...  150 us
    dot_general x11, matrix products, dot(): lax.dot_general(left, right, (((left_dim,), (right_dim,)), ((), ())), pre...  100 us
    pallas_call x1, Pallas kernels, closing(): pl.pallas_call(lambda *refs: closing_kernel(kinds, True, tp, refs), out_s...  93.7 us
    pallas_call x1, Pallas kernels, attention_backward(): pl.pallas_call(functools.partial(backward_kernel, tokens // block, contex...  64.2 us
    pallas_call x1, Pallas kernels, attention_forward(): pl.pallas_call(functools.partial(forward_kernel, tokens // block, context...  38.6 us
    ppermute x3, waiting for transfers between devices, scatter_row(): piece = lax.ppermute(piece, 'tp', pairs)  32.8 us
  transfers between devices with their start and end apart: 8, of which 1 were waited for; matrix products, arithmetic and copies ran while one was open for 10% of the time, Pallas kernels for 5%

profile of v3, /device:TPU:0, one launch (start us, length us, event | category | flops | bytes accessed | tf_op | source)
XLA Modules:
  0.0 803.4 jit_solution(17370035666645593250)
XLA Ops:
  6.5 208.0 %opening.1 = (bf16[2,4,256,1152]{3,2,1,0:T(8,128)(2,1)}, bf16[4,1152,1152]{2,1,0:T(8,128)(2,1)}, bf16[2,4,4,288,1076]{4,3,2,1,0:T(8,128)(2,1)}) custom-call(bf16[4,256,1152]{2,1,0:T(8,128)(2,1)S(1)} %copy-done, bf16[288,1152]{1,0:T(8,128)(2,1)S(1)} %concatenate.17.shard, bf16[2,288,1076]{2,1,0:T(8,128)(2,1)S(1)} %pad_maximum_fusion.ff_in), custom_call_target="tpu_custom_call" | custom-call | tf_op jit(solution)/shard_map/opening/pallas_call | solution.py:425
  216.1 2.6 dynamic-slice_bitcast_fusion.3
  219.7 2.9 collective-permute-start.3
  226.2 3.0 convert_reduce_fusion.1
  229.3 3.9 multiply_reduce_fusion
  233.2 3.0 slice.95
  236.9 5.1 subtract_multiply_fusion
  242.0 7.9 multiply_convert_fusion.q_ref
  250.0 14.8 %add_convert_fusion.k_ref.v_ref = bf16[2304,2048]{1,0:T(8,128)(2,1)} fusion(bf16[2304,1152]{1,0:T(8,128)(2,1)S(1)} %bitcast.101, bf16[2048,1152]{1,0:T(8,128)(2,1)S(1)} %get-tuple-element.78, f32[2304]{0:T(1024)S(1)} %concatenate.20), kind=kOutput, calls=%fused_computation | convolution fusion | flops 10881073152 | bytes 19473408 | tf_op jit(solution)/shard_map/dot_general | solution.py:21
  265.4 6.6 convert_element_type.72
  278.4 38.6 %attention_forward.1 = (bf16[1152,1024]{1,0:T(8,128)(2,1)}, f32[16,1,1024]{2,1,0:T(1,128)}) custom-call(s32[4]{0:T(128)} %get-tuple-element.73.count, s32[32]{0:T(128)} %reshape.266.index, bf16[1152,1024]{1,0:T(8,128)(2,1)} %multiply_convert_fusion.q_ref, bf16[2304,2048]{1,0:T(8,128)(2,1)} %add_convert_fusion.k_ref.v_ref, ...), custom_call_target="tpu_custom_call" | custom-call | flops 28991029248 | bytes 14155776 | tf_op jit(solution)/shard_map/attention_forward/pallas_call | solution.py:115
  316.9 7.9 fusion.26
  325.7 2.2 add_convert_fusion.4.n2
  330.5 149.8 %feed.1 = (f32[1024,1152]{1,0:T(8,128)}, f32[1024,1152]{1,0:T(8,128)}, f32[144,1076]{1,0:T(8,128)}, f32[144,1076]{1,0:T(8,128)}, f32[4,1,1076]{2,1,0:T(1,128)}) custom-call(bf16[1024,1152]{1,0:T(8,128)(2,1)} %add_convert_fusion.4.n2, bf16[1024,1152]{1,0:T(8,128)(2,1)} %bitcast.15.cot, f32[4,1,1076]{2,1,0:T(1,128)} %reshape.269.bias, ...), custom_call_target="tpu_custom_call" | custom-call | flops 60926459904 | bytes 38707200 | tf_op jit(solution)/shard_map/feed/pallas_call | solution.py:601
  480.4 5.9 multiply_reduce_fusion.2
  486.9 5.2 convert_reduce_fusion.3
  492.1 8.2 %convolution_convert_fusion.4.do_ref = bf16[1152,1024]{1,0:T(8,128)(2,1)} fusion(bf16[4,1152,1152]{2,1,0:T(8,128)(2,1)} %get-tuple-element.40, f32[1024,1152]{1,0:T(8,128)S(1)} %get-tuple-element.72), kind=kOutput, calls=%fused_computation.31 | convolution fusion | flops 2720268288 | bytes 9732096 | tf_op jit(solution)/shard_map/dot_general | solution.py:21
  500.3 4.8 convolution_convert_fusion
  505.1 64.2 %attention_backward.1 = (bf16[1152,1024]{1,0:T(8,128)(2,1)}, bf16[1152,2048]{1,0:T(8,128)(2,1)}, bf16[1152,2048]{1,0:T(8,128)(2,1)}) custom-call(s32[4]{0:T(128)} %get-tuple-element.73.count, s32[32]{0:T(128)} %reshape.266.index, bf16[1152,1024]{1,0:T(8,128)(2,1)} %multiply_convert_fusion.q_ref, bf16[2304,2048]{1,0:T(8,128)(2,1)} %add_convert_fusion.k_ref.v_ref, ...), custom_call_target="tpu_custom_call" | custom-call | flops 48318382080 | bytes 28311552 | tf_op jit(solution)/shard_map/attention_backward/pallas_call | solution.py:141
  569.3 12.1 %fusion.2 = f32[2048,1152]{1,0:T(8,128)} fusion(bf16[1152,2048]{1,0:T(8,128)(2,1)} %get-tuple-element.48, bf16[4,1152,1152]{2,1,0:T(8,128)(2,1)} %get-tuple-element.40), kind=kOutput, calls=%fused_computation.33 | convolution fusion | flops 5435817984 | bytes 16809984 | tf_op jit(solution)/shard_map/dot_general | solution.py:21
  581.4 7.8 convolution_convert_fusion.3
  589.3 7.8 convolution_convert_fusion.2
  597.1 10.7 %convolution_add_fusion = f32[2048,1152]{1,0:T(8,128)S(1)} fusion(f32[2048,1152]{1,0:T(8,128)} %fusion.2, bf16[1152,2048]{1,0:T(8,128)(2,1)S(1)} %bitcast.103, bf16[4,1152,1152]{2,1,0:T(8,128)(2,1)} %get-tuple-element.40), kind=kOutput, calls=%fused_computation.4 | convolution fusion | flops 5438177280 | bytes 26247168 | tf_op jit(solution)/shard_map/dot_general | solution.py:21
  611.2 4.8 convolution_convert_fusion.1
  617.2 7.3 collective-permute-start.4
  624.9 6.2 collective-permute-start.5
  632.4 2.6 convert_reduce_fusion.2
  641.0 32.8 %collective-permute-done.5 = bf16[256,1152]{1,0:T(8,128)(2,1)} collective-permute-done((bf16[256,1152]{1,0:T(8,128)(2,1)S(1)}, bf16[256,1152]{1,0:T(8,128)(2,1)}, u32[]{:S(2)}, u32[]{:S(2)}) %collective-permute-start.5) | collective-permute-done | bytes 589856 | tf_op jit(solution)/shard_map/ppermute | solution.py:937
  675.1 13.3 %multiply_reduce_fusion.1 = (f32[1024]{0:T(1024)S(1)}, f32[1152]{0:T(1024)S(1)}, f32[1024]{0:T(1024)S(1)}, f32[1152]{0:T(1024)S(1)}, f32[1024,1152]{1,0:T(8,128)}) fusion(f32[2048,1152]{1,0:T(8,128)} %get-tuple-element.77, f32[1152]{0:T(1024)S(1)} %copy-done.19, bf16[1024,1152]{1,0:T(8,128)(2,1)} %collective-permute-done.7, ...), kind=kOutput, calls=%fused_computation.16 | convolution fusion | flops 2729701376 | bytes 21550592 | tf_op jit(solution)/shard_map/dot_general | solution.py:21
  689.2 7.4 add_convert_fusion.2
  696.6 93.7 %closing.1 = (f32[144,288]{1,0:T(8,128)}, f32[144,288]{1,0:T(8,128)}, f32[144,288]{1,0:T(8,128)}, f32[144,288]{1,0:T(8,128)}, f32[112,128]{1,0:T(8,128)}, /*inde...) custom-call(bf16[2,2,2,144,1152]{4,3,2,1,0:T(8,128)(2,1)} %bitcast.1, ...), custom_call_target="tpu_custom_call" | custom-call | tf_op jit(solution)/shard_map/closing/pallas_call | solution.py:876
  794.5 4.2 convert_element_type.94
  (150 shorter events, 46.5 us)
Async XLA Ops:
  218.7 109.2 %collective-permute-start.1 = (bf16[256,1152]{1,0:T(8,128)(2,1)S(1)}, bf16[256,1152]{1,0:T(8,128)(2,1)S(1)}, u32[]{:S(2)}, u32[]{:S(2)}) collective-permute-start(bf16[256,1152]{1,0:T(8,128)(2,1)S(1)} %get-tuple-element.86), channel_id=1, source_target_pairs={{0,1},{1,2},{2,3},{3,0},{4,5},{5,6},{6,7},{7,4},{8,9},{9,10},{10,1... | collective-permute-start | bytes 1769480 | tf_op jit(solution)/shard_map/ppermute | solution.py:927
  218.7 110.1 %collective-permute-start.2 = (bf16[256,1152]{1,0:T(8,128)(2,1)S(1)}, bf16[256,1152]{1,0:T(8,128)(2,1)S(1)}, u32[]{:S(2)}, u32[]{:S(2)}) collective-permute-start(bf16[256,1152]{1,0:T(8,128)(2,1)S(1)} %get-tuple-element.85), channel_id=1, source_target_pairs={{0,2},{1,3},{2,0},{3,1},{4,6},{5,7},{6,4},{7,5},{8,10},{9,11},{10,... | collective-permute-start | bytes 1769480 | tf_op jit(solution)/shard_map/ppermute | solution.py:927
  219.7 110.0 %collective-permute-start.3 = (bf16[256,1152]{1,0:T(8,128)(2,1)S(1)}, bf16[256,1152]{1,0:T(8,128)(2,1)S(1)}, u32[]{:S(2)}, u32[]{:S(2)}) collective-permute-start(bf16[256,1152]{1,0:T(8,128)(2,1)S(1)} %get-tuple-element.84), channel_id=1, source_target_pairs={{0,3},{1,0},{2,1},{3,2},{4,7},{5,4},{6,5},{7,6},{8,11},{9,8},{10,9... | collective-permute-start | bytes 1769480 | tf_op jit(solution)/shard_map/ppermute | solution.py:927
  224.4 48.9 %collective-permute-start = (s32[1024]{0:T(1024)S(1)}, s32[1024]{0:T(1024)}, u32[]{:S(2)}, u32[]{:S(2)}) collective-permute-start(s32[1024]{0:T(1024)S(1)} %bitcast.117), channel_id=1, source_target_pairs={{4,0},{0,4},{5,1},{1,5},{6,2},{2,6},{7,3},{3,7},{12,8},{8,12},{13,... | collective-permute-start | bytes 12296 | tf_op jit(solution)/shard_map/ppermute | solution.py:957
  233.1 38.8 %copy-start.17 = (f32[2048]{0:T(1024)}, f32[2048]{0:T(1024)S(1)}, u32[]{:S(2)}) copy-start(f32[2048]{0:T(1024)S(1)} %add_rsqrt_fusion) | copy-start | bytes 24580
  242.0 8.0 copy-start.5
  278.4 38.6 %copy-start.31 = (f32[1152]{0:T(1024)S(1)}, f32[1152]{0:T(1024)}, u32[]{:S(2)}) copy-start(f32[1152]{0:T(1024)} %param.28) | copy-start | bytes 13828
  492.1 8.2 %copy-start.4 = (f32[1024,1152]{1,0:T(8,128)}, f32[1024,1152]{1,0:T(8,128)S(1)}, u32[]{:S(2)}) copy-start(f32[1024,1152]{1,0:T(8,128)S(1)} %get-tuple-element.72) | copy-start | bytes 14155780
  492.1 8.2 %copy-start.32 = (bf16[1152,1024]{1,0:T(8,128)(2,1)S(1)}, bf16[1152,1024]{1,0:T(8,128)(2,1)}, u32[]{:S(2)}) copy-start(bf16[1152,1024]{1,0:T(8,128)(2,1)} %get-tuple-element.41.o_ref) | copy-start | bytes 7077892
  500.3 81.1 %slice-start.4 = ((s8[4718592]{0:T(1024)(128)(4,1)}), s8[4194304]{0:T(1024)(128)(4,1)S(1)}, s32[]{:S(2)}) async-start(s8[4718592]{0:T(1024)(128)(4,1)} %bitcast.104), calls=%async_computation.4 | async-start | bytes 8388608
  505.1 76.3 %slice-start.5 = ((s8[4718592]{0:T(1024)(128)(4,1)}), s8[524288]{0:T(1024)(128)(4,1)S(1)}, s32[]{:S(2)}) async-start(s8[4718592]{0:T(1024)(128)(4,1)} %bitcast.104), calls=%async_computation.5 | async-start | bytes 1048576
  569.3 12.1 %copy-start.33 = (bf16[1152,2048]{1,0:T(8,128)(2,1)S(1)}, bf16[1152,2048]{1,0:T(8,128)(2,1)}, u32[]{:S(2)}) copy-start(bf16[1152,2048]{1,0:T(8,128)(2,1)} %get-tuple-element.48) | copy-start | bytes 14155780
  569.3 20.0 %slice-start.2 = ((s8[4718592]{0:T(1024)(128)(4,1)}), s8[4194304]{0:T(1024)(128)(4,1)S(1)}, s32[]{:S(2)}) async-start(s8[4718592]{0:T(1024)(128)(4,1)} %bitcast.102), calls=%async_computation.2 | async-start | bytes 8388608
  607.8 8.2 %copy-start.10 = (f32[2048,1152]{1,0:T(8,128)}, f32[2048,1152]{1,0:T(8,128)S(1)}, u32[]{:S(2)}) copy-start(f32[2048,1152]{1,0:T(8,128)S(1)} %convolution_add_fusion) | copy-start | bytes 28311556
  609.5 65.5 %collective-permute-start.7 = (bf16[1024,1152]{1,0:T(8,128)(2,1)}, bf16[1024,1152]{1,0:T(8,128)(2,1)}, u32[]{:S(2)}, u32[]{:S(2)}) collective-permute-start(bf16[1024,1152]{1,0:T(8,128)(2,1)} %slice.172), channel_id=1, source_target_pairs={{0,4},{4,0},{1,5},{5,1},{2,6},{6,2},{3,7},{7,3},{8,12},{12,8},{9,1... | collective-permute-start | bytes 7077896 | tf_op jit(solution)/shard_map/ppermute | solution.py:966
  617.2 22.7 %collective-permute-start.4 = (bf16[256,1152]{1,0:T(8,128)(2,1)}, bf16[256,1152]{1,0:T(8,128)(2,1)}, u32[]{:S(2)}, u32[]{:S(2)}) collective-permute-start(bf16[256,1152]{1,0:T(8,128)(2,1)} %get-tuple-element.82), channel_id=1, source_target_pairs={{1,0},{2,1},{3,2},{0,3},{5,4},{6,5},{7,6},{4,7},{9,8},{10,9},{11,1... | collective-permute-start | bytes 1769480 | tf_op jit(solution)/shard_map/ppermute | solution.py:937
  624.9 50.2 %copy-start.19 = (f32[1152]{0:T(1024)S(1)}, f32[1152]{0:T(1024)}, u32[]{:S(2)}) copy-start(f32[1152]{0:T(1024)} %param.20) | copy-start | bytes 13828
  624.9 48.9 %collective-permute-start.5 = (bf16[256,1152]{1,0:T(8,128)(2,1)S(1)}, bf16[256,1152]{1,0:T(8,128)(2,1)}, u32[]{:S(2)}, u32[]{:S(2)}) collective-permute-start(bf16[256,1152]{1,0:T(8,128)(2,1)S(1)} %get-tuple-element.81), channel_id=1, source_target_pairs={{2,0},{3,1},{0,2},{1,3},{6,4},{7,5},{4,6},{5,7},{10,8},{11,9},{8,1... | collective-permute-start | bytes 1769480 | tf_op jit(solution)/shard_map/ppermute | solution.py:937
  637.8 37.1 %collective-permute-start.6 = (bf16[256,1152]{1,0:T(8,128)(2,1)S(1)}, bf16[256,1152]{1,0:T(8,128)(2,1)S(1)}, u32[]{:S(2)}, u32[]{:S(2)}) collective-permute-start(bf16[256,1152]{1,0:T(8,128)(2,1)S(1)} %get-tuple-element.80), channel_id=1, source_target_pairs={{3,0},{0,1},{1,2},{2,3},{7,4},{4,5},{5,6},{6,7},{11,8},{8,9},{9,10... | collective-permute-start | bytes 1769480 | tf_op jit(solution)/shard_map/ppermute | solution.py:937
  675.0 13.4 %copy-start.6 = (bf16[4,256,1152]{2,1,0:T(8,128)(2,1)}, bf16[4,256,1152]{2,1,0:T(8,128)(2,1)S(1)}, u32[]{:S(2)}) copy-start(bf16[4,256,1152]{2,1,0:T(8,128)(2,1)S(1)} %bitcast_dynamic-update-slice_fusion) | copy-start | bytes 7077892
  675.1 13.4 %copy-start.15 = (f32[4304]{0:T(1024)S(1)}, f32[4304]{0:T(1024)}, u32[]{:S(2)}) copy-start(f32[4304]{0:T(1024)} %reshape.276) | copy-start | bytes 51652
  675.1 13.4 %copy-start.20 = (f32[1152]{0:T(1024)S(1)}, f32[1152]{0:T(1024)}, u32[]{:S(2)}) copy-start(f32[1152]{0:T(1024)} %get-tuple-element.71) | copy-start | bytes 13828
  675.1 13.4 %copy-start.21 = (f32[1152]{0:T(1024)S(1)}, f32[1152]{0:T(1024)}, u32[]{:S(2)}) copy-start(f32[1152]{0:T(1024)} %convert_reduce_fusion) | copy-start | bytes 13828
  675.1 13.4 %copy-start.22 = (f32[1152]{0:T(1024)S(1)}, f32[1152]{0:T(1024)}, u32[]{:S(2)}) copy-start(f32[1152]{0:T(1024)} %convert_reduce_fusion.2) | copy-start | bytes 13828
  675.1 13.4 %copy-start.23 = (f32[1152]{0:T(1024)S(1)}, f32[1152]{0:T(1024)}, u32[]{:S(2)}) copy-start(f32[1152]{0:T(1024)} %get-tuple-element.61) | copy-start | bytes 13828
  675.1 13.3 %copy-start.24 = (f32[1152]{0:T(1024)S(1)}, f32[1152]{0:T(1024)}, u32[]{:S(2)}) copy-start(f32[1152]{0:T(1024)} %get-tuple-element.66) | copy-start | bytes 13828
  675.1 14.1 %slice-start.6 = ((f32[2048]{0:T(1024)}), f32[1024]{0:T(1024)S(1)}, s32[]{:S(2)}) async-start(f32[2048]{0:T(1024)} %copy-done.17), calls=%async_computation.6 | async-start | bytes 8192 | tf_op jit(solution)/shard_map/slice | solution.py:1063
  790.2 8.5 %copy-start.14 = (f32[144,288]{1,0:T(8,128)S(1)}, f32[144,288]{1,0:T(8,128)}, u32[]{:S(2)}) copy-start(f32[144,288]{1,0:T(8,128)} %get-tuple-element.121) | copy-start | bytes 497668
  790.2 9.2 %copy-start.13 = (f32[144,288]{1,0:T(8,128)S(1)}, f32[144,288]{1,0:T(8,128)}, u32[]{:S(2)}) copy-start(f32[144,288]{1,0:T(8,128)} %get-tuple-element.123) | copy-start | bytes 497668
  790.3 9.9 %copy-start.12 = (f32[144,288]{1,0:T(8,128)S(1)}, f32[144,288]{1,0:T(8,128)}, u32[]{:S(2)}) copy-start(f32[144,288]{1,0:T(8,128)} %get-tuple-element.124) | copy-start | bytes 497668
  790.3 10.5 %copy-start.11 = (f32[144,288]{1,0:T(8,128)S(1)}, f32[144,288]{1,0:T(8,128)}, u32[]{:S(2)}) copy-start(f32[144,288]{1,0:T(8,128)} %get-tuple-element.56) | copy-start | bytes 497668
  790.3 11.2 %copy-start.9 = (f32[144,1076]{1,0:T(8,128)S(1)}, f32[144,1076]{1,0:T(8,128)}, u32[]{:S(2)}) copy-start(f32[144,1076]{1,0:T(8,128)} %get-tuple-element.130) | copy-start | bytes 1859332
  (17 other events, 74.9 us)

commit v4 on v3

--- a/solution.py
+++ b/solution.py
@@ -331,29 +331,6 @@
                 wait(t)
                 then(t)
 
-    onward(z)
-    local = pltpu.make_async_copy(tokens.at[z], x_all.at[0, z], own.at[0])
-    local.start()
-    for k in range(1, tp):
-        token(z ^ k, z).start()
-    for m in range(2):
-        mine[m].wait()
-        ff_cross(m, z).start()
-        ff_beside(m, z, 0).start()
-    local.wait()
-    half(z).start()
-    for d in range(1, tp):
-        arrivals(d, lambda t: along(t, 0).wait_recv(), onward)
-        block = z ^ d
-        token(block, block).wait_recv()
-        half(block).start()
-        cross(z ^ (d - 1)).wait_recv()
-        beside(z ^ (d - 1), 1).start()
-        if d == 1:
-            ff_pass(z)
-    cross(z ^ (tp - 1)).wait_recv()
-    beside(z ^ (tp - 1), 1).start()
-
     depth = shard.shape[0]
     columns = shard.shape[1] // 4
 
@@ -376,25 +353,52 @@
         ff_half(t, 1).start()
         ff_beside(c, t, 1).start()
 
+    def handed(t):
+        for i in range(2):
+            ff_half(t, i).wait_recv()
+            ff_beside(1 - c, t, i).start()
+
+    def nothing(t):
+        return None
+
+    onward(z)
+    local = pltpu.make_async_copy(tokens.at[z], x_all.at[0, z], own.at[0])
+    local.start()
+    for m in range(2):
+        mine[m].wait()
+    ff_pass(z)
+    for m in range(2):
+        ff_cross(m, z).start()
+        ff_beside(m, z, 0).start()
+    local.wait()
+    half(z).start()
     for d in range(1, tp):
+        arrivals(d, lambda t: along(t, 0).wait_recv(), onward)
         arrivals(d, lambda t: ff_along(t, 0).wait_recv(), ff_onward)
+        if d > 1:
+            token(z ^ (d - 1), z).start()
+        cross(z ^ (d - 1)).wait_recv()
+        beside(z ^ (d - 1), 1).start()
         if d == 1:
             for m in range(2):
                 ff_cross(m, z).wait_recv()
                 ff_beside(m, z, 1).start()
         else:
-            arrivals(d - 1, lambda t: None, ff_second)
-        turn(z ^ (d - 1))
-    turn(z ^ (tp - 1))
-    arrivals(tp - 1, lambda t: None, ff_second)
-    for d in range(1, tp):
-
-        def handed(t):
-            for i in range(2):
-                ff_half(t, i).wait_recv()
-                ff_beside(1 - c, t, i).start()
-
-        arrivals(d, lambda t: None, handed)
+            arrivals(d - 1, nothing, ff_second)
+    token(z ^ (tp - 1), z).start()
+    turn(z)
+    cross(z ^ (tp - 1)).wait_recv()
+    beside(z ^ (tp - 1), 1).start()
+    arrivals(tp - 1, nothing, ff_second)
+    turn(z ^ 1)
+    arrivals(1, nothing, handed)
+    token(z ^ 1, z ^ 1).wait_recv()
+    half(z ^ 1).start()
+    for d in range(2, tp):
+        turn(z ^ d)
+        arrivals(d, nothing, handed)
+        token(z ^ d, z ^ d).wait_recv()
+        half(z ^ d).start()
 
     for k in range(tp):
         t = z ^ k
@@ -441,6 +445,12 @@
     )(tokens, shard, ff_in)
 
 
+def turn_rows(source, target, g, depth, core):
+    place = g // 2 + 2 * (core if g % 2 else 1 - core)
+    rows = pl.ds(pl.multiple_of(place * depth, 32), depth)
+    target[rows, :] = source[:, g * depth : (g + 1) * depth].astype(F32).T.astype(BF16)
+
+
 def feed_kernel(
     tp, n2, cot, bias, ff, y, dn2, g_first, g_second, g_bias,
     n2t, cott, weights, act, d_pre, near_part, recv1, recv2, recv3, recvz,
@@ -465,14 +475,9 @@
     for k in range(1, tp):
         pl.semaphore_signal(barrier, inc=1, device_id={"tp": z ^ k}, device_id_type=MESH)
 
-    @pl.loop(0, width // 128)
-    def _(i):
-        part = pl.ds(pl.multiple_of(i * 128, 128), 128)
-        n2t[part, :] = n2[:, part].astype(F32).T.astype(BF16)
-        cott[part, :] = cot[:, part].astype(F32).T.astype(BF16)
-
-    y[...] = jnp.zeros_like(y)
-    dn2[...] = jnp.zeros_like(dn2)
+    for g in range(4):
+        turn_rows(n2, n2t, g, depth, core)
+        turn_rows(cot, cott, g, depth, core)
     pl.semaphore_wait(barrier, 2 + tp)
 
     def remote(src, dst, send, recv, where):
@@ -526,7 +531,30 @@
             if order[i]:
                 last(j, m, order[i]).start()
 
-    rows_tile = 256
+    rows_tile = 512
+    sides = ((n2t, d_pre), (cott, act))
+
+    def sums(first_time, which):
+        @pl.loop(0, tokens // rows_tile)
+        def _(n):
+            r = pl.ds(pl.multiple_of(n * rows_tile, rows_tile), rows_tile)
+            for total, left, m in ((y, act, 1), (dn2, d_pre, 0)):
+                if m in which:
+                    part = dot(left[r, :], weights[m], 1, 1)
+                    total[r, :] = part if first_time else total[r, :] + part
+
+    def own_part(i):
+        for m, (left, right) in enumerate(sides):
+            j = 2 * i + m
+            first(j, m).wait_recv()
+
+            grad = dot(left[2 * depth :, :], right[...], 1, 0)
+            for n in range(4):
+                a, b = divmod(n, 2)
+                recv1[j, a, b] = (grad[n * half : (n + 1) * half] + recv1[j, a, b].astype(F32)).astype(BF16)
+
+            second(j, m).start()
+
     for i in range(tp):
         for copy in load(i):
             copy.wait()
@@ -541,42 +569,32 @@
             back = (dot(cot[r, :], weights[1], 1, 0) * slope).astype(BF16)
             d_pre[r, :] = back
             g_bias[t] += jnp.sum(back.astype(F32), axis=0, keepdims=True)
-            y[r, :] += dot(act[r, :], weights[1], 1, 1)
-            dn2[r, :] += dot(back, weights[0], 1, 1)
-
-        if i + 1 < tp:
-            for copy in load(i + 1):
-                copy.start()
-        if i:
-            stage2(i - 1)
-        sides = ((n2t, d_pre), (cott, act))
+
         for m, (left, right) in enumerate(sides):
             j = 2 * i + m
             if i:
                 first(j - 2, m).wait_send()
 
-            @pl.loop(0, 2)
-            def _(a):
-                rows = pl.ds(pl.multiple_of((2 * a + 1 - core) * depth, 32), depth)
-                grad = dot(left[rows, :], right[...], 1, 0).astype(BF16)
-                for b in range(2):
-                    near_part[m, a, b] = grad[b * half : (b + 1) * half]
+            grad = dot(left[: 2 * depth, :], right[...], 1, 0).astype(BF16)
+            for n in range(4):
+                near_part[m, n // 2, n % 2] = grad[n * half : (n + 1) * half]
 
             first(j, m).start()
         if i:
-            stage3(i - 1)
-        for m, (left, right) in enumerate(sides):
-            j = 2 * i + m
-            first(j, m).wait_recv()
-
-            @pl.loop(0, 2)
-            def _(a):
-                rows = pl.ds(pl.multiple_of((2 * a + core) * depth, 32), depth)
-                grad = dot(left[rows, :], right[...], 1, 0)
-                for b in range(2):
-                    recv1[j, a, b] = (grad[b * half : (b + 1) * half] + recv1[j, a, b].astype(F32)).astype(BF16)
-
-            second(j, m).start()
+            stage2(i - 1)
+        if i + 1 < tp:
+            sums(i == 0, (0, 1))
+            for copy in load(i + 1):
+                copy.start()
+            if i:
+                stage3(i - 1)
+            own_part(i)
+        else:
+            sums(i == 0, (1,))
+            if i:
+                stage3(i - 1)
+            own_part(i)
+            sums(i == 0, (0,))
     stage2(tp - 1)
     stage3(tp - 1)
     for m, out in enumerate((g_first, g_second)):
@@ -633,42 +651,37 @@
     )(n2, cot, bias, ff)
 
 
-def closing_kernel(kinds, moved, tp, refs):
-    jobs = len(kinds)
-    grads, (vec, gt) = refs[:jobs], refs[jobs : jobs + 2]
-    rest = list(refs[jobs + 2 :])
-
-    def take(n):
-        out = rest[:n]
-        del rest[:n]
-        return out
-
-    units = sorted({slot for part, slot in kinds if part is not None})
-    heads = sorted({slot for part, slot in kinds if part is None})
-    out_units, out_heads = take(len(units)), take(len(heads))
-    vec_out, gt_out = take(2)
-    arrived = take(jobs)
-    widths = [g.shape[-1] for g in grads]
-    pools = {w: take(2) for w in sorted(set(widths))}
-    slots = [widths[:j].count(widths[j]) % 2 for j in range(jobs)]
-    own = [pools[widths[j]][0].at[slots[j]] for j in range(jobs)]
-    come = [pools[widths[j]][1].at[slots[j]] for j in range(jobs)]
-    keep, send2, recv2, send3, recv3 = (take(jobs) for _ in range(5))
-    last_units, last_heads, piece_heads = take(len(units)), take(len(heads)), take(len(heads))
-    (vec_in,) = take(1)
-    s1, r1, s2, r2, s3, r3, l1, l2 = take(8)
-    s4, r4, sv, rv, sg, rg, lg = take(7)
-
+def closing_kernel(
+    tp, d_other, d_own, d_h, x_own, n1, d_att, gain, dqt, dkt, dvt, ot, vec,
+    g_q, g_k, g_v, g_o, vec_out, gt_out,
+    n1t, d_att_t, stage, come, block_a, block_b, block_x, gt, g_gain, g_bias, near_part, recv1, recv2, recv3, piece, recvz, vec_in,
+    sy, ry, lb, sg, rg, lg, ls, s1, r1, s2, r2, s3, r3, s4, r4, sv, rv
+):
     f, c, z = lax.axis_index("fsdp"), lax.axis_index("ctx"), lax.axis_index("tp")
     x, core = f // 2, f % 2
-    near, across = f + 1 - 2 * core, f + 2 - 4 * x
-    other_c = 1 - c
+    near, across, other_c = f + 1 - 2 * core, f + 2 - 4 * x, 1 - c
+    span, width = come.shape[1:]
+    tokens = tp * span
+    depth = width // 4
+    half = depth // 2
+    tile = 48
+    order = list(range(tp - 1, -1, -1))
+
+    def loads(i):
+        b, slot = z ^ order[i], i % 2
+        return [
+            pltpu.make_async_copy(source.at[b], target.at[slot], lb.at[n, slot])
+            for n, (source, target) in enumerate(((d_own, block_a), (d_h, block_b), (x_own, block_x)))
+        ]
+
+    for copy in loads(0):
+        copy.start()
 
     barrier = pltpu.get_barrier_semaphore()
     for where in ({"fsdp": near}, {"fsdp": across}, {"ctx": other_c}):
         pl.semaphore_signal(barrier, inc=1, device_id=where, device_id_type=MESH)
     for k in range(1, tp):
-        pl.semaphore_signal(barrier, inc=1, device_id={"tp": lax.rem(z + k, tp)}, device_id_type=MESH)
+        pl.semaphore_signal(barrier, inc=1, device_id={"tp": z ^ k}, device_id_type=MESH)
     pl.semaphore_wait(barrier, 2 + tp)
 
     def remote(src, dst, send, recv, where):
@@ -676,101 +689,144 @@
             src_ref=src, dst_ref=dst, send_sem=send, recv_sem=recv, device_id=where, device_id_type=MESH
         )
 
-    for k in range(tp if moved else 0):
-        @pl.when(z != k)
-        def _():
-            remote(gt.at[k], gt_out.at[z], sg.at[k], rg.at[z], {"tp": k}).start()
-
-        @pl.when(z == k)
-        def _():
-            pltpu.make_async_copy(gt.at[k], gt_out.at[z], lg).start()
-
-    first = [remote(grads[j].at[:, 1 - core], arrived[j], s1.at[j], r1.at[j], {"fsdp": near}) for j in range(jobs)]
-    mine = [pltpu.make_async_copy(grads[j].at[:, core], own[j], l1.at[j]) for j in range(jobs)]
-    theirs = [pltpu.make_async_copy(arrived[j], come[j], l2.at[j]) for j in range(jobs)]
-    for copy in first:
-        copy.start()
-
-    def turn(j):
-        return j % 2 == 0
-
-    second, third = [], []
-    for j in range(jobs):
-        where2 = {"fsdp": across} if turn(j) else {"ctx": other_c}
-        where3 = {"ctx": other_c} if turn(j) else {"fsdp": across}
-        second.append(remote(send2[j], recv2[j], s2.at[j], r2.at[j], where2))
-        third.append(remote(send3[j], recv3[j], s3.at[j], r3.at[j], where3))
-
-    def rows_loop(rows, body):
-        tile = 48
-
-        @pl.loop(0, rows // tile)
-        def _(i):
-            body(pl.ds(pl.multiple_of(i * tile, 16), tile))
-
-    def stage1(j):
-        mine[j].wait()
-        theirs[j].wait()
-        rows = send3[j].shape[0]
-        for i in range(2):
-
-            def body(r, i=i):
-                if turn(j):
-                    out_at, in_at = (1 - x, i), (x, i)
-                else:
-                    out_at, in_at = (i, 1 - c), (i, c)
-                send2[j][i, r] = (own[j][out_at[0], out_at[1], r].astype(F32) + come[j][out_at[0], out_at[1], r].astype(F32)).astype(BF16)
-                keep[j][i, r] = (own[j][in_at[0], in_at[1], r].astype(F32) + come[j][in_at[0], in_at[1], r].astype(F32)).astype(BF16)
-
-            rows_loop(rows, body)
-        second[j].start()
+    def over(k):
+        return remote(d_other.at[z ^ k], come.at[z ^ k], sy.at[k], ry.at[k], {"ctx": other_c})
+
+    for k in order:
+        over(k).start()
+
+    def first(j):
+        return remote(near_part.at[j], recv1.at[j], s1.at[j], r1.at[j], {"fsdp": near})
+
+    def second(j):
+        return remote(recv1.at[j, 1 - x], recv2.at[j], s2.at[j], r2.at[j], {"fsdp": across})
+
+    def third(j):
+        return remote(recv2.at[j, 1 - c], recv3.at[j], s3.at[j], r3.at[j], {"ctx": other_c})
+
+    def last(j, k):
+        return remote(piece.at[j, z ^ k], recvz.at[j, k - 1], s4.at[j, k - 1], r4.at[j, k - 1], {"tp": z ^ k})
+
+    def move(k):
+        return remote(gt.at[z ^ k], gt_out.at[z], sg.at[k], rg.at[k], {"tp": z ^ k})
+
+    jobs = ((d_att_t, ot, tokens), (n1t, dkt, 2 * tokens), (n1t, dvt, 2 * tokens), (n1t, dqt, tokens))
+
+    def near_side(j):
+        left, right, length = jobs[j]
+        grad = dot(left[: 2 * depth, :length], right[...], 1, 1).astype(BF16)
+        for n in range(4):
+            near_part[j, n // 2, n % 2] = grad[n * half : (n + 1) * half]
+        first(j).start()
+
+    def own_side(j):
+        left, right, length = jobs[j]
+        grad = dot(left[2 * depth :, :length], right[...], 1, 1)
+        first(j).wait_recv()
+        for n in range(4):
+            a, b = divmod(n, 2)
+            recv1[j, a, b] = (grad[n * half : (n + 1) * half] + recv1[j, a, b].astype(F32)).astype(BF16)
+        second(j).start()
+
+    def fetch(source, n, slot):
+        rows = pl.ds(pl.multiple_of(n * span, span), span)
+        return pltpu.make_async_copy(source.at[rows], stage.at[slot], ls.at[slot])
+
+    def turned(source, target, blocks):
+        fetch(source, 0, 0).start()
+
+        @pl.loop(0, blocks)
+        def _(n):
+            slot = lax.rem(n, 2)
+
+            @pl.when(n + 1 < blocks)
+            def _():
+                fetch(source, n + 1, 1 - slot).start()
+
+            fetch(source, n, slot).wait()
+            cols = pl.ds(pl.multiple_of(n * span, span), span)
+            for g in range(4):
+                place = g // 2 + 2 * (core if g % 2 else 1 - core)
+                rows = pl.ds(pl.multiple_of(place * depth, 32), depth)
+                part = stage[slot, :, g * depth : (g + 1) * depth]
+                target[rows, cols] = part.astype(F32).T.astype(BF16)
 
     def stage2(j):
-        second[j].wait()
-        at = c if turn(j) else x
-
-        def body(r):
-            send3[j][r] = (keep[j][1 - at, r].astype(F32) + recv2[j][1 - at, r].astype(F32)).astype(BF16)
-            keep[j][at, r] = (keep[j][at, r].astype(F32) + recv2[j][at, r].astype(F32)).astype(BF16)
-
-        rows_loop(send3[j].shape[0], body)
-        third[j].start()
+        second(j).wait()
+
+        @pl.loop(0, half // tile)
+        def _(n):
+            r = pl.ds(pl.multiple_of(n * tile, 16), tile)
+            for a in range(2):
+                recv2[j, a, r] = (recv1[j, x, a, r].astype(F32) + recv2[j, a, r].astype(F32)).astype(BF16)
+
+        third(j).start()
 
     def stage3(j):
-        third[j].wait()
-        at = c if turn(j) else x
-        part, slot = kinds[j]
-        if part is None:
-            width = piece_heads[slot].shape[-1]
-
-            def body(r):
-                total = keep[j][at, r].astype(F32) + recv3[j][r].astype(F32)
-                for t in range(tp):
-                    piece_heads[slot][t, r] = total[:, t * width : (t + 1) * width].astype(BF16)
-
-            rows_loop(send3[j].shape[0], body)
+        third(j).wait()
+        columns = width // tp
+
+        @pl.loop(0, half // tile)
+        def _(n):
+            r = pl.ds(pl.multiple_of(n * tile, 16), tile)
+            total = recv2[j, c, r].astype(F32) + recv3[j, r].astype(F32)
             for t in range(tp):
-                @pl.when(z != t)
-                def _():
-                    remote(piece_heads[slot].at[t], last_heads[slot].at[z], s4.at[j, t], r4.at[len(units) + slot, z], {"tp": t}).start()
-        else:
-
-            def body(r):
-                send3[j][r] = (keep[j][at, r].astype(F32) + recv3[j][r].astype(F32)).astype(BF16)
-
-            rows_loop(send3[j].shape[0], body)
-
-            @pl.when(z != part)
-            def _():
-                remote(send3[j], last_units[slot].at[z], s4.at[j, part], r4.at[slot, z], {"tp": part}).start()
-
-    flips = [{"fsdp": near}, {"fsdp": across}, {"ctx": other_c}]
-    bit = 1
-    while bit < tp:
-        flips.append({"tp": z + bit - 2 * bit * lax.rem(lax.div(z, bit), 2)})
-        bit *= 2
+                piece[j, t, r] = total[:, t * columns : (t + 1) * columns].astype(BF16)
+
+        for k in range(1, tp):
+            last(j, k).start()
+
+    g_gain[...] = jnp.zeros_like(g_gain)
+    g_bias[...] = jnp.zeros_like(g_bias)
+
+    def token_block(i):
+        k = order[i]
+        b, slot = z ^ k, i % 2
+        if i + 1 < tp:
+            for copy in loads(i + 1):
+                copy.start()
+        for copy in loads(i):
+            copy.wait()
+        over(k).wait()
+        lines = 32
+
+        @pl.loop(0, span // lines)
+        def _(n):
+            r = pl.ds(pl.multiple_of(n * lines, lines), lines)
+            scaled, inverse = norm_stats(block_x[slot, r].astype(F32))
+            d_n1 = block_a[slot, r] + come[b, r].astype(F32)
+            g_gain[...] += jnp.sum(d_n1 * scaled, axis=0, keepdims=True)
+            g_bias[...] += jnp.sum(d_n1, axis=0, keepdims=True)
+            gt[b, r] = (block_b[slot, r] + norm_back(d_n1, scaled, inverse, gain[...])).astype(BF16)
+
+        if k:
+            move(k).start()
+
+    turned(d_att, d_att_t, tp)
+    near_side(0)
+    own_side(0)
+    turned(n1, n1t, 2 * tp)
+    near_side(1)
+    token_block(0)
+    own_side(1)
+    near_side(2)
+    token_block(1)
+    near_side(3)
+    own_side(2)
+    stage2(0)
+    own_side(3)
+    for i in range(2, tp):
+        token_block(i)
+    local = pltpu.make_async_copy(gt.at[z], gt_out.at[z], lg)
+    local.start()
+
+    flips = [{"fsdp": near}, {"fsdp": across}, {"ctx": other_c}] + [{"tp": z ^ (1 << i)} for i in range(bits_of(tp))]
     swaps = [remote(vec_out, vec_in.at[i], sv.at[i], rv.at[i], where) for i, where in enumerate(flips)]
     vec_out[...] = vec[...]
+    lanes = width // 128
+    for n, part in enumerate((g_gain, g_bias)):
+        for i in range(lanes):
+            vec_out[n * lanes + i : n * lanes + i + 1, :] = part[:, i * 128 : (i + 1) * 128]
     swaps[0].start()
 
     def small(i):
@@ -779,111 +835,76 @@
         if i + 1 < len(swaps):
             swaps[i + 1].start()
 
-    mine[0].start()
-    first[0].wait()
-    theirs[0].start()
-    lag = 2
-    for step in range(jobs + 2 * lag):
-        if step + 1 < jobs:
-            mine[step + 1].start()
-            first[step + 1].wait()
-            theirs[step + 1].start()
-        if step < jobs:
-            stage1(step)
-        if 0 <= step - lag < jobs:
-            stage2(step - lag)
-        if 0 <= step - 2 * lag < jobs:
-            stage3(step - 2 * lag)
-        if step % 2 == 0 and step // 2 < len(swaps):
-            small(step // 2)
-    for i in range((jobs + 2 * lag + 1) // 2, len(swaps)):
+    small(0)
+    stage2(1)
+    stage3(0)
+    small(1)
+    stage2(2)
+    stage3(1)
+    small(2)
+    stage2(3)
+    stage3(2)
+    stage3(3)
+    for i in range(3, len(swaps)):
         small(i)
-
-    for j, (part, slot) in enumerate(kinds):
-        for t in range(tp):
-            if part is None:
-                @pl.when(z != t)
-                def _():
-                    remote(piece_heads[slot].at[t], last_heads[slot].at[z], s4.at[j, t], r4.at[len(units) + slot, z], {"tp": t}).wait_send()
-                    remote(piece_heads[slot].at[t], last_heads[slot].at[t], s4.at[j, t], r4.at[len(units) + slot, t], {"tp": t}).wait_recv()
-            elif t == part:
-                @pl.when(z != t)
-                def _():
-                    remote(send3[j], last_units[slot].at[z], s4.at[j, t], r4.at[slot, z], {"tp": t}).wait_send()
-
-                @pl.when(z == t)
-                def _():
-                    for other in range(tp):
-                        if other != t:
-                            remote(send3[j], last_units[slot].at[other], s4.at[j, t], r4.at[slot, other], {"tp": t}).wait_recv()
-                    last_units[slot][t] = send3[j][...]
-    for slot in heads:
-        last_heads[slot][z] = piece_heads[slot][z]
-    for slots, last, out in ((units, last_units, out_units), (heads, last_heads, out_heads)):
-        for slot in slots:
-
-            def body(r, last=last, out=out, slot=slot):
-                total = last[slot][0, r].astype(F32)
-                for t in range(1, tp):
-                    total = total + last[slot][t, r].astype(F32)
-                out[slot][r] = total
-
-            rows_loop(out[slot].shape[0], body)
-    for k in range(tp if moved else 0):
-        @pl.when(z != k)
-        def _():
-            remote(gt.at[k], gt_out.at[z], sg.at[k], rg.at[z], {"tp": k}).wait_send()
-            remote(gt.at[k], gt_out.at[k], sg.at[k], rg.at[k], {"tp": k}).wait_recv()
-
-        @pl.when(z == k)
-        def _():
-            pltpu.make_async_copy(gt.at[k], gt_out.at[z], lg).wait()
-
-
-def closing(unit_grads, head_grads, vector, token_grads, tp):
-    kinds, operands = [], []
-    for t in range(tp if unit_grads else 0):
-        for slot, parts in enumerate(unit_grads):
-            kinds.append((t, slot))
-            operands.append(parts[t])
-    for slot, grad in enumerate(head_grads):
-        kinds.append((None, slot))
-        operands.append(grad)
-    operands = [g.reshape((2, 2, 2, g.shape[0] // 8, g.shape[1])) for g in operands]
-    rows = operands[0].shape[3]
-    jobs = len(kinds)
+    for j, out in enumerate((g_o, g_k, g_v, g_q)):
+        first(j).wait_send()
+        for k in range(1, tp):
+            last(j, k).wait()
+
+        @pl.loop(0, half // tile)
+        def _(n):
+            r = pl.ds(pl.multiple_of(n * tile, 16), tile)
+            total = piece[j, z, r].astype(F32)
+            for k in range(1, tp):
+                total = total + recvz[j, k - 1, r].astype(F32)
+            out[r] = total
+
+    local.wait()
+    for k in range(1, tp):
+        move(k).wait()
+
+
+def closing(d_other, d_own, d_h, x_own, n1, d_att, gain, dqt, dkt, dvt, ot, vector, tp):
+    context, width = n1.shape
+    tokens = context // 2
+    span = tokens // tp
+    half, columns = width // 8, width // tp
     vmem, hbm = pl.BlockSpec(memory_space=pltpu.VMEM), pl.BlockSpec(memory_space=pl.ANY)
-    heads_w = head_grads[0].shape[1] // tp
-    units_w = unit_grads[0][0].shape[1] if unit_grads else 0
-    out_shape = (
-        [jax.ShapeDtypeStruct((rows, units_w), F32)] * len(unit_grads)
-        + [jax.ShapeDtypeStruct((rows, heads_w), F32)] * len(head_grads)
-        + [jax.ShapeDtypeStruct(vector.shape, F32), jax.ShapeDtypeStruct(token_grads.shape, token_grads.dtype)]
-        + [jax.ShapeDtypeStruct((2, 2, rows, g.shape[-1]), BF16) for g in operands]
-    )
-    out_specs = [vmem] * (len(unit_grads) + len(head_grads) + 1) + [hbm] * (1 + jobs)
-    widths = [g.shape[-1] for g in operands]
-    scratch = [pltpu.VMEM((2, 2, 2, rows, w), BF16) for w in sorted(set(widths)) for _ in range(2)]
-    scratch += [pltpu.VMEM((2, rows, w), BF16) for w in widths] * 3
-    scratch += [pltpu.VMEM((rows, w), BF16) for w in widths] * 2
-    scratch += [pltpu.VMEM((tp, rows, units_w), BF16)] * len(unit_grads)
-    scratch += [pltpu.VMEM((tp, rows, heads_w), BF16)] * (2 * len(head_grads))
+    dma = pltpu.SemaphoreType.DMA
     swaps = 3 + bits_of(tp)
-    scratch += [pltpu.VMEM((swaps,) + vector.shape, F32)]
-    scratch += [pltpu.SemaphoreType.DMA((jobs,))] * 8
-    scratch += [pltpu.SemaphoreType.DMA((jobs, tp)), pltpu.SemaphoreType.DMA((len(unit_grads) + len(head_grads), tp))]
-    scratch += [pltpu.SemaphoreType.DMA((swaps,))] * 2 + [pltpu.SemaphoreType.DMA((tp,))] * 2 + [pltpu.SemaphoreType.DMA]
-    outs = pl.pallas_call(
-        lambda *refs: closing_kernel(kinds, True, tp, refs),
-        out_shape=out_shape,
-        in_specs=[hbm] * jobs + [vmem, hbm],
-        out_specs=out_specs,
-        scratch_shapes=scratch,
-        compiler_params=pltpu.CompilerParams(collective_id=1, has_side_effects=True, vmem_limit_bytes=62 << 20),
+    blocks = [a.reshape(tp, span, width) for a in (d_other, d_own, d_h, x_own)]
+    return pl.pallas_call(
+        functools.partial(closing_kernel, tp),
+        out_shape=[jax.ShapeDtypeStruct((half, columns), F32)] * 4
+        + [jax.ShapeDtypeStruct(vector.shape, F32), jax.ShapeDtypeStruct((tp, span, width), BF16)],
+        in_specs=[hbm] * 6 + [vmem] * 6,
+        out_specs=[vmem] * 5 + [hbm],
+        scratch_shapes=[
+            pltpu.VMEM((width, context), BF16),
+            pltpu.VMEM((width, tokens), BF16),
+            pltpu.VMEM((2, span, width), BF16),
+            pltpu.VMEM((tp, span, width), BF16),
+            pltpu.VMEM((2, span, width), F32),
+            pltpu.VMEM((2, span, width), F32),
+            pltpu.VMEM((2, span, width), BF16),
+            pltpu.VMEM((tp, span, width), BF16),
+            pltpu.VMEM((1, width), F32),
+            pltpu.VMEM((1, width), F32),
+            pltpu.VMEM((4, 2, 2, half, width), BF16),
+            pltpu.VMEM((4, 2, 2, half, width), BF16),
+            pltpu.VMEM((4, 2, half, width), BF16),
+            pltpu.VMEM((4, half, width), BF16),
+            pltpu.VMEM((4, tp, half, columns), BF16),
+            pltpu.VMEM((4, tp - 1, half, columns), BF16),
+            pltpu.VMEM((swaps,) + vector.shape, F32),
+            dma((tp,)), dma((tp,)), dma((3, 2)), dma((tp,)), dma((tp,)), dma, dma((2,)),
+            dma((4,)), dma((4,)), dma((4,)), dma((4,)), dma((4,)), dma((4,)),
+            dma((4, tp - 1)), dma((4, tp - 1)), dma((swaps,)), dma((swaps,)),
+        ],
+        compiler_params=pltpu.CompilerParams(collective_id=1, has_side_effects=True, vmem_limit_bytes=63 << 20),
         name="closing",
-    )(*operands, vector, token_grads)
-    n_u, n_h = len(unit_grads), len(head_grads)
-    return outs[:n_u], outs[n_u : n_u + n_h], outs[n_u + n_h], outs[n_u + n_h + 1]
+    )(*blocks, n1, d_att, gain, dqt, dkt, dvt, ot, vector)
 
 
 def shards(
@@ -969,12 +990,15 @@
     steps = group * ctx
 
     heads_dev, units = w_query.shape[1], w_first.shape[1]
+    padding = -units % 128
     both = ("tp", "fsdp")
     shard = jnp.concatenate([w_query, w_key, w_value, w_output.T], axis=1)
     paired = sizes["fsdp"] == 4 and ctx == 2 and group == 1 and bits_of(tp)
     if paired:
-        x_all16, qkvo, both_ff = opening(tokens, shard, jnp.stack([w_first, w_second.T]), tp)
-        both_ff = both_ff.reshape(2, tp, width, units)
+        x_all16, qkvo, both_ff = opening(
+            tokens, shard, jnp.pad(jnp.stack([w_first, w_second.T]), ((0, 0), (0, 0), (0, padding))), tp
+        )
+        both_ff = both_ff.reshape(2, tp, width, units + padding)
         x_all16 = x_all16.reshape(2 * rows * span, width)
     else:
         first = lax.all_gather(w_first, both, axis=0, tiled=True).reshape(tp, width, units)
@@ -1015,8 +1039,11 @@
     scaled2, inverse2 = norm_stats(h)
     n2 = (scaled2 * ln2_gain + ln2_bias).astype(BF16)
     if paired:
-        y, d_n2, g_first, g_second, g_bf = feed(n2, cot, b_first.reshape(tp, 1, units), both_ff, tp)
-        g_bf = g_bf.reshape(-1)
+        y, d_n2, g_first, g_second, g_bf = feed(
+            n2, cot, jnp.pad(b_first.reshape(tp, 1, units), ((0, 0), (0, 0), (0, padding))), both_ff, tp
+        )
+        g_first, g_second = g_first[:, :units], g_second[:, :units]
+        g_bf = g_bf[:, :, :units].reshape(-1)
         y = h + b_second + y
     else:
         y = h + b_second
@@ -1049,45 +1076,46 @@
     g_bo = jnp.sum(d_att.astype(F32), axis=0)
     d_ot = dot(wo, d_att, 1, 1).astype(BF16)
     dqt, dkt, dvt = attention_backward(blocks, index, qt, kvt, d_ot, ot, lse, qm, km, block)
-    d_all = dot(dkt, wkv[: tp * heads_dev], 0, 0) + dot(dvt, wkv[tp * heads_dev :], 0, 0)
-    d_n1 = d_all[:count] + dot(dqt, wq, 0, 0)
-    for i in range(1, steps):
-        d_n1 = d_n1 + give(d_all[i * count : (i + 1) * count].astype(BF16), i).astype(F32)
-    g_query = dot(n1[:count], dqt, 0, 1)
-    g_key = dot(n1, dkt, 0, 1)
-    g_value = dot(n1, dvt, 0, 1)
-    g_out = dot(d_att, ot, 0, 1)
+    wk, wv = wkv[: tp * heads_dev], wkv[tp * heads_dev :]
     g_bq = jnp.sum(dqt.astype(F32), axis=1)
     g_bv = jnp.sum(dvt.astype(F32), axis=1)
-
     scaled1, inverse1 = scaled_all[:count], inverse_all[:count]
-    g_g1 = jnp.sum(d_n1 * scaled1, axis=0)
-    g_c1 = jnp.sum(d_n1, axis=0)
-    grad_tokens = (d_h + norm_back(d_n1, scaled1, inverse1, ln1_gain)).astype(BF16)
-    small = [g_g1, g_c1, g_bq, g_bv, g_bo, g_g2, g_c2, g_bf, g_bs]
-    vector = jnp.concatenate(small)
-    vector = jnp.pad(vector, (0, -vector.shape[0] % 1024)).reshape(-1, 128)
-    head_grads = [g.astype(BF16) for g in (g_query, g_key, g_value, g_out)]
+
+    def pack(parts):
+        vector = jnp.concatenate(parts)
+        return jnp.pad(vector, (0, -vector.shape[0] % 1024)).reshape(-1, 128)
+
+    small = [g_bq, g_bv, g_bo, g_g2, g_c2, g_bf, g_bs]
     if paired:
-        _, heads_out, vector, grad_tokens = closing(
-            [], head_grads, vector, grad_tokens.reshape(rows, span, width), tp
+        d_other = (dot(dkt[:, count:], wk, 0, 0) + dot(dvt[:, count:], wv, 0, 0)).astype(BF16)
+        d_own = dot(dkt[:, :count], wk, 0, 0) + dot(dvt[:, :count], wv, 0, 0) + dot(dqt, wq, 0, 0)
+        free = [jnp.zeros((2 * width,), F32)]
+        g_query, g_key, g_value, g_out, vector, grad_tokens = closing(
+            d_other, d_own, d_h, x_all16[:count], n1, d_att, ln1_gain[None, :], dqt, dkt, dvt, ot,
+            pack(free + small), tp,
         )
-        g_query, g_key, g_value, g_out = heads_out
     else:
+        d_all = dot(dkt, wk, 0, 0) + dot(dvt, wv, 0, 0)
+        d_n1 = d_all[:count] + dot(dqt, wq, 0, 0)
+        for i in range(1, steps):
+            d_n1 = d_n1 + give(d_all[i * count : (i + 1) * count].astype(BF16), i).astype(F32)
+        head_grads = [dot(n1[:count], dqt, 0, 1), dot(n1, dkt, 0, 1), dot(n1, dvt, 0, 1), dot(d_att, ot, 0, 1)]
         g_first, g_second = (
             scatter_units([halve(g, sizes, i % 2 == 0) for g in parts], tp)
             for i, parts in enumerate((g_first, g_second))
         )
-        halved = [halve(g, sizes, i % 2 == 0) for i, g in enumerate(head_grads)]
+        halved = [halve(g.astype(BF16), sizes, i % 2 == 0) for i, g in enumerate(head_grads)]
         g_query, g_key, g_value, g_out = (
             scatter_units([g[:, t * heads_dev : (t + 1) * heads_dev] for t in range(tp)], tp) for g in halved
         )
-        vector = butterfly(vector, sizes)
+        vector = butterfly(pack([jnp.sum(d_n1 * scaled1, axis=0), jnp.sum(d_n1, axis=0)] + small), sizes)
+        grad_tokens = (d_h + norm_back(d_n1, scaled1, inverse1, ln1_gain)).astype(BF16)
         grad_tokens = scatter_row([grad_tokens[k * span : (k + 1) * span] for k in range(rows)])
     grad_tokens = grad_tokens.astype(F32)
     g_out, g_second = g_out.T, g_second.T
     vector = vector.reshape(-1)
-    ends = [sum(p.shape[0] for p in small[:i]) for i in range(len(small) + 1)]
+    lengths = [width, width] + [p.shape[0] for p in small]
+    ends = [sum(lengths[:i]) for i in range(len(lengths) + 1)]
     g_g1, g_c1, g_bq, g_bv, g_bo, g_g2, g_c2, g_bf, g_bs = (vector[i:j] for i, j in zip(ends, ends[1:]))
     return (
         output, grad_tokens, g_g1, g_c1, g_query, g_bq, g_key, g_value, g_bv, g_out, g_bo,

time: 815 us -> 767 us (0.941)
  matrix products: 100 us -> 75.9 us
  waiting for transfers between devices: 32.8 us -> 14.9 us
  starting transfers between devices: 20.5 us -> 5.59 us
  Pallas kernels: 554 us -> 568 us
  other arithmetic: 57.5 us -> 47.1 us
    pallas_call x1, Pallas kernels: 93.7 us -> 124 us  [closing(): pl.pallas_call(functools.partial(closing_kernel, tp), out_shape=[jax.Shap...]
    dot_general x11 -> x9, matrix products: 100 us -> 75.9 us  [dot(): lax.dot_general(left, right, (((left_dim,), (right_dim,)), ((), ())), pre...]
    pallas_call x1, Pallas kernels: 150 us -> 128 us  [feed(): pl.pallas_call(functools.partial(feed_kernel, tp), out_shape=(jax.ShapeDt...]
    ppermute x3, waiting for transfers between devices: 32.8 us -> 14.9 us  [scatter_row(): piece = lax.ppermute(piece, 'tp', pairs)]
    ppermute x3, starting transfers between devices: 15.6 us -> 1.19 us  [scatter_row(): piece = lax.ppermute(piece, 'tp', pairs)]
    pallas_call x1, Pallas kernels: 208 us -> 194 us  [opening(): pl.pallas_call(functools.partial(opening_kernel, tp), out_shape=(jax.Shap...]
    pallas_call x1, Pallas kernels: 64.2 us -> 76.2 us  [attention_backward(): pl.pallas_call(functools.partial(backward_kernel, tokens // block, contex...]
  transfers between devices with their start and end apart: 8 -> 7, of which waited for: 1 -> 1; matrix products, arithmetic and copies ran while one was open for 10% -> 12% of each run, Pallas kernels for 5% -> 23%
where the time goes in v4:
time: 767 us; the launch traced here: 754 us
  Pallas kernels  568 us (74%)
  matrix products  75.9 us (10%)
  other arithmetic  47.1 us (6%)
  local copies, waits for them, and re-layouts  40.6 us (5%)
  waiting for transfers between devices  14.9 us (2%)
    pallas_call x1, Pallas kernels, opening(): pl.pallas_call(functools.partial(opening_kernel, tp), out_shape=(jax.Shap...  194 us
    pallas_call x1, Pallas kernels, feed(): pl.pallas_call(functools.partial(feed_kernel, tp), out_shape=(jax.ShapeDt...  128 us
    pallas_call x1, Pallas kernels, closing(): pl.pallas_call(functools.partial(closing_kernel, tp), out_shape=[jax.Shap...  124 us
    pallas_call x1, Pallas kernels, attention_backward(): pl.pallas_call(functools.partial(backward_kernel, tokens // block, contex...  76.2 us
    dot_general x9, matrix products, dot(): lax.dot_general(left, right, (((left_dim,), (right_dim,)), ((), ())), pre...  75.9 us
    pallas_call x1, Pallas kernels, attention_forward(): pl.pallas_call(functools.partial(forward_kernel, tokens // block, context...  45.9 us
  transfers between devices with their start and end apart: 7, of which 1 were waited for; matrix products, arithmetic and copies ran while one was open for 12% of the time, Pallas kernels for 23%

profile of v4, /device:TPU:0, one launch (start us, length us, event | category | flops | bytes accessed | tf_op | source)
XLA Modules:
  0.0 754.1 jit_solution(8296481989968435224)
XLA Ops:
  3.3 1.5 concatenate.17.shard
  4.8 1.7 copy-done
  6.4 194.0 %opening.1 = (bf16[2,4,256,1152]{3,2,1,0:T(8,128)(2,1)}, bf16[4,1152,1152]{2,1,0:T(8,128)(2,1)}, bf16[2,4,4,288,1152]{4,3,2,1,0:T(8,128)(2,1)}) custom-call(bf16[4,256,1152]{2,1,0:T(8,128)(2,1)S(1)} %copy-done, bf16[288,1152]{1,0:T(8,128)(2,1)S(1)} %concatenate.17.shard, bf16[2,288,1152]{2,1,0:T(8,128)(2,1)S(1)} %fusion.26.ff_in), custom_call_target="tpu_custom_call" | custom-call | tf_op jit(solution)/shard_map/opening/pallas_call | solution.py:429
  200.6 2.6 dynamic-slice_bitcast_fusion.3
  205.2 1.8 collective-permute-start.3
  210.7 3.0 convert_reduce_fusion.1
  213.8 3.9 multiply_reduce_fusion
  217.7 3.0 slice.104
  221.4 1.9 add_convert_fusion.1.n1
  223.4 8.0 %multiply_convert_fusion.q_ref = bf16[1152,1024]{1,0:T(8,128)(2,1)} fusion(bf16[2048,1152]{1,0:T(8,128)(2,1)S(1)} %add_convert_fusion.1.n1, f32[1152]{0:T(1024)S(1)} %copy-done.29, bf16[4,1152,1152]{2,1,0:T(8,128)(2,1)} %get-tuple-element.40), kind=kOutput, calls=%fused_computation.17 | convolution fusion | flops 2721447936 | bytes 7380992 | tf_op jit(solution)/shard_map/dot_general | solution.py:21
  231.3 14.8 %add_convert_fusion.k_ref.v_ref = bf16[2304,2048]{1,0:T(8,128)(2,1)} fusion(bf16[2304,1152]{1,0:T(8,128)(2,1)S(1)} %bitcast.100, bf16[2048,1152]{1,0:T(8,128)(2,1)S(1)} %add_convert_fusion.1.n1, f32[2304]{0:T(1024)S(1)} %concatenate.20), kind=kOutput, calls=%fused_computation | convolution fusion | flops 10881073152 | bytes 19473408 | tf_op jit(solution)/shard_map/dot_general | solution.py:21
  246.7 6.5 convert_element_type.60
  253.2 3.2 slice.114
  264.9 45.9 %attention_forward.1 = (bf16[1152,1024]{1,0:T(8,128)(2,1)}, f32[16,1,1024]{2,1,0:T(1,128)}) custom-call(s32[4]{0:T(128)} %get-tuple-element.70.count, s32[32]{0:T(128)} %reshape.240.index, bf16[1152,1024]{1,0:T(8,128)(2,1)} %multiply_convert_fusion.q_ref, bf16[2304,2048]{1,0:T(8,128)(2,1)} %add_convert_fusion.k_ref.v_ref, ...), custom_call_target="tpu_custom_call" | custom-call | flops 28991029248 | bytes 14155776 | tf_op jit(solution)/shard_map/attention_forward/pallas_call | solution.py:115
  310.8 7.9 %fusion.35 = (f32[1024]{0:T(1024)S(1)}, f32[1024,1152]{1,0:T(8,128)S(1)}) fusion(f32[1152]{0:T(1024)S(1)} %copy-done.30, bf16[1152,1024]{1,0:T(8,128)(2,1)} %get-tuple-element.41.o_ref.ot, bf16[4,1152,1152]{2,1,0:T(8,128)(2,1)} %get-tuple-element.40, f32[2048,1152]{1,0:T(8,128)} %convert_element_type.60), kind=kOutput, calls=%fused_computation.99 | convolution fusion | flops 2721446912 | bytes 14459392 | tf_op jit(solution)/shard_map/dot_general | solution.py:21
  319.5 2.2 add_convert_fusion.4.n2
  325.2 1.4 copy-done.3
  327.6 127.9 %feed.1 = (f32[1024,1152]{1,0:T(8,128)}, f32[1024,1152]{1,0:T(8,128)}, f32[144,1152]{1,0:T(8,128)}, f32[144,1152]{1,0:T(8,128)}, f32[4,1,1152]{2,1,0:T(1,128)}) custom-call(bf16[1024,1152]{1,0:T(8,128)(2,1)} %add_convert_fusion.4.n2, bf16[1024,1152]{1,0:T(8,128)(2,1)} %bitcast.96, f32[4,1,1152]{2,1,0:T(1,128)} %pad.14.bias, bf16[2,4,1152,1152]{3,2,1,0:T(8,128)(2,1)} %bitcast.115), custom_call_target="tpu_custom_call" | custom-call | flops 65229815808 | bytes 40108032 | tf_op jit(solution)/shard_map/feed/pallas_call | solution.py:619
  455.6 5.7 multiply_reduce_fusion.1
  461.4 6.8 convert_reduce_fusion.3
  468.2 7.2 convolution_convert_fusion.do_ref
  475.4 76.2 %attention_backward.1 = (bf16[1152,1024]{1,0:T(8,128)(2,1)}, bf16[1152,2048]{1,0:T(8,128)(2,1)}, bf16[1152,2048]{1,0:T(8,128)(2,1)}) custom-call(s32[4]{0:T(128)} %get-tuple-element.70.count, s32[32]{0:T(128)} %reshape.240.index, bf16[1152,1024]{1,0:T(8,128)(2,1)} %multiply_convert_fusion.q_ref, bf16[2304,2048]{1,0:T(8,128)(2,1)} %add_convert_fusion.k_ref.v_ref, ...), custom_call_target="tpu_custom_call" | custom-call | flops 48318382080 | bytes 28311552 | tf_op jit(solution)/shard_map/attention_backward/pallas_call | solution.py:141
  551.6 3.2 convert_reduce_fusion
  555.4 7.2 fusion.2
  562.6 7.1 fusion.5
  569.7 7.1 fusion.7
  578.1 9.2 %add_convert_fusion.2 = bf16[1024,1152]{1,0:T(8,128)(2,1)} fusion(f32[1024,1152]{1,0:T(8,128)} %fusion.7, bf16[1152,2048]{1,0:T(8,128)(2,1)} %get-tuple-element.48.dvt, bf16[4,1152,1152]{2,1,0:T(8,128)(2,1)} %get-tuple-element.40), kind=kOutput, calls=%fused_computation.11 | convolution fusion | flops 2720268288 | bytes 12091392 | tf_op jit(solution)/shard_map/dot_general | solution.py:21
  591.4 7.3 add_add_fusion
  598.7 124.3 %closing.1 = (f32[144,288]{1,0:T(8,128)}, f32[144,288]{1,0:T(8,128)}, f32[144,288]{1,0:T(8,128)}, f32[144,288]{1,0:T(8,128)}, f32[112,128]{1,0:T(8,128)}, /*index=5*/bf16[4,256,1152]{2,1,0:T(8,128)(2,1)}) custom-call(bf16[4,256,1152]{2,1,0:T(8,128)(2,1)} %bitcast.104, f32[4,256,1152]{2,1,0:T(8,128)} %bitcast.103, f32[4,256,1152]{2,1,0:T(8,128)} %bitcast.97, ...), custom_call_target="tpu_custom_call" | custom-call | tf_op jit(solution)/shard_map/closing/pallas_call | solution.py:877
  723.9 1.6 slice_bitcast_fusion.1
  728.3 4.3 convert_element_type.77
  734.9 14.9 %collective-permute-done.6 = bf16[256,1152]{1,0:T(8,128)(2,1)S(1)} collective-permute-done((bf16[256,1152]{1,0:T(8,128)(2,1)S(1)}, bf16[256,1152]{1,0:T(8,128)(2,1)S(1)}, u32[]{:S(2)}, u32[]{:S(2)}) %collective-permute-start.6) | collective-permute-done | bytes 589856 | tf_op jit(solution)/shard_map/ppermute | solution.py:958
  (143 shorter events, 39.0 us)
Async XLA Ops:
  203.2 118.5 %collective-permute-start.1 = (bf16[256,1152]{1,0:T(8,128)(2,1)}, bf16[256,1152]{1,0:T(8,128)(2,1)}, u32[]{:S(2)}, u32[]{:S(2)}) collective-permute-start(bf16[256,1152]{1,0:T(8,128)(2,1)} %get-tuple-element.81), channel_id=1, source_target_pairs={{0,1},{1,2},{2,3},{3,0},{4,5},{5,6},{6,7},{7,4},{8,9},{9,10},{10,1... | collective-permute-start | bytes 1769480 | tf_op jit(solution)/shard_map/ppermute | solution.py:948
  203.8 119.1 %collective-permute-start.2 = (bf16[256,1152]{1,0:T(8,128)(2,1)S(1)}, bf16[256,1152]{1,0:T(8,128)(2,1)}, u32[]{:S(2)}, u32[]{:S(2)}) collective-permute-start(bf16[256,1152]{1,0:T(8,128)(2,1)S(1)} %get-tuple-element.80), channel_id=1, source_target_pairs={{0,2},{1,3},{2,0},{3,1},{4,6},{5,7},{6,4},{7,5},{8,10},{9,11},{10,... | collective-permute-start | bytes 1769480 | tf_op jit(solution)/shard_map/ppermute | solution.py:948
  205.2 118.8 %collective-permute-start.3 = (bf16[256,1152]{1,0:T(8,128)(2,1)S(1)}, bf16[256,1152]{1,0:T(8,128)(2,1)}, u32[]{:S(2)}, u32[]{:S(2)}) collective-permute-start(bf16[256,1152]{1,0:T(8,128)(2,1)S(1)} %get-tuple-element.79), channel_id=1, source_target_pairs={{0,3},{1,0},{2,1},{3,2},{4,7},{5,4},{6,5},{7,6},{8,11},{9,8},{10,9... | collective-permute-start | bytes 1769480 | tf_op jit(solution)/shard_map/ppermute | solution.py:948
  209.0 50.8 %collective-permute-start = (s32[1024]{0:T(1024)S(1)}, s32[1024]{0:T(1024)}, u32[]{:S(2)}, u32[]{:S(2)}) collective-permute-start(s32[1024]{0:T(1024)S(1)} %bitcast.112), channel_id=1, source_target_pairs={{4,0},{0,4},{5,1},{1,5},{6,2},{2,6},{7,3},{3,7},{12,8},{8,12},{13,... | collective-permute-start | bytes 12296 | tf_op jit(solution)/shard_map/ppermute | solution.py:978
  213.8 7.6 %slice-start = ((s8[4718592]{0:T(1024)(128)(4,1)}), s8[4194304]{0:T(1024)(128)(4,1)S(1)}, s32[]{:S(2)}) async-start(s8[4718592]{0:T(1024)(128)(4,1)} %bitcast.93), calls=%async_computation | async-start | bytes 8388608
  223.4 8.0 %copy-start.5 = (bf16[2048,1152]{1,0:T(8,128)(2,1)}, bf16[2048,1152]{1,0:T(8,128)(2,1)S(1)}, u32[]{:S(2)}) copy-start(bf16[2048,1152]{1,0:T(8,128)(2,1)S(1)} %add_convert_fusion.1.n1) | copy-start | bytes 14155780
  264.9 45.9 %copy-start.30 = (f32[1152]{0:T(1024)S(1)}, f32[1152]{0:T(1024)}, u32[]{:S(2)}) copy-start(f32[1152]{0:T(1024)} %param.28) | copy-start | bytes 13828
  455.5 5.7 copy-start.2
  455.5 5.9 copy-start.4
  455.5 5.9 copy-start.25
  468.2 7.2 copy-start.7
  551.6 11.0 %slice-start.2 = ((s8[4718592]{0:T(1024)(128)(4,1)}), s8[4194304]{0:T(1024)(128)(4,1)S(1)}, s32[]{:S(2)}) async-start(s8[4718592]{0:T(1024)(128)(4,1)} %bitcast.101), calls=%async_computation.2 | async-start | bytes 8388608
  555.4 7.2 slice-start.3
  569.7 7.1 copy-start.8
  569.7 7.5 copy-start.23
  569.7 7.7 %copy-start.21 = (f32[1152]{0:T(1024)S(1)}, f32[1152]{0:T(1024)}, u32[]{:S(2)}) copy-start(f32[1152]{0:T(1024)} %convert_reduce_fusion.2) | copy-start | bytes 13828
  577.5 13.9 %slice-start.4 = ((s8[4718592]{0:T(1024)(128)(4,1)}), s8[4194304]{0:T(1024)(128)(4,1)S(1)}, s32[]{:S(2)}) async-start(s8[4718592]{0:T(1024)(128)(4,1)} %bitcast.116), calls=%async_computation.4 | async-start | bytes 8388608
  577.5 13.9 %slice-start.6 = ((s8[4718592]{0:T(1024)(128)(4,1)}), s8[4194304]{0:T(1024)(128)(4,1)S(1)}, s32[]{:S(2)}) async-start(s8[4718592]{0:T(1024)(128)(4,1)} %bitcast.118), calls=%async_computation.6 | async-start | bytes 8388608
  578.1 9.4 %copy-start.9 = (bf16[1024,1152]{1,0:T(8,128)(2,1)S(1)}, bf16[1024,1152]{1,0:T(8,128)(2,1)}, u32[]{:S(2)}) copy-start(bf16[1024,1152]{1,0:T(8,128)(2,1)} %get-tuple-element.74) | copy-start | bytes 7077892
  578.1 13.2 %slice-start.5 = ((s8[4718592]{0:T(1024)(128)(4,1)}), s8[524288]{0:T(1024)(128)(4,1)S(1)}, s32[]{:S(2)}) async-start(s8[4718592]{0:T(1024)(128)(4,1)} %bitcast.116), calls=%async_computation.5 | async-start | bytes 1048576
  578.1 13.2 %slice-start.7 = ((s8[4718592]{0:T(1024)(128)(4,1)}), s8[524288]{0:T(1024)(128)(4,1)S(1)}, s32[]{:S(2)}) async-start(s8[4718592]{0:T(1024)(128)(4,1)} %bitcast.118), calls=%async_computation.7 | async-start | bytes 1048576
  590.2 142.4 %collective-permute-start.4 = (bf16[256,1152]{1,0:T(8,128)(2,1)}, bf16[256,1152]{1,0:T(8,128)(2,1)}, u32[]{:S(2)}, u32[]{:S(2)}) collective-permute-start(bf16[256,1152]{1,0:T(8,128)(2,1)} %get-tuple-element.77), channel_id=1, source_target_pairs={{1,0},{2,1},{3,2},{0,3},{5,4},{6,5},{7,6},{4,7},{9,8},{10,9},{11,1... | collective-permute-start | bytes 1769480 | tf_op jit(solution)/shard_map/ppermute | solution.py:958
  591.3 142.4 %collective-permute-start.5 = (bf16[256,1152]{1,0:T(8,128)(2,1)}, bf16[256,1152]{1,0:T(8,128)(2,1)}, u32[]{:S(2)}, u32[]{:S(2)}) collective-permute-start(bf16[256,1152]{1,0:T(8,128)(2,1)} %get-tuple-element.76), channel_id=1, source_target_pairs={{2,0},{3,1},{0,2},{1,3},{6,4},{7,5},{4,6},{5,7},{10,8},{11,9},{8,1... | collective-permute-start | bytes 1769480 | tf_op jit(solution)/shard_map/ppermute | solution.py:958
  598.7 124.3 %copy-start.14 = (f32[144,1152]{1,0:T(8,128)S(1)}, f32[144,1152]{1,0:T(8,128)}, u32[]{:S(2)}) copy-start(f32[144,1152]{1,0:T(8,128)} %get-tuple-element.58) | copy-start | bytes 1990660
  723.0 9.6 %copy-start.15 = (bf16[256,1152]{1,0:T(8,128)(2,1)S(1)}, bf16[256,1152]{1,0:T(8,128)(2,1)}, u32[]{:S(2)}) copy-start(bf16[256,1152]{1,0:T(8,128)(2,1)} %get-tuple-element.75) | copy-start | bytes 1769476
  723.0 9.6 %copy-start.11 = (bf16[4,256,1152]{2,1,0:T(8,128)(2,1)S(1)}, bf16[4,256,1152]{2,1,0:T(8,128)(2,1)}, u32[]{:S(2)}) copy-start(bf16[4,256,1152]{2,1,0:T(8,128)(2,1)} %copy-done.10) | copy-start | bytes 7077892
  728.3 21.6 %copy-start.19 = (f32[144,288]{1,0:T(8,128)S(1)}, f32[144,288]{1,0:T(8,128)}, u32[]{:S(2)}) copy-start(f32[144,288]{1,0:T(8,128)} %get-tuple-element.115) | copy-start | bytes 497668
  728.3 22.3 %copy-start.18 = (f32[144,288]{1,0:T(8,128)S(1)}, f32[144,288]{1,0:T(8,128)}, u32[]{:S(2)}) copy-start(f32[144,288]{1,0:T(8,128)} %get-tuple-element.117) | copy-start | bytes 497668
  728.3 23.1 %copy-start.17 = (f32[144,288]{1,0:T(8,128)S(1)}, f32[144,288]{1,0:T(8,128)}, u32[]{:S(2)}) copy-start(f32[144,288]{1,0:T(8,128)} %get-tuple-element.118) | copy-start | bytes 497668
  728.3 23.8 %copy-start.16 = (f32[144,288]{1,0:T(8,128)S(1)}, f32[144,288]{1,0:T(8,128)}, u32[]{:S(2)}) copy-start(f32[144,288]{1,0:T(8,128)} %get-tuple-element.56) | copy-start | bytes 497668
  728.3 24.5 %copy-start.13 = (f32[144,1152]{1,0:T(8,128)S(1)}, f32[144,1152]{1,0:T(8,128)}, u32[]{:S(2)}) copy-start(f32[144,1152]{1,0:T(8,128)} %get-tuple-element.57) | copy-start | bytes 1990660
  732.6 17.2 %collective-permute-start.6 = (bf16[256,1152]{1,0:T(8,128)(2,1)S(1)}, bf16[256,1152]{1,0:T(8,128)(2,1)S(1)}, u32[]{:S(2)}, u32[]{:S(2)}) collective-permute-start(bf16[256,1152]{1,0:T(8,128)(2,1)S(1)} %copy-done.15), channel_id=1, source_target_pairs={{3,0},{0,1},{1,2},{2,3},{7,4},{4,5},{5,6},{6,7},{11,8},{8,9},{9,10... | collective-permute-start | bytes 1769480 | tf_op jit(solution)/shard_map/ppermute | solution.py:958
  (14 other events, 36.4 us)
